TPU v7x, 32 devices: a whole 2x2x4 slice. The times are simulated.
32 devices in a mesh: parts: 2 (over x), wide: 16 (over z, y, core).
Axes of the slice: x: 2, y: 2, z: 4, core: 2. Of those that a mesh axis runs over, the one named last changes fastest.
Arguments:
- potential_pool: bfloat16 [32, 512, 512], P(('parts', 'wide')), parts along dimension 0, may hold values from 0 to 1.5
- slice_owner: int32 [4], P('parts'), parts along dimension 0, may hold values from 0 to 15
- beam_index: int32 [16, 2], replicated, may hold values from -128 to 127
- aperture: int32 [16], replicated, may hold values 0 or 1
- probe_position: int32 [16, 2], P('parts'), parts along dimension 0, may hold values from 0 to 511
Outputs:
- probes: float32 [512, 2, 8, 256], P(('parts', 'wide')), parts along dimension 0
There are 2 independent parts, one for each index of `parts`. A program takes and returns all parts, laid end to end along the dimension named above; an argument that names none is the same for every part. Nothing has to cross between parts.
All inputs are finite; a program needn't handle non-finite values.
Results may differ from a plain program's by a relative error of at most 0.0003.
Values may be sent and summed in bfloat16 or wider, within the bound.
No kernel may reach another device: no remote copies, remote signals or barrier semaphores. Data moves between devices by JAX's collectives and lax.ppermute only.
A program may use at most 64 MiB of HBM per device.

v0:
```python
import math

import jax
import jax.numpy as jnp
import numpy as np
from jax import lax
from jax.experimental import pallas as pl
from jax.experimental.pallas import tpu as pltpu
from jax.sharding import PartitionSpec as P

FRESNEL = 4.7e-05
TWO_PI = 2.0 * math.pi
F32 = jnp.float32
BF16 = jnp.bfloat16
QUAD = 4


def flip(array, bit, groups):
    return lax.ppermute(array, "wide", [(i, i ^ bit) for i in range(groups)])


def half(array, which):
    rows = array.shape[0] // 2
    return lax.dynamic_slice_in_dim(array, which * rows, rows, 0)


def spread_slabs(own_slab, slice_owner, groups, device):
    count = slice_owner.shape[0]
    bits = [1 << b for b in range(groups.bit_length() - 1)]
    side = device & 1
    kept = half(own_slab, side)
    received = flip(half(own_slab, 1 - side), 1, groups)
    zero = jnp.zeros_like(kept)
    parts = [
        jnp.where(slice_owner[s] == device, kept, jnp.where(slice_owner[s] == (device ^ 1), received, zero))
        for s in range(count)
    ]
    for bit in bits[1:-1]:
        side = (device // bit) & 1
        parts = [half(part, side) + flip(half(part, 1 - side), bit, groups) for part in parts]
    parts = [part + flip(part, bits[-1], groups) for part in parts]
    for bit in reversed(bits[:-1]):
        side = (device // bit) & 1
        grown = []
        for part in parts:
            other = flip(part, bit, groups)
            low = jnp.where(side == 0, part, other)
            high = jnp.where(side == 0, other, part)
            grown.append(jnp.concatenate([low, high], axis=0))
        parts = grown
    return parts


def class_frequencies(grid):
    top = grid // 3
    classes = [[u for u in range(-top, top + 1) if u % 4 == c] for c in range(4)]
    padded = -(-max(len(c) for c in classes) // 8) * 8
    freq = np.zeros((4, padded), np.int32)
    real = np.zeros((4, padded), np.float32)
    for c, members in enumerate(classes):
        freq[c, : len(members)] = members
        real[c, : len(members)] = 1.0
    return freq, real


def split_table(table):
    high = lax.reduce_precision(table, 8, 7)
    return high.astype(BF16), (table - high).astype(BF16)


def block(a, b, c, d):
    return jnp.concatenate([jnp.concatenate([a, b], axis=-1), jnp.concatenate([c, d], axis=-1)], axis=-2)


def make_tables(grid):
    freq, real = class_frequencies(grid)
    kp = freq.shape[1]
    q = grid // 4
    turns = np.mod(freq[:, None, :].astype(np.int64) * np.arange(q)[None, :, None], grid)
    angle = TWO_PI * turns / grid
    cos = np.zeros((4, q, q), np.float32)
    sin = np.zeros((4, q, q), np.float32)
    cos[:, :, :kp] = np.cos(angle) * real[:, None, :]
    sin[:, :, :kp] = np.sin(angle) * real[:, None, :]
    cos, sin = lax.optimization_barrier((jnp.asarray(cos), jnp.asarray(sin)))
    cos_t, sin_t = jnp.swapaxes(cos, 1, 2), jnp.swapaxes(sin, 1, 2)
    lane_fwd = block(cos, -sin, sin, cos)
    row_fwd = block(cos_t[:, :kp], sin_t[:, :kp], -sin_t[:, :kp], cos_t[:, :kp])
    row_inv = block(cos[:, :, :kp], -sin[:, :, :kp], sin[:, :, :kp], cos[:, :, :kp])
    lane_inv = block(cos_t, sin_t, -sin_t, cos_t)
    return [split_table(t) for t in (lane_fwd, row_fwd, row_inv, lane_inv)]


def make_propagator(grid):
    freq, real = class_frequencies(grid)
    kp = freq.shape[1]
    q = grid // 4
    lanes = np.full((4, q), grid, np.int32)
    lanes[:, :kp] = np.where(real > 0, freq, grid)
    rows = np.where(real > 0, freq, grid)
    rows, lanes = lax.optimization_barrier((jnp.asarray(rows, jnp.int32), jnp.asarray(lanes.reshape(-1), jnp.int32)))
    squared = (rows * rows)[:, :, None] + (lanes * lanes)[None, None, :]
    keep = (9 * squared <= grid * grid).astype(F32) * (1.0 / (grid * grid))
    turning = -FRESNEL * squared.astype(F32)
    return jnp.cos(turning) * keep, jnp.sin(turning) * keep


def rows_table(grid, first_row, rows):
    freq, real = class_frequencies(grid)
    x = first_row + jnp.arange(rows, dtype=jnp.int32)
    turns = jnp.mod(x[None, :, None] * jnp.asarray(freq)[:, None, :], grid)
    angle = TWO_PI * turns.astype(F32) / grid
    cos = jnp.cos(angle) * jnp.asarray(real)[:, None, :]
    sin = jnp.sin(angle) * jnp.asarray(real)[:, None, :]
    return split_table(block(cos, -sin, sin, cos))


def probe_waves(grid, beam_index, aperture, position):
    beams = beam_index.shape[0]
    pixels = jnp.arange(grid, dtype=jnp.int32)

    def turned(turns, sign):
        angle = sign * TWO_PI * jnp.mod(turns, grid).astype(F32) / grid
        return jnp.cos(angle), jnp.sin(angle)

    weight = aperture.astype(F32) / math.sqrt(beams)
    mixing = beam_index[:, 0][None, :] * position[:, 0][:, None] + beam_index[:, 1][None, :] * position[:, 1][:, None]
    coef_r, coef_i = turned(mixing, -1.0)
    coef_r, coef_i = coef_r * weight[None, :], coef_i * weight[None, :]
    row_r, row_i = turned(pixels[:, None] * beam_index[:, 0][None, :], 1.0)
    col_r, col_i = turned(beam_index[:, 1][:, None] * pixels[None, :], 1.0)
    left_r = coef_r[:, None, :] * row_r - coef_i[:, None, :] * row_i
    left_i = coef_r[:, None, :] * row_i + coef_i[:, None, :] * row_r
    left = jnp.concatenate([left_r, left_i], axis=-1)
    right = jnp.stack([jnp.concatenate([col_r, -col_i], axis=0), jnp.concatenate([col_i, col_r], axis=0)])
    return jnp.einsum("pxb,rby->prxy", left, right, precision=lax.Precision.HIGHEST)


def split(x):
    high = x.astype(BF16)
    return high, (x - high.astype(F32)).astype(BF16)


def dot(a, b):
    return jnp.dot(a, b, preferred_element_type=F32)


def dot3(ah, al, bh, bl):
    return dot(ah, bh) + dot(al, bh) + dot(ah, bl)


def butterfly(parts, sign):
    (r0, i0), (r1, i1), (r2, i2), (r3, i3) = parts
    sr, si, dr, di = r0 + r2, i0 + i2, r0 - r2, i0 - i2
    tr, ti, er, ei = r1 + r3, i1 + i3, r1 - r3, i1 - i3
    up = (dr - sign * ei, di + sign * er)
    down = (dr + sign * ei, di - sign * er)
    return [(sr + tr, si + ti), up, (sr - tr, si - ti), down]


def cos_sin(v):
    t = v * v
    c = 1.0
    for n in range(14, 0, -2):
        c = 1.0 - t * (1.0 / (n * (n - 1))) * c
    s = 1.0
    for n in range(15, 1, -2):
        s = 1.0 - t * (1.0 / (n * (n - 1))) * s
    return c, v * s


def transmit_tables(slab_ref, tr_ref, ti_ref):
    rows = 32
    q = slab_ref.shape[1] // 4

    def body(b, carry):
        at = pl.ds(pl.multiple_of(b * rows, rows), rows)
        for j in range(4):
            lanes = pl.ds(j * q, q)
            c, s = cos_sin(slab_ref[at, lanes].astype(F32))
            tr_ref[at, lanes] = c
            ti_ref[at, lanes] = s
        return carry

    lax.fori_loop(0, slab_ref.shape[0] // rows, body, 0)


def forward(wave_ref, tr_ref, ti_ref, lane, row, prop, scratch):
    yh, yl, sr, si, zh, zl, uh, ul = scratch
    n = tr_ref.shape[0]
    q = n // 4
    kp2 = uh.shape[1]
    kp = kp2 // 2
    rows = 32

    def fold_lanes(b, carry):
        at = pl.ds(pl.multiple_of(b * rows, rows), rows)
        parts = []
        for j in range(4):
            lanes = pl.ds(j * q, q)
            wr, wi = wave_ref[0, 0, at, lanes], wave_ref[0, 1, at, lanes]
            cr, ci = tr_ref[at, lanes], ti_ref[at, lanes]
            parts.append((wr * cr - wi * ci, wr * ci + wi * cr))
        for c, (r, i) in enumerate(butterfly(parts, -1.0)):
            yh[c, at, :q], yl[c, at, :q] = split(r)
            yh[c, at, q:], yl[c, at, q:] = split(i)
        return carry

    lax.fori_loop(0, n // rows, fold_lanes, 0)
    for c in range(4):
        out = dot3(yh[c], yl[c], lane[0][c], lane[1][c])
        sr[:, c * q : (c + 1) * q] = out[:, :q]
        si[:, c * q : (c + 1) * q] = out[:, q:]

    def fold_rows(b, carry):
        first = pl.multiple_of(b * rows, rows)
        for l in range(4):
            lanes = pl.ds(l * q, q)
            parts = [(sr[pl.ds(j * q + first, rows), lanes], si[pl.ds(j * q + first, rows), lanes]) for j in range(4)]
            for c, (r, i) in enumerate(butterfly(parts, -1.0)):
                zh[c, pl.ds(first, rows), lanes], zl[c, pl.ds(first, rows), lanes] = split(r)
                zh[c, pl.ds(q + first, rows), lanes], zl[c, pl.ds(q + first, rows), lanes] = split(i)
        return carry

    lax.fori_loop(0, q // rows, fold_rows, 0)
    for c in range(4):
        out = dot3(row[0][c], row[1][c], zh[c], zl[c])
        r, i = out[:kp], out[kp:]
        pr, pi = prop[0][c], prop[1][c]
        uh[c], ul[c] = split(jnp.concatenate([r * pr - i * pi, r * pi + i * pr], axis=0))


def first_kernel(slab_ref, wave_ref, lfh, lfl, rfh, rfl, rih, ril, lih, lil, pr, pi, out_ref, tr, ti, yh, yl, sr, si, zh, zl, uh, ul, g, h):
    n = slab_ref.shape[0]
    q = n // 4
    rows = 32

    @pl.when(pl.program_id(0) == 0)
    def _():
        transmit_tables(slab_ref, tr, ti)

    forward(wave_ref, tr, ti, (lfh, lfl), (rfh, rfl), (pr, pi), (yh, yl, sr, si, zh, zl, uh, ul))
    for c in range(4):
        g[c] = dot3(rih[c], ril[c], uh[c], ul[c])

    def unfold_rows(b, carry):
        first = pl.multiple_of(b * rows, rows)
        for l in range(4):
            lanes = pl.ds(l * q, q)
            parts = [(g[c, pl.ds(first, rows), lanes], g[c, pl.ds(q + first, rows), lanes]) for c in range(4)]
            for j, (r, i) in enumerate(butterfly(parts, 1.0)):
                yh[l, pl.ds(j * q + first, rows), :q], yl[l, pl.ds(j * q + first, rows), :q] = split(r)
                yh[l, pl.ds(j * q + first, rows), q:], yl[l, pl.ds(j * q + first, rows), q:] = split(i)
        return carry

    lax.fori_loop(0, q // rows, unfold_rows, 0)
    for c in range(4):
        h[c] = dot3(yh[c], yl[c], lih[c], lil[c])

    def unfold_lanes(b, carry):
        at = pl.ds(pl.multiple_of(b * rows, rows), rows)
        parts = [(h[c, at, :q], h[c, at, q:]) for c in range(4)]
        for j, (r, i) in enumerate(butterfly(parts, 1.0)):
            out_ref[0, 0, at, pl.ds(j * q, q)] = r
            out_ref[0, 1, at, pl.ds(j * q, q)] = i
        return carry

    lax.fori_loop(0, n // rows, unfold_lanes, 0)


def last_kernel(slab_ref, wave_ref, lfh, lfl, rfh, rfl, dh, dl, lih, lil, pr, pi, out_ref, tr, ti, yh, yl, sr, si, zh, zl, uh, ul):
    n = slab_ref.shape[0]
    q = n // 4
    take = dh.shape[1] // 2

    @pl.when(pl.program_id(0) == 0)
    def _():
        transmit_tables(slab_ref, tr, ti)

    forward(wave_ref, tr, ti, (lfh, lfl), (rfh, rfl), (pr, pi), (yh, yl, sr, si, zh, zl, uh, ul))
    out = dot3(dh[0], dl[0], uh[0], ul[0])
    for c in range(1, 4):
        out = out + dot3(dh[c], dl[c], uh[c], ul[c])
    parts = []
    for c in range(4):
        lanes = slice(c * q, (c + 1) * q)
        high, low = split(jnp.concatenate([out[:take, lanes], out[take:, lanes]], axis=1))
        back = dot3(high, low, lih[c], lil[c])
        parts.append((back[:, :q], back[:, q:]))
    for j, (r, i) in enumerate(butterfly(parts, 1.0)[1:3]):
        out_ref[0, 0, :, j * q : (j + 1) * q] = r
        out_ref[0, 1, :, j * q : (j + 1) * q] = i


def whole(array):
    return pl.BlockSpec(array.shape, lambda p: (0,) * array.ndim, pipeline_mode=pl.Buffered(1))


def one(shape):
    return pl.BlockSpec((1,) + shape[1:], lambda p: (p,) + (0,) * (len(shape) - 1))


def forward_scratch(n, kp2):
    q = n // 4
    return [
        pltpu.VMEM((n, n), F32),
        pltpu.VMEM((n, n), F32),
        pltpu.VMEM((4, n, 2 * q), BF16),
        pltpu.VMEM((4, n, 2 * q), BF16),
        pltpu.VMEM((n, n), F32),
        pltpu.VMEM((n, n), F32),
        pltpu.VMEM((4, 2 * q, n), BF16),
        pltpu.VMEM((4, 2 * q, n), BF16),
        pltpu.VMEM((4, kp2, n), BF16),
        pltpu.VMEM((4, kp2, n), BF16),
    ]


def run_kernel(kernel, name, slab, waves, tables, out_shape, extra):
    n = slab.shape[0]
    kp2 = tables[2].shape[1]
    return pl.pallas_call(
        kernel,
        name=name,
        grid=(waves.shape[0],),
        in_specs=[whole(slab), one(waves.shape)] + [whole(t) for t in tables],
        out_specs=one(out_shape),
        out_shape=jax.ShapeDtypeStruct(out_shape, F32),
        scratch_shapes=forward_scratch(n, kp2) + extra,
        compiler_params=pltpu.CompilerParams(vmem_limit_bytes=48 << 20),
    )(slab, waves, *tables)


def local(potential_pool, slice_owner, beam_index, aperture, probe_position):
    grid = potential_pool.shape[-1]
    crop = grid // 2
    margin = grid // 4
    q = grid // 4
    groups = lax.axis_size("wide")
    device = lax.axis_index("wide")
    probes = probe_position.shape[0]
    per_device = probes // QUAD
    quad_rows = crop // (groups // QUAD)
    own_rows = crop // groups
    place = device % QUAD
    quad = device // QUAD

    slabs = spread_slabs(potential_pool[0], slice_owner, groups, device)

    position = lax.dynamic_slice_in_dim(probe_position, place * per_device, per_device, 0)
    waves = probe_waves(grid, beam_index, aperture, position)
    lane_fwd, row_fwd, row_inv, lane_inv = make_tables(grid)
    prop = make_propagator(grid)
    last_rows = rows_table(grid, margin + quad * quad_rows, quad_rows)

    for slab in slabs[:-1]:
        tables = (*lane_fwd, *row_fwd, *row_inv, *lane_inv, *prop)
        extra = [pltpu.VMEM((4, 2 * q, grid), F32), pltpu.VMEM((4, grid, 2 * q), F32)]
        waves = run_kernel(first_kernel, "slice_full", slab, waves, tables, waves.shape, extra)
    tables = (*lane_fwd, *row_fwd, *last_rows, *lane_inv, *prop)
    cut = run_kernel(last_kernel, "slice_last", slabs[-1], waves, tables, (per_device, 2, quad_rows, crop), [])

    side = (place // 2) & 1
    pair = cut.reshape(per_device, 2, 2, quad_rows // 2, crop)
    kept = lax.dynamic_index_in_dim(pair, side, 2, False)
    other = flip(lax.dynamic_index_in_dim(pair, 1 - side, 2, False), 2, groups)
    both = jnp.stack([jnp.where(side == 0, kept, other), jnp.where(side == 0, other, kept)])
    side = place & 1
    pair = both.reshape(2, per_device, 2, 2, own_rows, crop)
    kept = lax.dynamic_index_in_dim(pair, side, 3, False)
    other = flip(lax.dynamic_index_in_dim(pair, 1 - side, 3, False), 1, groups)
    all_probes = jnp.stack([jnp.where(side == 0, kept, other), jnp.where(side == 0, other, kept)], axis=1)
    return jnp.transpose(all_probes.reshape(probes, 2, own_rows, crop), (2, 1, 0, 3))


def solution(mesh):
    placed = (P(("parts", "wide"), None, None), P("parts"), P(), P(), P("parts", None))
    return jax.shard_map(
        local,
        mesh=mesh,
        in_specs=placed,
        out_specs=P(("parts", "wide"), None, None, None),
        check_vma=False,
    )
```

profile of v0, /device:TPU:0, one launch (start us, length us, event | category | flops | bytes accessed | tf_op | source)
XLA Modules:
  0.0 104.8 jit_solution(8820585308240371003)
XLA Ops:
  1.6 1.7 %bitcast_negate_fusion = f32[4,128,128]{2,1,0:T(8,128)} fusion(f32[4,128,128]{1,2,0:T(8,128)} %constant.170.clone), kind=kLoop, calls=%fused_computation.132 | loop fusion | flops 65536 | bytes 524288 | tf_op jit(solution)/shard_map/neg | solution.py:90
  3.3 1.7 %slice_negate_fusion.1 = (f32[4,128,88]{1,2,0:T(8,128)}, f32[4,128,88]{1,2,0:T(8,128)}) fusion(f32[4,128,128]{1,2,0:T(8,128)} %constant.170.clone), kind=kLoop, calls=%fused_computation.134 | loop fusion | flops 45056 | bytes 540672 | tf_op jit(solution)/shard_map/neg | solution.py:89
  8.3 1.7 %fusion.42 = (f32[4,88,128]{2,1,0:T(8,128)}, f32[4,88,128]{2,1,0:T(8,128)}) fusion(f32[4,128,128]{2,1,0:T(8,128)} %bitcast.57), kind=kLoop, calls=%fused_computation.135 | loop fusion | flops 45056 | bytes 540672 | tf_op jit(solution)/shard_map/slice | solution.py:88
  10.1 2.0 %fusion.20 = (f32[4,64,88]{2,1,0:T(8,128)}, f32[4,64,88]{2,1,0:T(8,128)}, f32[4,64,88]{2,1,0:T(8,128)}) fusion(f32[4,88]{1,0:T(4,128)} %constant.174.clone, s32[4,88]{1,0:T(4,128)} %constant.173.clone, s32[64]{0:T(128)S(1)} %iota_add_fusion), kind=kLoop, calls=%fused_computation.94 | loop fusion | flops 382976 | bytes 273408 | tf_op jit(solution)/shard_map/neg | solution.py:115
  16.3 2.7 %select_multiply_fusion = (f32[4,88,512]{2,1,0:T(8,128)S(1)}, f32[4,88,512]{2,1,0:T(8,128)S(1)}) fusion(s32[512]{0:T(512)S(1)} %mul.275, s32[4,88]{1,0:T(4,128)S(1)} %mul.274), kind=kLoop, calls=%fused_computation.15 | loop fusion | flops 1441792 | bytes 1445248 | tf_op jit(solution)/shard_map/mul | solution.py:105
  19.2 2.6 %collective-permute-start.1 = (bf16[128,512]{1,0:T(8,128)(2,1)S(1)}, bf16[128,512]{1,0:T(8,128)(2,1)S(1)}, u32[]{:S(2)}, u32[]{:S(2)}) collective-permute-start(bf16[128,512]{1,0:T(8,128)(2,1)S(1)} %constant_dynamic-slice_fusion.4), channel_id=1, source_target_pairs={{0,2},{1,3},{2,0},{3,1},{4,6},{5,7},{6,4},{7,5},{8,10},{9,11},{10,... | collective-permute-start | bytes 393224 | tf_op jit(solution)/shard_map/ppermute | solution.py:19
  21.8 5.0 %convolution_bitcast_fusion.wave_ref = f32[2,2,512,512]{3,2,1,0:T(8,128)} fusion(f32[1,32,512]{2,1,0:T(8,128)S(1)} %get-tuple-element.48, f32[1,32,512]{2,1,0:T(8,128)S(1)} %get-tuple-element.47, f32[2,512,16]{1,2,0:T(8,128)S(1)} %get-tuple-element.46, f32[2,512,16]{1,2,0:T(8,128)S(1)} %get-tuple-element.45), kind=kOutput, calls=%fused_computation | convolution fusion | flops 402718720 | bytes 4456448 | tf_op jit(solution)/shard_map/pxb,rby->prxy/dot_general | solution.py:136
  27.2 1.9 %collective-permute-start.2 = (bf16[64,512]{1,0:T(8,128)(2,1)S(1)}, bf16[64,512]{1,0:T(8,128)(2,1)S(1)}, u32[]{:S(2)}, u32[]{:S(2)}) collective-permute-start(bf16[64,512]{1,0:T(8,128)(2,1)S(1)} %constant_dynamic-slice_fusion.3), channel_id=1, source_target_pairs={{0,4},{1,5},{2,6},{3,7},{4,0},{5,1},{6,2},{7,3},{8,12},{9,13},{10,... | collective-permute-start | bytes 196616 | tf_op jit(solution)/shard_map/ppermute | solution.py:19
  29.1 3.4 %collective-permute-done.7 = bf16[128,512]{1,0:T(8,128)(2,1)S(1)} collective-permute-done((bf16[128,512]{1,0:T(8,128)(2,1)S(1)}, bf16[128,512]{1,0:T(8,128)(2,1)S(1)}, u32[]{:S(2)}, u32[]{:S(2)}) %collective-permute-start.7) | collective-permute-done | bytes 131104 | tf_op jit(solution)/shard_map/ppermute | solution.py:19
  32.6 1.6 %collective-permute-start.8 = (bf16[64,512]{1,0:T(8,128)(2,1)S(1)}, bf16[64,512]{1,0:T(8,128)(2,1)S(1)}, u32[]{:S(2)}, u32[]{:S(2)}) collective-permute-start(bf16[64,512]{1,0:T(8,128)(2,1)S(1)} %constant_dynamic-slice_fusion.1), channel_id=1, source_target_pairs={{0,4},{1,5},{2,6},{3,7},{4,0},{5,1},{6,2},{7,3},{8,12},{9,13},{10,... | collective-permute-start | bytes 196616 | tf_op jit(solution)/shard_map/ppermute | solution.py:19
  34.2 2.6 %collective-permute-start.3 = (bf16[64,512]{1,0:T(8,128)(2,1)S(1)}, bf16[64,512]{1,0:T(8,128)(2,1)S(1)}, u32[]{:S(2)}, u32[]{:S(2)}) collective-permute-start(bf16[64,512]{1,0:T(8,128)(2,1)S(1)} %dynamic-slice_add_fusion.3), channel_id=1, source_target_pairs={{0,8},{1,9},{2,10},{3,11},{4,12},{5,13},{6,14},{7,15},{8,0},{9,1},... | collective-permute-start | bytes 196616 | tf_op jit(solution)/shard_map/ppermute | solution.py:19
  36.9 2.6 %collective-permute-start.9 = (bf16[64,512]{1,0:T(8,128)(2,1)S(1)}, bf16[64,512]{1,0:T(8,128)(2,1)S(1)}, u32[]{:S(2)}, u32[]{:S(2)}) collective-permute-start(bf16[64,512]{1,0:T(8,128)(2,1)S(1)} %dynamic-slice_add_fusion.2), channel_id=1, source_target_pairs={{0,8},{1,9},{2,10},{3,11},{4,12},{5,13},{6,14},{7,15},{8,0},{9,1},... | collective-permute-start | bytes 196616 | tf_op jit(solution)/shard_map/ppermute | solution.py:19
  39.6 1.8 %collective-permute-done.3 = bf16[64,512]{1,0:T(8,128)(2,1)S(1)} collective-permute-done((bf16[64,512]{1,0:T(8,128)(2,1)S(1)}, bf16[64,512]{1,0:T(8,128)(2,1)S(1)}, u32[]{:S(2)}, u32[]{:S(2)}) %collective-permute-start.3) | collective-permute-done | bytes 65568 | tf_op jit(solution)/shard_map/ppermute | solution.py:19
  42.5 2.1 %collective-permute-start.10 = (bf16[64,512]{1,0:T(8,128)(2,1)S(1)}, bf16[64,512]{1,0:T(8,128)(2,1)S(1)}, u32[]{:S(2)}, u32[]{:S(2)}) collective-permute-start(bf16[64,512]{1,0:T(8,128)(2,1)S(1)} %add.156), channel_id=1, source_target_pairs={{0,4},{1,5},{2,6},{3,7},{4,0},{5,1},{6,2},{7,3},{8,12},{9,13},{10,... | collective-permute-start | bytes 196616 | tf_op jit(solution)/shard_map/ppermute | solution.py:19
  47.1 1.6 %collective-permute-start.11 = (bf16[128,512]{1,0:T(8,128)(2,1)S(1)}, bf16[128,512]{1,0:T(8,128)(2,1)}, u32[]{:S(2)}, u32[]{:S(2)}) collective-permute-start(bf16[128,512]{1,0:T(8,128)(2,1)S(1)} %pad_maximum_fusion.6), channel_id=1, source_target_pairs={{0,2},{1,3},{2,0},{3,1},{4,6},{5,7},{6,4},{7,5},{8,10},{9,11},{10,... | collective-permute-start | bytes 393224 | tf_op jit(solution)/shard_map/ppermute | solution.py:19
  49.9 1.8 %fusion.3 = (bf16[4,256,176]{1,2,0:T(8,128)(2,1)S(1)}, bf16[4,256,176]{1,2,0:T(8,128)(2,1)}) fusion(f32[4,128,88]{1,2,0:T(8,128)S(1)} %slice.46, f32[4,128,88]{1,2,0:T(8,128)} %get-tuple-element.34, f32[4,128,88]{1,2,0:T(8,128)} %get-tuple-element.33), kind=kLoop, calls=%fused_computation.20 | loop fusion | flops 1261568 | bytes 1261568 | tf_op jit(solution)/shard_map/convert_element_type | solution.py:68
  51.8 1.4 %collective-permute-done.11 = bf16[128,512]{1,0:T(8,128)(2,1)} collective-permute-done((bf16[128,512]{1,0:T(8,128)(2,1)S(1)}, bf16[128,512]{1,0:T(8,128)(2,1)}, u32[]{:S(2)}, u32[]{:S(2)}) %collective-permute-start.11) | collective-permute-done | bytes 131104 | tf_op jit(solution)/shard_map/ppermute | solution.py:19
  53.2 1.8 %broadcast_select_fusion.5 = (bf16[128,512]{1,0:T(8,128)(2,1)S(1)}, bf16[128,512]{1,0:T(8,128)(2,1)S(1)}, bf16[128,512]{1,0:T(8,128)(2,1)}, bf16[128,512]{1,0:T(8,128)(2,1)}) fusion(bf16[128,512]{1,0:T(8,128)(2,1)} %collective-permute-done.11, pred[]{:T(512)S(6)} %eq.51, bf16[64,512]{1,0:T(8,128)(2,1)} %copy-done.12, bf16[64,512]{1,0:T(8,128)(2,1)} %copy-done.11, ...), kind=kLoop, calls=%fused_computation.75 | loop fusion | flops 786432 | bytes 1048577 | tf_op jit(solution)/shard_map/jit(_where)/select_n | solution.py:47
  55.8 2.0 %fusion.8 = (bf16[4,128,176]{2,1,0:T(8,128)(2,1)S(1)}, bf16[4,128,176]{2,1,0:T(8,128)(2,1)}) fusion(f32[4,64,88]{2,1,0:T(8,128)} %get-tuple-element.51, f32[4,64,88]{2,1,0:T(8,128)} %get-tuple-element.50, f32[4,64,88]{2,1,0:T(8,128)} %get-tuple-element.49), kind=kLoop, calls=%fused_computation.27 | loop fusion | flops 630784 | bytes 630784 | tf_op jit(solution)/shard_map/convert_element_type | solution.py:68
  57.9 2.0 %copy.38.rih = bf16[4,256,176]{2,1,0:T(8,128)(2,1)} copy(bf16[4,256,176]{1,2,0:T(8,128)(2,1)} %get-tuple-element.20) | data formatting | bytes 720896 | tf_op jit(solution)/shard_map/convert_element_type | solution.py:68
  62.4 1.4 %fusion.1 = (bf16[4,256,256]{2,1,0:T(8,128)(2,1)S(1)}, bf16[4,256,256]{2,1,0:T(8,128)(2,1)S(1)}) fusion(f32[4,128,128]{2,1,0:T(8,128)} %bitcast.59, f32[4,128,128]{2,1,0:T(8,128)} %bitcast_negate_fusion, f32[4,128,128]{2,1,0:T(8,128)} %bitcast.58), kind=kLoop, calls=%fused_computation.6 | loop fusion | flops 1835008 | bytes 1835008 | tf_op jit(solution)/shard_map/convert_element_type | solution.py:68
  66.8 16.7 %slice_full.1.wave_ref = f32[2,2,512,512]{3,2,1,0:T(8,128)} custom-call(bf16[512,512]{1,0:T(8,128)(2,1)S(1)} %pad_maximum_fusion.1.slab_ref, f32[2,2,512,512]{3,2,1,0:T(8,128)} %convolution_bitcast_fusion.wave_ref, bf16[4,256,256]{2,1,0:T(8,128)(2,1)S(1)} %copy.36.lfh, bf16[4,256,256]{2,1,0:T(8,128)(2,1)S(1)} %copy.37.lfl, ...), custom_call_target="tpu_custom_call" | custom-call | tf_op jit(solution)/shard_map/slice_full/pallas_call | solution.py:322
  83.5 11.5 %slice_last.1 = f32[2,2,64,256]{3,2,1,0:T(8,128)S(1)} custom-call(bf16[512,512]{1,0:T(8,128)(2,1)S(1)} %pad_maximum_fusion.slab_ref, f32[2,2,512,512]{3,2,1,0:T(8,128)} %slice_full.1.wave_ref, bf16[4,256,256]{2,1,0:T(8,128)(2,1)S(1)} %copy.36.lfh, bf16[4,256,256]{2,1,0:T(8,128)(2,1)S(1)} %copy.37.lfl, bf16[4,176,256]{2,1,0:T(8,128)(2,1)S(1)} %get-tuple-element.22.rfh, ...), custom_call_target="tpu_custom_call" | custom-call | tf_op jit(solution)/shard_map/slice_last/pallas_call | solution.py:322
  96.3 5.2 %collective-permute-done.13 = f32[2,2,32,256]{3,2,1,0:T(8,128)S(1)} collective-permute-done((f32[2,2,32,256]{3,2,1,0:T(8,128)S(1)}, f32[2,2,32,256]{3,2,1,0:T(8,128)S(1)}, u32[]{:S(2)}, u32[]{:S(2)}) %collective-permute-start.13) | collective-permute-done | bytes 131104 | tf_op jit(solution)/shard_map/ppermute | solution.py:19
  (97 shorter events, 22.9 us)
Async XLA Ops:
  0.0 6.3 %copy-start = (s32[8,2]{0,1:T(2,128)S(1)}, s32[8,2]{0,1:T(2,128)}, u32[]{:S(2)}) copy-start(s32[8,2]{0,1:T(2,128)} %param.15) | copy-start | bytes 196
  0.0 19.0 %copy-start.13 = (bf16[1,512,512]{2,1,0:T(8,128)(2,1)S(1)}, bf16[1,512,512]{2,1,0:T(8,128)(2,1)}, u32[]{:S(2)}) copy-start(bf16[1,512,512]{2,1,0:T(8,128)(2,1)} %param.11) | copy-start | bytes 1572868
  1.0 18.0 %collective-permute-start = (bf16[256,512]{1,0:T(8,128)(2,1)S(1)}, bf16[256,512]{1,0:T(8,128)(2,1)S(1)}, u32[]{:S(2)}, u32[]{:S(2)}) collective-permute-start(bf16[256,512]{1,0:T(8,128)(2,1)S(1)} %dynamic-slice_bitcast_fusion), channel_id=1, source_target_pairs={{0,1},{1,0},{2,3},{3,2},{4,5},{5,4},{6,7},{7,6},{8,9},{9,8},{10,11... | collective-permute-start | bytes 786440 | tf_op jit(solution)/shard_map/ppermute | solution.py:19
  9.9 16.8 %copy-start.5 = (f32[4,128,128]{1,2,0:T(8,128)S(1)}, f32[4,128,128]{1,2,0:T(8,128)}, u32[]{:S(2)}) copy-start(f32[4,128,128]{1,2,0:T(8,128)} %constant.170.clone) | copy-start | bytes 786436
  19.0 22.5 %copy-start.6 = (f32[4,128,128]{1,2,0:T(8,128)S(1)}, f32[4,128,128]{1,2,0:T(8,128)}, u32[]{:S(2)}) copy-start(f32[4,128,128]{1,2,0:T(8,128)} %constant.169.clone) | copy-start | bytes 786436
  19.2 7.9 %collective-permute-start.1 = (bf16[128,512]{1,0:T(8,128)(2,1)S(1)}, bf16[128,512]{1,0:T(8,128)(2,1)S(1)}, u32[]{:S(2)}, u32[]{:S(2)}) collective-permute-start(bf16[128,512]{1,0:T(8,128)(2,1)S(1)} %constant_dynamic-slice_fusion.4), channel_id=1, source_target_pairs={{0,2},{1,3},{2,0},{3,1},{4,6},{5,7},{6,4},{7,5},{8,10},{9,11},{10,... | collective-permute-start | bytes 393224 | tf_op jit(solution)/shard_map/ppermute | solution.py:19
  26.8 5.7 %collective-permute-start.7 = (bf16[128,512]{1,0:T(8,128)(2,1)S(1)}, bf16[128,512]{1,0:T(8,128)(2,1)S(1)}, u32[]{:S(2)}, u32[]{:S(2)}) collective-permute-start(bf16[128,512]{1,0:T(8,128)(2,1)S(1)} %constant_dynamic-slice_fusion.2), channel_id=1, source_target_pairs={{0,2},{1,3},{2,0},{3,1},{4,6},{5,7},{6,4},{7,5},{8,10},{9,11},{10,... | collective-permute-start | bytes 393224 | tf_op jit(solution)/shard_map/ppermute | solution.py:19
  27.2 7.0 %collective-permute-start.2 = (bf16[64,512]{1,0:T(8,128)(2,1)S(1)}, bf16[64,512]{1,0:T(8,128)(2,1)S(1)}, u32[]{:S(2)}, u32[]{:S(2)}) collective-permute-start(bf16[64,512]{1,0:T(8,128)(2,1)S(1)} %constant_dynamic-slice_fusion.3), channel_id=1, source_target_pairs={{0,4},{1,5},{2,6},{3,7},{4,0},{5,1},{6,2},{7,3},{8,12},{9,13},{10,... | collective-permute-start | bytes 196616 | tf_op jit(solution)/shard_map/ppermute | solution.py:19
  32.6 4.3 %collective-permute-start.8 = (bf16[64,512]{1,0:T(8,128)(2,1)S(1)}, bf16[64,512]{1,0:T(8,128)(2,1)S(1)}, u32[]{:S(2)}, u32[]{:S(2)}) collective-permute-start(bf16[64,512]{1,0:T(8,128)(2,1)S(1)} %constant_dynamic-slice_fusion.1), channel_id=1, source_target_pairs={{0,4},{1,5},{2,6},{3,7},{4,0},{5,1},{6,2},{7,3},{8,12},{9,13},{10,... | collective-permute-start | bytes 196616 | tf_op jit(solution)/shard_map/ppermute | solution.py:19
  34.2 7.1 %collective-permute-start.3 = (bf16[64,512]{1,0:T(8,128)(2,1)S(1)}, bf16[64,512]{1,0:T(8,128)(2,1)S(1)}, u32[]{:S(2)}, u32[]{:S(2)}) collective-permute-start(bf16[64,512]{1,0:T(8,128)(2,1)S(1)} %dynamic-slice_add_fusion.3), channel_id=1, source_target_pairs={{0,8},{1,9},{2,10},{3,11},{4,12},{5,13},{6,14},{7,15},{8,0},{9,1},... | collective-permute-start | bytes 196616 | tf_op jit(solution)/shard_map/ppermute | solution.py:19
  36.9 5.5 %collective-permute-start.9 = (bf16[64,512]{1,0:T(8,128)(2,1)S(1)}, bf16[64,512]{1,0:T(8,128)(2,1)S(1)}, u32[]{:S(2)}, u32[]{:S(2)}) collective-permute-start(bf16[64,512]{1,0:T(8,128)(2,1)S(1)} %dynamic-slice_add_fusion.2), channel_id=1, source_target_pairs={{0,8},{1,9},{2,10},{3,11},{4,12},{5,13},{6,14},{7,15},{8,0},{9,1},... | collective-permute-start | bytes 196616 | tf_op jit(solution)/shard_map/ppermute | solution.py:19
  41.4 4.5 %collective-permute-start.4 = (bf16[64,512]{1,0:T(8,128)(2,1)S(1)}, bf16[64,512]{1,0:T(8,128)(2,1)S(1)}, u32[]{:S(2)}, u32[]{:S(2)}) collective-permute-start(bf16[64,512]{1,0:T(8,128)(2,1)S(1)} %add.153), channel_id=1, source_target_pairs={{0,4},{1,5},{2,6},{3,7},{4,0},{5,1},{6,2},{7,3},{8,12},{9,13},{10,... | collective-permute-start | bytes 196616 | tf_op jit(solution)/shard_map/ppermute | solution.py:19
  42.5 4.6 %collective-permute-start.10 = (bf16[64,512]{1,0:T(8,128)(2,1)S(1)}, bf16[64,512]{1,0:T(8,128)(2,1)S(1)}, u32[]{:S(2)}, u32[]{:S(2)}) collective-permute-start(bf16[64,512]{1,0:T(8,128)(2,1)S(1)} %add.156), channel_id=1, source_target_pairs={{0,4},{1,5},{2,6},{3,7},{4,0},{5,1},{6,2},{7,3},{8,12},{9,13},{10,... | collective-permute-start | bytes 196616 | tf_op jit(solution)/shard_map/ppermute | solution.py:19
  46.6 5.3 %collective-permute-start.5 = (bf16[128,512]{1,0:T(8,128)(2,1)}, bf16[128,512]{1,0:T(8,128)(2,1)}, u32[]{:S(2)}, u32[]{:S(2)}) collective-permute-start(bf16[128,512]{1,0:T(8,128)(2,1)} %pad_maximum_fusion.5), channel_id=1, source_target_pairs={{0,2},{1,3},{2,0},{3,1},{4,6},{5,7},{6,4},{7,5},{8,10},{9,11},{10,... | collective-permute-start | bytes 393224 | tf_op jit(solution)/shard_map/ppermute | solution.py:19
  47.1 6.1 %collective-permute-start.11 = (bf16[128,512]{1,0:T(8,128)(2,1)S(1)}, bf16[128,512]{1,0:T(8,128)(2,1)}, u32[]{:S(2)}, u32[]{:S(2)}) collective-permute-start(bf16[128,512]{1,0:T(8,128)(2,1)S(1)} %pad_maximum_fusion.6), channel_id=1, source_target_pairs={{0,2},{1,3},{2,0},{3,1},{4,6},{5,7},{6,4},{7,5},{8,10},{9,11},{10,... | collective-permute-start | bytes 393224 | tf_op jit(solution)/shard_map/ppermute | solution.py:19
  55.1 5.8 %copy-start.9 = (bf16[128,512]{1,0:T(8,128)(2,1)}, bf16[128,512]{1,0:T(8,128)(2,1)S(1)}, u32[]{:S(2)}) copy-start(bf16[128,512]{1,0:T(8,128)(2,1)S(1)} %get-tuple-element.37) | copy-start | bytes 393220
  55.8 9.6 %collective-permute-start.12 = (bf16[256,512]{1,0:T(8,128)(2,1)}, bf16[256,512]{1,0:T(8,128)(2,1)}, u32[]{:S(2)}, u32[]{:S(2)}) collective-permute-start(bf16[256,512]{1,0:T(8,128)(2,1)} %pad_maximum_fusion.3), channel_id=1, source_target_pairs={{0,1},{1,0},{2,3},{3,2},{4,5},{5,4},{6,7},{7,6},{8,9},{9,8},{10,11... | collective-permute-start | bytes 786440 | tf_op jit(solution)/shard_map/ppermute | solution.py:19
  62.3 4.2 %copy-start.7 = (bf16[128,512]{1,0:T(8,128)(2,1)S(1)}, bf16[128,512]{1,0:T(8,128)(2,1)}, u32[]{:S(2)}) copy-start(bf16[128,512]{1,0:T(8,128)(2,1)} %get-tuple-element.67) | copy-start | bytes 393220
  62.4 4.4 %copy-start.1 = (bf16[4,256,176]{2,1,0:T(8,128)(2,1)S(1)}, bf16[4,256,176]{2,1,0:T(8,128)(2,1)}, u32[]{:S(2)}) copy-start(bf16[4,256,176]{2,1,0:T(8,128)(2,1)} %copy.38.rih) | copy-start | bytes 1081348
  62.4 4.4 %copy-start.2 = (bf16[4,256,176]{2,1,0:T(8,128)(2,1)S(1)}, bf16[4,256,176]{2,1,0:T(8,128)(2,1)}, u32[]{:S(2)}) copy-start(bf16[4,256,176]{2,1,0:T(8,128)(2,1)} %copy.39.ril) | copy-start | bytes 1081348
  64.8 1.8 %collective-permute-start.6 = (bf16[256,512]{1,0:T(8,128)(2,1)S(1)}, bf16[256,512]{1,0:T(8,128)(2,1)S(1)}, u32[]{:S(2)}, u32[]{:S(2)}) collective-permute-start(bf16[256,512]{1,0:T(8,128)(2,1)S(1)} %pad_maximum_fusion.2), channel_id=1, source_target_pairs={{0,1},{1,0},{2,3},{3,2},{4,5},{5,4},{6,7},{7,6},{8,9},{9,8},{10,11... | collective-permute-start | bytes 786440 | tf_op jit(solution)/shard_map/ppermute | solution.py:19
  66.8 16.7 %copy-start.3 = (bf16[4,128,176]{2,1,0:T(8,128)(2,1)S(1)}, bf16[4,128,176]{2,1,0:T(8,128)(2,1)}, u32[]{:S(2)}) copy-start(bf16[4,128,176]{2,1,0:T(8,128)(2,1)} %get-tuple-element.32.dh) | copy-start | bytes 540676
  95.7 5.8 %collective-permute-start.13 = (f32[2,2,32,256]{3,2,1,0:T(8,128)S(1)}, f32[2,2,32,256]{3,2,1,0:T(8,128)S(1)}, u32[]{:S(2)}, u32[]{:S(2)}) collective-permute-start(f32[2,2,32,256]{3,2,1,0:T(8,128)S(1)} %dynamic-slice_bitcast_fusion.1), channel_id=1, source_target_pairs={{0,2},{1,3},{2,0},{3,1},{4,6},{5,7},{6,4},{7,5},{8,10},{9,11},{10,... | collective-permute-start | bytes 393224 | tf_op jit(solution)/shard_map/ppermute | solution.py:19
  102.4 1.4 %collective-permute-start.14 = (f32[2,2,2,16,256]{4,3,2,1,0:T(8,128)S(1)}, f32[2,2,2,16,256]{4,3,2,1,0:T(8,128)S(1)}, u32[]{:S(2)}, u32[]{:S(2)}) collective-permute-start(f32[2,2,2,16,256]{4,3,2,1,0:T(8,128)S(1)} %fusion.13), channel_id=1, source_target_pairs={{0,1},{1,0},{2,3},{3,2},{4,5},{5,4},{6,7},{7,6},{8,9},{9,8},{10,11... | collective-permute-start | bytes 393224 | tf_op jit(solution)/shard_map/ppermute | solution.py:19
  (5 other events, 11.2 us)
where the time goes:
time: 105 us
  Pallas kernels  28.2 us (27%)
  other arithmetic  26.9 us (26%)
  starting transfers between devices  17.8 us (17%)
  waiting for transfers between devices  14.6 us (14%)
  local copies, waits for them, and re-layouts  9.42 us (9%)
  matrix products  4.98 us (5%)
  between operations  2.94 us (3%)
    pallas_call x2, Pallas kernels, run_kernel(): pl.pallas_call(kernel, name=name, grid=(waves.shape[0],), in_specs=[whole...  28.2 us
    ppermute x15, starting transfers between devices, flip(): return lax.ppermute(array, 'wide', [(i, i ^ bit) for i in range(groups)])  17.8 us
    ppermute x15, waiting for transfers between devices, flip(): return lax.ppermute(array, 'wide', [(i, i ^ bit) for i in range(groups)])  14.6 us
    convert_element_type x5, other arithmetic, split_table(): return (high.astype(BF16), (table - high).astype(BF16))  7.37 us
    dot_general x1, matrix products, probe_waves(): jnp.einsum('pxb,rby->prxy', left, right, precision=lax.Precision.HIGHEST)  4.98 us
    convert_element_type x4, local copies, waits for them, and re-layouts, split_table(): return (high.astype(BF16), (table - high).astype(BF16))  4.46 us
    select_n x5, other arithmetic, spread_slabs(): low = jnp.where(side == 0, part, other)  3.1 us
    mul x1, other arithmetic, make_propagator(): return (jnp.cos(turning) * keep, jnp.sin(turning) * keep)  2.73 us
  transfers between devices with their start and end apart: 15, of which 7 were waited for; matrix products, arithmetic and copies ran while one was open for 33% of the time, Pallas kernels for 0%

commit v1 on v0

v1 whole, which is shorter than its diff:
```python
import functools
import math

import jax
import jax.numpy as jnp
import numpy as np
from jax import lax
from jax.experimental import pallas as pl
from jax.experimental.pallas import tpu as pltpu
from jax.sharding import PartitionSpec as P

FRESNEL = 4.7e-05
TWO_PI = 2.0 * math.pi
F32 = jnp.float32
BF16 = jnp.bfloat16
QUAD = 4
ROW_STEPS = 2


def flip(array, bit, groups):
    return lax.ppermute(array, "wide", [(i, i ^ bit) for i in range(groups)])


def half(array, which):
    rows = array.shape[0] // 2
    return lax.dynamic_slice_in_dim(array, which * rows, rows, 0)


def spread_slabs(own_slab, slice_owner, groups, device):
    count = slice_owner.shape[0]
    bits = [1 << b for b in range(groups.bit_length() - 1)]
    side = device & 1
    own = side
    kept = half(own_slab, side)
    received = flip(half(own_slab, 1 - side), 1, groups)
    zero = jnp.zeros_like(kept)
    parts = [
        jnp.where(slice_owner[s] == device, kept, jnp.where(slice_owner[s] == (device ^ 1), received, zero))
        for s in range(count)
    ]
    for bit in bits[1:-1]:
        side = (device // bit) & 1
        own = own * 2 + side
        parts = [half(part, side) + flip(half(part, 1 - side), bit, groups) for part in parts]
    parts = [part + flip(part, bits[-1], groups) for part in parts]
    for bit in reversed(bits[:-1]):
        parts = [jnp.concatenate([part, flip(part, bit, groups)], axis=0) for part in parts]
    return parts, own.astype(jnp.int32).reshape(1)


def class_frequencies(grid):
    top = grid // 3
    freq = np.zeros((4, grid // 4), np.int32)
    real = np.zeros((4, grid // 4), np.float32)
    longest = 0
    for c in range(4):
        members = [u for u in range(-top, top + 1) if u % 4 == c]
        freq[c, : len(members)] = members
        real[c, : len(members)] = 1.0
        longest = max(longest, len(members))
    return freq, real, -(-longest // 16) * 16


def cos_turns(turns, grid):
    turns = (turns + grid // 2) & (grid - 1)
    h = (turns - grid // 2).astype(F32) * (math.pi / grid)
    t = h * h
    p = -1.0 / math.factorial(11)
    for n in (9, 7, 5, 3, 1):
        p = p * t + (1.0 if n % 4 == 1 else -1.0) / math.factorial(n)
    s = h * p
    return 1.0 - 2.0 * (s * s)


def table_kernel(first_ref, cos_ref, sin_ref, rowf, lanef, lanew, lanep, wh, wl, vh, vl, pr, pi, dh, dl):
    q = cos_ref.shape[1]
    n = 4 * q
    kp = pr.shape[1]
    take = dh.shape[1] // 2
    for c in range(4):
        cos, sin = cos_ref[c], sin_ref[c]
        for a, b, part in ((0, 0, cos), (0, 1, -sin), (1, 0, sin), (1, 1, cos)):
            wh[c, a * q : (a + 1) * q, b * q : (b + 1) * q], wl[c, a * q : (a + 1) * q, b * q : (b + 1) * q] = split(part)
        cos, sin = cos.T, sin.T
        for a, b, part in ((0, 0, cos), (0, 1, sin), (1, 0, -sin), (1, 1, cos)):
            vh[c, a * q : (a + 1) * q, b * q : (b + 1) * q], vl[c, a * q : (a + 1) * q, b * q : (b + 1) * q] = split(part)
        for l in range(4):
            lanes = pl.ds(l * q, q)
            squared = rowf[c] + lanef[:, lanes]
            kept = 9.0 * squared <= float(n * n)
            re, im = cos_sin(jnp.where(kept, FRESNEL * squared, 0.0))
            pr[c, :, lanes] = jnp.where(kept, re * (1.0 / (n * n)), 0.0)
            pi[c, :, lanes] = jnp.where(kept, im * (-1.0 / (n * n)), 0.0)
        row = lax.broadcasted_iota(jnp.int32, (2 * take, 2 * q), 0)
        x = first_ref[0] + jnp.where(row < take, row, row - take)
        shift = lanep[...] - jnp.where(row < take, 0, n // 4)
        dh[c], dl[c] = split(cos_turns(x * lanew[c, 0] + shift, n) * lanew[c, 1].astype(F32))


def make_tables(grid, first_row, rows):
    freq, real, kp = class_frequencies(grid)
    q = grid // 4
    turns = np.mod(freq[:, None, :].astype(np.int64) * np.arange(q)[None, :, None], grid)
    angle = TWO_PI * turns / grid
    cos = (np.cos(angle) * real[:, None, :]).astype(np.float32)
    sin = (np.sin(angle) * real[:, None, :]).astype(np.float32)
    square = np.where(real > 0, freq.astype(np.float32) ** 2, float(grid * grid)).astype(np.float32)
    lane_pair = np.stack([np.tile(freq, (1, 2)), np.tile(real, (1, 2)).astype(np.int32)], axis=1)[:, :, None, :]
    lane_shift = np.repeat(np.array([0, grid // 4], np.int32), q)[None, :]
    inputs = (cos, sin, square[:, :kp, None], square.reshape(1, grid), lane_pair, lane_shift)
    inputs = [jnp.asarray(v) for v in inputs]
    full = jax.ShapeDtypeStruct((4, 2 * q, 2 * q), BF16)
    prop = jax.ShapeDtypeStruct((4, kp, grid), F32)
    last = jax.ShapeDtypeStruct((4, 2 * rows, 2 * q), BF16)
    vmem = pl.BlockSpec(memory_space=pltpu.VMEM)
    out = pl.pallas_call(
        table_kernel,
        name="tables",
        in_specs=[pl.BlockSpec(memory_space=pltpu.SMEM)] + [vmem] * len(inputs),
        out_specs=[vmem] * 8,
        out_shape=[full, full, full, full, prop, prop, last, last],
        compiler_params=pltpu.CompilerParams(vmem_limit_bytes=16 << 20),
    )(first_row.astype(jnp.int32).reshape(1), *inputs)
    return out[0:2], out[2:4], out[4:6], out[6:8]


def wave_kernel(row_freq, row_turn, row_weight, row_low, col_freq, col_turn, col_low, out_ref):
    n = out_ref.shape[2]
    k = row_freq.shape[1]

    def pick(value, low):
        high = value.astype(BF16).astype(F32)
        return jnp.where(low > 0, value - high, high).astype(BF16)

    x = lax.broadcasted_iota(jnp.int32, (n, k), 0)
    left = pick(cos_turns(x * row_freq[...] + row_turn[0], n) * row_weight[...], row_low[...])
    y = lax.broadcasted_iota(jnp.int32, (k, n), 1)
    for part in range(2):
        right = pick(cos_turns(y * col_freq[...] + col_turn[part], n), col_low[...])
        out_ref[0, part] = dot(left, right)


def probe_waves(grid, beam_index, aperture, position):
    beams = beam_index.shape[0]
    quarter = grid // 4
    zeros = np.zeros(beams, np.int32)
    k = 6 * beams
    row_freq = jnp.tile(beam_index[:, 0], 6).reshape(1, k)
    mixing = beam_index[:, 0][None, :] * position[:, 0][:, None] + beam_index[:, 1][None, :] * position[:, 1][:, None]
    row_turn = (np.tile(np.concatenate([zeros, zeros - quarter]), 3)[None, :] - jnp.tile(mixing, (1, 6)))[:, None, :]
    weight = jnp.tile(aperture.astype(F32) / math.sqrt(beams), 6).reshape(1, k)
    group = np.repeat(np.arange(3, dtype=np.int32), 2 * beams)
    col_freq = jnp.tile(beam_index[:, 1], 6).reshape(k, 1)
    col_turn = np.stack([np.tile(np.concatenate([zeros, zeros + quarter]), 3), np.tile(np.concatenate([zeros - quarter, zeros]), 3)])
    inputs = (row_freq, row_turn, weight, jnp.asarray((group == 1).astype(np.int32)[None, :]), col_freq, jnp.asarray(col_turn[:, :, None]), jnp.asarray((group == 2).astype(np.int32)[:, None]))
    shape = (position.shape[0], 2, grid, grid)
    specs = [whole(v) for v in inputs]
    specs[1] = one(row_turn.shape)
    return pl.pallas_call(
        wave_kernel,
        name="probe_waves",
        grid=(shape[0],),
        in_specs=specs,
        out_specs=one(shape),
        out_shape=jax.ShapeDtypeStruct(shape, F32),
        compiler_params=pltpu.CompilerParams(vmem_limit_bytes=16 << 20),
    )(*inputs)


def split(x):
    high = x.astype(BF16)
    return high, (x - high.astype(F32)).astype(BF16)


def dot(a, b):
    return jnp.dot(a, b, preferred_element_type=F32)


def dot3(ah, al, bh, bl):
    return dot(ah, bh) + dot(al, bh) + dot(ah, bl)


def butterfly(parts, sign):
    (r0, i0), (r1, i1), (r2, i2), (r3, i3) = parts
    sr, si, dr, di = r0 + r2, i0 + i2, r0 - r2, i0 - i2
    tr, ti, er, ei = r1 + r3, i1 + i3, r1 - r3, i1 - i3
    up = (dr - sign * ei, di + sign * er)
    down = (dr + sign * ei, di - sign * er)
    return [(sr + tr, si + ti), up, (sr - tr, si - ti), down]


def chebyshev(function, top, terms):
    fit = np.polynomial.chebyshev.Chebyshev.interpolate(function, terms - 1, domain=[0.0, top])
    return [float(v) for v in fit.convert(kind=np.polynomial.Polynomial).coef]


COS = chebyshev(lambda t: np.cos(np.sqrt(t)), 2.56, 5)
SIN = chebyshev(lambda t: np.sinc(np.sqrt(t) / np.pi), 2.56, 5)


def horner(coefficients, t):
    value = coefficients[-1]
    for coefficient in coefficients[-2::-1]:
        value = value * t + coefficient
    return value


def cos_sin(v):
    t = v * v
    return horner(COS, t), v * horner(SIN, t)


def transmit_tables(own_ref, slab_ref, tr_ref, ti_ref, blocks):
    n = slab_ref.shape[0]
    q = n // 4
    block_rows = n // blocks
    rows = min(32, block_rows)

    def body(b, carry):
        first = pl.multiple_of(b * rows, rows)
        place = ((first // block_rows) ^ own_ref[0]) * block_rows + first % block_rows
        place = pl.multiple_of(place, rows)
        for j in range(4):
            lanes = pl.ds(j * q, q)
            c, s = cos_sin(slab_ref[pl.ds(first, rows), lanes].astype(F32))
            tr_ref[pl.ds(place, rows), lanes] = c
            ti_ref[pl.ds(place, rows), lanes] = s
        return carry

    lax.fori_loop(0, n // rows, body, 0)


def forward(wave_ref, tr_ref, ti_ref, wh, wl, vh, vl, pr, pi, scratch, after):
    yh, yl, sr, si, zh, zl, uh, ul = scratch
    n = tr_ref.shape[0]
    q = n // 4
    kp = pr.shape[1]
    rows = 32

    def fold_lanes(first):
        at = pl.ds(first, rows)
        parts = []
        for j in range(4):
            lanes = pl.ds(j * q, q)
            wr, wi = wave_ref[0, 0, at, lanes], wave_ref[0, 1, at, lanes]
            cr, ci = tr_ref[at, lanes], ti_ref[at, lanes]
            parts.append((wr * cr - wi * ci, wr * ci + wi * cr))
        for c, (r, i) in enumerate(butterfly(parts, -1.0)):
            yh[c, at, :q], yl[c, at, :q] = split(r)
            yh[c, at, q:], yl[c, at, q:] = split(i)

    def fold_rows(l):
        lanes = pl.ds(l * q, q)
        for first in range(0, q, rows):
            parts = [(sr[pl.ds(j * q + first, rows), lanes], si[pl.ds(j * q + first, rows), lanes]) for j in range(4)]
            for c, (r, i) in enumerate(butterfly(parts, -1.0)):
                zh[c, pl.ds(first, rows), lanes], zl[c, pl.ds(first, rows), lanes] = split(r)
                zh[c, pl.ds(q + first, rows), lanes], zl[c, pl.ds(q + first, rows), lanes] = split(i)

    step = n // ROW_STEPS
    for b in range(ROW_STEPS):
        for first in range(b * step, (b + 1) * step, rows):
            fold_lanes(first)
        at = pl.ds(b * step, step)
        for c in range(4):
            out = dot3(yh[c, at], yl[c, at], wh[c], wl[c])
            sr[at, c * q : (c + 1) * q] = out[:, :q]
            si[at, c * q : (c + 1) * q] = out[:, q:]
            if b == ROW_STEPS - 1:
                fold_rows(c)
    for h in range(2):
        lanes = pl.ds(h * 2 * q, 2 * q)
        for c in range(4):
            zhc, zlc = zh[c, :, lanes], zl[c, :, lanes]
            r = dot3(vh[c, :kp], vl[c, :kp], zhc, zlc)
            i = dot3(vh[c, q : q + kp], vl[c, q : q + kp], zhc, zlc)
            re, im = pr[c, :, lanes], pi[c, :, lanes]
            uh[c, :kp, lanes], ul[c, :kp, lanes] = split(r * re - i * im)
            uh[c, q : q + kp, lanes], ul[c, q : q + kp, lanes] = split(r * im + i * re)
        after(h)


def first_kernel(blocks, own_ref, slab_ref, wave_ref, wh, wl, vh, vl, pr, pi, out_ref, tr, ti, yh, yl, sr, si, zh, zl, uh, ul, g, hr):
    n = slab_ref.shape[0]
    q = n // 4
    rows = 32

    @pl.when(pl.program_id(0) == 0)
    def _():
        transmit_tables(own_ref, slab_ref, tr, ti, blocks)
        uh[...] = jnp.zeros_like(uh)
        ul[...] = jnp.zeros_like(ul)

    def unfold_rows(l):
        lanes = pl.ds(l * q, q)
        for first in range(0, q, rows):
            parts = [(g[c, pl.ds(first, rows), lanes], g[c, pl.ds(q + first, rows), lanes]) for c in range(4)]
            for j, (r, i) in enumerate(butterfly(parts, 1.0)):
                at = pl.ds(j * q + first, rows)
                yh[l, at, :q], yl[l, at, :q] = split(r)
                yh[l, at, q:], yl[l, at, q:] = split(i)

    def after(h):
        lanes = pl.ds(h * 2 * q, 2 * q)
        for c in range(4):
            g[c, :, lanes] = dot3(wh[c], wl[c], uh[c, :, lanes], ul[c, :, lanes])
        for l in (2 * h, 2 * h + 1):
            unfold_rows(l)

    forward(wave_ref, tr, ti, wh, wl, vh, vl, pr, pi, (yh, yl, sr, si, zh, zl, uh, ul), after)
    step = n // ROW_STEPS
    for b in range(ROW_STEPS):
        at = pl.ds(b * step, step)
        for c in range(4):
            hr[c, at] = dot3(yh[c, at], yl[c, at], vh[c], vl[c])
        for first in range(b * step, (b + 1) * step, rows):
            at = pl.ds(first, rows)
            parts = [(hr[c, at, :q], hr[c, at, q:]) for c in range(4)]
            for j, (r, i) in enumerate(butterfly(parts, 1.0)):
                out_ref[0, 0, at, pl.ds(j * q, q)] = r
                out_ref[0, 1, at, pl.ds(j * q, q)] = i


def last_kernel(blocks, own_ref, slab_ref, wave_ref, wh, wl, vh, vl, pr, pi, dh, dl, out_ref, tr, ti, yh, yl, sr, si, zh, zl, uh, ul):
    n = slab_ref.shape[0]
    q = n // 4
    take = dh.shape[1] // 2

    @pl.when(pl.program_id(0) == 0)
    def _():
        transmit_tables(own_ref, slab_ref, tr, ti, blocks)
        uh[...] = jnp.zeros_like(uh)
        ul[...] = jnp.zeros_like(ul)

    half_out = []

    def after(h):
        lanes = pl.ds(h * 2 * q, 2 * q)
        out = dot3(dh[0], dl[0], uh[0, :, lanes], ul[0, :, lanes])
        for c in range(1, 4):
            out = out + dot3(dh[c], dl[c], uh[c, :, lanes], ul[c, :, lanes])
        half_out.append(out)

    forward(wave_ref, tr, ti, wh, wl, vh, vl, pr, pi, (yh, yl, sr, si, zh, zl, uh, ul), after)
    parts = []
    for c in range(4):
        lanes = slice(c % 2 * q, c % 2 * q + q)
        out = half_out[c // 2]
        high, low = split(jnp.concatenate([out[:take, lanes], out[take:, lanes]], axis=1))
        back = dot3(high, low, vh[c], vl[c])
        parts.append((back[:, :q], back[:, q:]))
    for j, (r, i) in enumerate(butterfly(parts, 1.0)[1:3]):
        out_ref[0, 0, :, j * q : (j + 1) * q] = r
        out_ref[0, 1, :, j * q : (j + 1) * q] = i


def whole(array):
    return pl.BlockSpec(array.shape, lambda p: (0,) * array.ndim, pipeline_mode=pl.Buffered(1))


def one(shape):
    return pl.BlockSpec((1,) + shape[1:], lambda p: (p,) + (0,) * (len(shape) - 1))


def forward_scratch(n):
    q = n // 4
    return [
        pltpu.VMEM((n, n), F32),
        pltpu.VMEM((n, n), F32),
        pltpu.VMEM((4, n, 2 * q), BF16),
        pltpu.VMEM((4, n, 2 * q), BF16),
        pltpu.VMEM((n, n), F32),
        pltpu.VMEM((n, n), F32),
        pltpu.VMEM((4, 2 * q, n), BF16),
        pltpu.VMEM((4, 2 * q, n), BF16),
        pltpu.VMEM((4, 2 * q, n), BF16),
        pltpu.VMEM((4, 2 * q, n), BF16),
    ]


def run_kernel(kernel, name, own, slab, waves, tables, out_shape, extra, blocks):
    n = slab.shape[0]
    return pl.pallas_call(
        functools.partial(kernel, blocks),
        name=name,
        grid=(waves.shape[0],),
        in_specs=[pl.BlockSpec(memory_space=pltpu.SMEM), whole(slab), one(waves.shape)] + [whole(t) for t in tables],
        out_specs=one(out_shape),
        out_shape=jax.ShapeDtypeStruct(out_shape, F32),
        scratch_shapes=forward_scratch(n) + extra,
        compiler_params=pltpu.CompilerParams(vmem_limit_bytes=40 << 20),
    )(own, slab, waves, *tables)


def local(potential_pool, slice_owner, beam_index, aperture, probe_position):
    grid = potential_pool.shape[-1]
    crop = grid // 2
    margin = grid // 4
    q = grid // 4
    groups = lax.axis_size("wide")
    device = lax.axis_index("wide")
    probes = probe_position.shape[0]
    per_device = probes // QUAD
    quad_rows = crop // (groups // QUAD)
    own_rows = crop // groups
    place = device % QUAD
    quad = device // QUAD

    slabs, own = spread_slabs(potential_pool[0], slice_owner, groups, device)
    blocks = groups // 2

    position = lax.dynamic_slice_in_dim(probe_position, place * per_device, per_device, 0)
    waves = probe_waves(grid, beam_index, aperture, position)
    forward_table, inverse_table, prop, last_rows = make_tables(grid, margin + quad * quad_rows, quad_rows)
    tables = (*forward_table, *inverse_table, *prop)

    for slab in slabs[:-1]:
        extra = [pltpu.VMEM((4, 2 * q, grid), F32), pltpu.VMEM((4, grid, 2 * q), F32)]
        waves = run_kernel(first_kernel, "slice_full", own, slab, waves, tables, waves.shape, extra, blocks)
    cut_shape = (per_device, 2, quad_rows, crop)
    cut = run_kernel(last_kernel, "slice_last", own, slabs[-1], waves, (*tables, *last_rows), cut_shape, [], blocks)

    side = (place // 2) & 1
    pair = cut.reshape(per_device, 2, 2, quad_rows // 2, crop)
    kept = lax.dynamic_index_in_dim(pair, side, 2, False)
    other = flip(lax.dynamic_index_in_dim(pair, 1 - side, 2, False), 2, groups)
    both = jnp.stack([jnp.where(side == 0, kept, other), jnp.where(side == 0, other, kept)])
    side = place & 1
    pair = both.reshape(2, per_device, 2, 2, own_rows, crop)
    kept = lax.dynamic_index_in_dim(pair, side, 3, False)
    other = flip(lax.dynamic_index_in_dim(pair, 1 - side, 3, False), 1, groups)
    all_probes = jnp.stack([jnp.where(side == 0, kept, other), jnp.where(side == 0, other, kept)], axis=1)
    return jnp.transpose(all_probes.reshape(probes, 2, own_rows, crop), (2, 1, 0, 3))


def solution(mesh):
    placed = (P(("parts", "wide"), None, None), P("parts"), P(), P(), P("parts", None))
    return jax.shard_map(
        local,
        mesh=mesh,
        in_specs=placed,
        out_specs=P(("parts", "wide"), None, None, None),
        check_vma=False,
    )
```

time: 105 us -> 68.9 us (0.66)
  other arithmetic: 26.9 us -> 1.52 us
  Pallas kernels: 28.2 us -> 22.6 us
  matrix products: 4.98 us -> 0 us
  local copies, waits for them, and re-layouts: 9.42 us -> 4.63 us
  starting transfers between devices: 17.8 us -> 22.2 us
    convert_element_type x5 -> x0, other arithmetic: 7.37 us -> none  [split_table(): return (high.astype(BF16), (table - high).astype(BF16))]
    neg x5 -> x0, other arithmetic: 5.65 us -> none  [the longest x1 2.04 us: rows_table(): return split_table(block(cos, -sin, sin, cos))]
    pallas_call x2 -> x4, Pallas kernels: 28.2 us -> 22.6 us  [the longest x2 19.1 us: run_kernel(): pl.pallas_call(functools.partial(kernel, blocks), name=name, grid=(waves....]
    dot_general x1 -> x0, matrix products: 4.98 us -> none  [probe_waves(): jnp.einsum('pxb,rby->prxy', left, right, precision=lax.Precision.HIGHEST)]
    convert_element_type x4 -> x0, local copies, waits for them, and re-layouts: 4.46 us -> none  [split_table(): return (high.astype(BF16), (table - high).astype(BF16))]
    ppermute x15, starting transfers between devices: 17.8 us -> 22.2 us  [flip(): return lax.ppermute(array, 'wide', [(i, i ^ bit) for i in range(groups)])]
    mul x4 -> x0, other arithmetic: 4.38 us -> none  [the longest x1 2.73 us: make_propagator(): return (jnp.cos(turning) * keep, jnp.sin(turning) * keep)]
    select_n x5 -> x0, other arithmetic: 3.1 us -> none  [spread_slabs(): low = jnp.where(side == 0, part, other)]
  transfers between devices with their start and end apart: 15 -> 15, of which waited for: 7 -> 7; matrix products, arithmetic and copies ran while one was open for 33% -> 4% of each run, Pallas kernels for 0% -> 21%
where the time goes in v1:
time: 68.9 us; the launch traced here: 68.5 us
  Pallas kernels  22.6 us (33%)
  starting transfers between devices  22.2 us (32%)
  waiting for transfers between devices  14.5 us (21%)
  local copies, waits for them, and re-layouts  4.63 us (7%)
  between operations  3.01 us (4%)
  other arithmetic  1.52 us (2%)
    ppermute x15, starting transfers between devices, flip(): return lax.ppermute(array, 'wide', [(i, i ^ bit) for i in range(groups)])  22.2 us
    pallas_call x2, Pallas kernels, run_kernel(): pl.pallas_call(functools.partial(kernel, blocks), name=name, grid=(waves....  19.1 us
    ppermute x15, waiting for transfers between devices, flip(): return lax.ppermute(array, 'wide', [(i, i ^ bit) for i in range(groups)])  14.5 us
    pallas_call x1, Pallas kernels, probe_waves(): pl.pallas_call(wave_kernel, name='probe_waves', grid=(shape[0],), in_spec...  2.03 us
    pallas_call x1, Pallas kernels, make_tables(): pl.pallas_call(table_kernel, name='tables', in_specs=[pl.BlockSpec(memory...  1.47 us
    slice x1, local copies, waits for them, and re-layouts, spread_slabs(): slice_owner[s] == device  1.38 us
  transfers between devices with their start and end apart: 15, of which 7 were waited for; matrix products, arithmetic and copies ran while one was open for 4% of the time, Pallas kernels for 21%

profile of v1, /device:TPU:0, one launch (start us, length us, event | category | flops | bytes accessed | tf_op | source)
XLA Modules:
  0.0 68.5 jit_solution(2439299194747356954)
XLA Ops:
  0.0 1.1 %dynamic-slice_bitcast_fusion = bf16[256,512]{1,0:T(8,128)(2,1)S(1)} fusion(bf16[1,512,512]{2,1,0:T(8,128)(2,1)} %param.15, s32[]{:T(128)S(6)} %select_n.116), kind=kLoop, calls=%fused_computation.11 | loop fusion | bytes 524292 | tf_op jit(solution)/shard_map/dynamic_slice | solution.py:26
  1.7 1.4 %fusion.4 = (s32[1]{0:T(128)}, s32[1]{0:T(128)}) fusion(s32[2]{0:T(128)} %param.16), kind=kLoop, calls=%fused_computation.38 | loop fusion | bytes 16 | tf_op jit(solution)/shard_map/slice | solution.py:38
  5.7 1.1 %bitcast_select_fusion = (bf16[256,512]{1,0:T(8,128)(2,1)S(1)}, bf16[256,512]{1,0:T(8,128)(2,1)S(1)}) fusion(bf16[256,512]{1,0:T(8,128)(2,1)S(1)} %collective-permute-done, pred[]{:T(512)S(6)} %eq.27, pred[]{:T(512)S(6)} %eq.26, bf16[1,512,512]{2,1,0:T(8,128)(2,1)} %param.15, s32[]{:T(128)S(6)} %select_n.114, pred[]{:T(512)S(6)} %eq.25, pred[]{:T(512)S(6)} %eq.24), kind=kLoop, calls=%fused_computation.9 | loop fusion | flops 524288 | bytes 1048584 | tf_op jit(solution)/shard_map/jit(_where)/select_n | solution.py:38
  6.9 2.6 %collective-permute-start.7 = (bf16[128,512]{1,0:T(8,128)(2,1)S(1)}, bf16[128,512]{1,0:T(8,128)(2,1)S(1)}, u32[]{:S(2)}, u32[]{:S(2)}) collective-permute-start(bf16[128,512]{1,0:T(8,128)(2,1)S(1)} %constant_dynamic-slice_fusion.2), channel_id=1, source_target_pairs={{0,2},{1,3},{2,0},{3,1},{4,6},{5,7},{6,4},{7,5},{8,10},{9,11},{10,... | collective-permute-start | bytes 393224 | tf_op jit(solution)/shard_map/ppermute | solution.py:21
  9.6 4.2 %collective-permute-done.7 = bf16[128,512]{1,0:T(8,128)(2,1)S(1)} collective-permute-done((bf16[128,512]{1,0:T(8,128)(2,1)S(1)}, bf16[128,512]{1,0:T(8,128)(2,1)S(1)}, u32[]{:S(2)}, u32[]{:S(2)}) %collective-permute-start.7) | collective-permute-done | bytes 131104 | tf_op jit(solution)/shard_map/ppermute | solution.py:21
  13.9 2.1 %collective-permute-start.8 = (bf16[64,512]{1,0:T(8,128)(2,1)S(1)}, bf16[64,512]{1,0:T(8,128)(2,1)S(1)}, u32[]{:S(2)}, u32[]{:S(2)}) collective-permute-start(bf16[64,512]{1,0:T(8,128)(2,1)S(1)} %constant_dynamic-slice_fusion.1), channel_id=1, source_target_pairs={{0,4},{1,5},{2,6},{3,7},{4,0},{5,1},{6,2},{7,3},{8,12},{9,13},{10,... | collective-permute-start | bytes 196616 | tf_op jit(solution)/shard_map/ppermute | solution.py:21
  16.5 1.9 %collective-permute-start.2 = (bf16[64,512]{1,0:T(8,128)(2,1)S(1)}, bf16[64,512]{1,0:T(8,128)(2,1)S(1)}, u32[]{:S(2)}, u32[]{:S(2)}) collective-permute-start(bf16[64,512]{1,0:T(8,128)(2,1)S(1)} %constant_dynamic-slice_fusion.3), channel_id=1, source_target_pairs={{0,4},{1,5},{2,6},{3,7},{4,0},{5,1},{6,2},{7,3},{8,12},{9,13},{10,... | collective-permute-start | bytes 196616 | tf_op jit(solution)/shard_map/ppermute | solution.py:21
  18.4 3.0 %collective-permute-start.9 = (bf16[64,512]{1,0:T(8,128)(2,1)S(1)}, bf16[64,512]{1,0:T(8,128)(2,1)S(1)}, u32[]{:S(2)}, u32[]{:S(2)}) collective-permute-start(bf16[64,512]{1,0:T(8,128)(2,1)S(1)} %dynamic-slice_add_fusion.2), channel_id=1, source_target_pairs={{0,8},{1,9},{2,10},{3,11},{4,12},{5,13},{6,14},{7,15},{8,0},{9,1},... | collective-permute-start | bytes 196616 | tf_op jit(solution)/shard_map/ppermute | solution.py:21
  21.4 2.4 %collective-permute-start.3 = (bf16[64,512]{1,0:T(8,128)(2,1)S(1)}, bf16[64,512]{1,0:T(8,128)(2,1)S(1)}, u32[]{:S(2)}, u32[]{:S(2)}) collective-permute-start(bf16[64,512]{1,0:T(8,128)(2,1)S(1)} %dynamic-slice_add_fusion.3), channel_id=1, source_target_pairs={{0,8},{1,9},{2,10},{3,11},{4,12},{5,13},{6,14},{7,15},{8,0},{9,1},... | collective-permute-start | bytes 196616 | tf_op jit(solution)/shard_map/ppermute | solution.py:21
  23.8 2.9 %collective-permute-start.10 = (bf16[64,512]{1,0:T(8,128)(2,1)S(1)}, bf16[64,512]{1,0:T(8,128)(2,1)S(1)}, u32[]{:S(2)}, u32[]{:S(2)}) collective-permute-start(bf16[64,512]{1,0:T(8,128)(2,1)S(1)} %add.96), channel_id=1, source_target_pairs={{0,4},{1,5},{2,6},{3,7},{4,0},{5,1},{6,2},{7,3},{8,12},{9,13},{10,... | collective-permute-start | bytes 196616 | tf_op jit(solution)/shard_map/ppermute | solution.py:21
  27.5 1.1 %collective-permute-start.4 = (bf16[64,512]{1,0:T(8,128)(2,1)S(1)}, bf16[64,512]{1,0:T(8,128)(2,1)S(1)}, u32[]{:S(2)}, u32[]{:S(2)}) collective-permute-start(bf16[64,512]{1,0:T(8,128)(2,1)S(1)} %add.93), channel_id=1, source_target_pairs={{0,4},{1,5},{2,6},{3,7},{4,0},{5,1},{6,2},{7,3},{8,12},{9,13},{10,... | collective-permute-start | bytes 196616 | tf_op jit(solution)/shard_map/ppermute | solution.py:21
  28.6 0.9 %collective-permute-done.10 = bf16[64,512]{1,0:T(8,128)(2,1)S(1)} collective-permute-done((bf16[64,512]{1,0:T(8,128)(2,1)S(1)}, bf16[64,512]{1,0:T(8,128)(2,1)S(1)}, u32[]{:S(2)}, u32[]{:S(2)}) %collective-permute-start.10) | collective-permute-done | bytes 65568 | tf_op jit(solution)/shard_map/ppermute | solution.py:21
  29.5 2.5 %collective-permute-start.11 = (bf16[128,512]{1,0:T(8,128)(2,1)S(1)}, bf16[128,512]{1,0:T(8,128)(2,1)S(1)}, u32[]{:S(2)}, u32[]{:S(2)}) collective-permute-start(bf16[128,512]{1,0:T(8,128)(2,1)S(1)} %pad_maximum_fusion.6), channel_id=1, source_target_pairs={{0,2},{1,3},{2,0},{3,1},{4,6},{5,7},{6,4},{7,5},{8,10},{9,11},{10,... | collective-permute-start | bytes 393224 | tf_op jit(solution)/shard_map/ppermute | solution.py:21
  32.0 1.4 %collective-permute-start.5 = (bf16[128,512]{1,0:T(8,128)(2,1)S(1)}, bf16[128,512]{1,0:T(8,128)(2,1)S(1)}, u32[]{:S(2)}, u32[]{:S(2)}) collective-permute-start(bf16[128,512]{1,0:T(8,128)(2,1)S(1)} %pad_maximum_fusion.5), channel_id=1, source_target_pairs={{0,2},{1,3},{2,0},{3,1},{4,6},{5,7},{6,4},{7,5},{8,10},{9,11},{10,... | collective-permute-start | bytes 393224 | tf_op jit(solution)/shard_map/ppermute | solution.py:21
  33.8 1.6 %collective-permute-done.11 = bf16[128,512]{1,0:T(8,128)(2,1)S(1)} collective-permute-done((bf16[128,512]{1,0:T(8,128)(2,1)S(1)}, bf16[128,512]{1,0:T(8,128)(2,1)S(1)}, u32[]{:S(2)}, u32[]{:S(2)}) %collective-permute-start.11) | collective-permute-done | bytes 131104 | tf_op jit(solution)/shard_map/ppermute | solution.py:21
  35.5 1.6 %collective-permute-done.5 = bf16[128,512]{1,0:T(8,128)(2,1)S(1)} collective-permute-done((bf16[128,512]{1,0:T(8,128)(2,1)S(1)}, bf16[128,512]{1,0:T(8,128)(2,1)S(1)}, u32[]{:S(2)}, u32[]{:S(2)}) %collective-permute-start.5) | collective-permute-done | bytes 131104 | tf_op jit(solution)/shard_map/ppermute | solution.py:21
  37.3 2.0 %probe_waves.1.wave_ref = f32[2,2,512,512]{3,2,1,0:T(8,128)S(1)} custom-call(s32[1,96]{1,0:T(1,128)S(1)} %reshape_tile.9.row_freq, s32[2,1,96]{2,1,0:T(1,128)S(1)} %sub.50.row_turn, f32[1,96]{1,0:T(1,128)S(1)} %reshape_tile.10.row_weight, s32[1,96]{1,0:T(1,128)S(1)} %copy-done.9, s32[96,1]{1,0:T(8,128)S(1)} %reshape_tile.12.col_freq, ...), custom_call_target="tpu_custom_call" | custom-call | tf_op jit(solution)/shard_map/probe_waves/pallas_call | solution.py:159
  39.4 1.5 %tables.1 = (bf16[4,256,256]{2,1,0:T(8,128)(2,1)S(1)}, bf16[4,256,256]{2,1,0:T(8,128)(2,1)S(1)}, bf16[4,256,256]{2,1,0:T(8,128)(2,1)S(1)}, bf16[4,256,256]{2,1,0...) custom-call(s32[1]{0:T(128)} %bitcast.11.first_ref, ...), custom_call_target="tpu_custom_call" | custom-call | tf_op jit(solution)/shard_map/tables/pallas_call | solution.py:116
  41.0 10.6 %slice_full.1.wave_ref = f32[2,2,512,512]{3,2,1,0:T(8,128)S(1)} custom-call(s32[1]{0:T(128)} %bitcast.own_ref, bf16[512,512]{1,0:T(8,128)(2,1)S(1)} %pad_maximum_fusion.1.slab_ref, f32[2,2,512,512]{3,2,1,0:T(8,128)S(1)} %probe_waves.1.wave_ref, bf16[4,256,256]{2,1,0:T(8,128)(2,1)S(1)} %get-tuple-element.13.wh, ...), custom_call_target="tpu_custom_call" | custom-call | tf_op jit(solution)/shard_map/slice_full/pallas_call | solution.py:383
  51.7 8.5 %slice_last.1 = f32[2,2,64,256]{3,2,1,0:T(8,128)S(1)} custom-call(s32[1]{0:T(128)} %bitcast.own_ref, bf16[512,512]{1,0:T(8,128)(2,1)S(1)} %pad_maximum_fusion.slab_ref, f32[2,2,512,512]{3,2,1,0:T(8,128)S(1)} %slice_full.1.wave_ref, bf16[4,256,256]{2,1,0:T(8,128)(2,1)S(1)} %get-tuple-element.13.wh, bf16[4,256,256]{2,1,0:T(8,128)(2,1)S(1)} %get-tuple-element.14.wl, ...), custom_call_target="tpu_custom_call" | custom-call | tf_op jit(solution)/shard_map/slice_last/pallas_call | solution.py:383
  60.2 1.5 %collective-permute-start.13 = (f32[2,2,32,256]{3,2,1,0:T(8,128)S(1)}, f32[2,2,32,256]{3,2,1,0:T(8,128)S(1)}, u32[]{:S(2)}, u32[]{:S(2)}) collective-permute-start(f32[2,2,32,256]{3,2,1,0:T(8,128)S(1)} %dynamic-slice_bitcast_fusion.1), channel_id=1, source_target_pairs={{0,2},{1,3},{2,0},{3,1},{4,6},{5,7},{6,4},{7,5},{8,10},{9,11},{10,... | collective-permute-start | bytes 393224 | tf_op jit(solution)/shard_map/ppermute | solution.py:21
  61.7 4.4 %collective-permute-done.13 = f32[2,2,32,256]{3,2,1,0:T(8,128)S(1)} collective-permute-done((f32[2,2,32,256]{3,2,1,0:T(8,128)S(1)}, f32[2,2,32,256]{3,2,1,0:T(8,128)S(1)}, u32[]{:S(2)}, u32[]{:S(2)}) %collective-permute-start.13) | collective-permute-done | bytes 131104 | tf_op jit(solution)/shard_map/ppermute | solution.py:21
  66.3 1.3 %collective-permute-done.14 = f32[2,2,2,16,256]{4,3,2,1,0:T(8,128)S(1)} collective-permute-done((f32[2,2,2,16,256]{4,3,2,1,0:T(8,128)S(1)}, f32[2,2,2,16,256]{4,3,2,1,0:T(8,128)S(1)}, u32[]{:S(2)}, u32[]{:S(2)}) %collective-permute-start.14) | collective-permute-done | bytes 131104 | tf_op jit(solution)/shard_map/ppermute | solution.py:21
  67.7 0.9 %copy.31 = f32[16,2,8,256]{3,2,1,0:T(8,128)} copy(f32[16,2,8,256]{3,0,1,2:T(8,128)S(1)} %bitcast.48) | data formatting | bytes 524288 | tf_op jit(solution)/shard_map/transpose | solution.py:433
  (75 shorter events, 3.1 us)
Async XLA Ops:
  0.0 37.3 %copy-start.11 = (s32[96]{0:T(128)S(1)}, s32[96]{0:T(128)}, u32[]{:S(2)}) copy-start(s32[96]{0:T(128)} %constant.112) | copy-start | bytes 1156
  0.0 37.3 %copy-start.9 = (s32[1,96]{1,0:T(1,128)S(1)}, s32[1,96]{1,0:T(1,128)}, u32[]{:S(2)}) copy-start(s32[1,96]{1,0:T(1,128)} %constant.102.clone.row_low) | copy-start | bytes 1156
  0.0 37.3 %copy-start.4 = (s32[2,96,1]{2,1,0:T(8,128)S(1)}, s32[2,96,1]{2,1,0:T(8,128)}, u32[]{:S(2)}) copy-start(s32[2,96,1]{2,1,0:T(8,128)} %constant.103.clone.col_turn) | copy-start | bytes 2308
  0.0 37.3 %copy-start.5 = (s32[96,1]{1,0:T(8,128)S(1)}, s32[96,1]{1,0:T(8,128)}, u32[]{:S(2)}) copy-start(s32[96,1]{1,0:T(8,128)} %constant.104.clone.col_low) | copy-start | bytes 1156
  0.0 37.2 %copy-start.10 = (s32[16]{0:T(128)S(1)}, s32[16]{0:T(128)}, u32[]{:S(2)}) copy-start(s32[16]{0:T(128)} %param.18) | copy-start | bytes 196
  1.1 4.6 %collective-permute-start = (bf16[256,512]{1,0:T(8,128)(2,1)S(1)}, bf16[256,512]{1,0:T(8,128)(2,1)S(1)}, u32[]{:S(2)}, u32[]{:S(2)}) collective-permute-start(bf16[256,512]{1,0:T(8,128)(2,1)S(1)} %dynamic-slice_bitcast_fusion), channel_id=1, source_target_pairs={{0,1},{1,0},{2,3},{3,2},{4,5},{5,4},{6,7},{7,6},{8,9},{9,8},{10,11... | collective-permute-start | bytes 786440 | tf_op jit(solution)/shard_map/ppermute | solution.py:21
  6.8 32.5 %copy-start.1 = (f32[4,128,128]{2,1,0:T(8,128)S(1)}, f32[4,128,128]{2,1,0:T(8,128)}, u32[]{:S(2)}) copy-start(f32[4,128,128]{2,1,0:T(8,128)} %constant.105.clone.cos_ref) | copy-start | bytes 786436
  6.8 32.5 %copy-start.2 = (f32[4,128,128]{2,1,0:T(8,128)S(1)}, f32[4,128,128]{2,1,0:T(8,128)}, u32[]{:S(2)}) copy-start(f32[4,128,128]{2,1,0:T(8,128)} %constant.106.clone.sin_ref) | copy-start | bytes 786436
  6.9 32.5 %copy-start.3 = (f32[4,96,1]{2,1,0:T(8,128)S(1)}, f32[4,96,1]{2,1,0:T(8,128)}, u32[]{:S(2)}) copy-start(f32[4,96,1]{2,1,0:T(8,128)} %constant.107.clone.rowf) | copy-start | bytes 4612
  6.9 32.5 %copy-start.6 = (s32[4,2,1,256]{3,2,1,0:T(1,128)S(1)}, s32[4,2,1,256]{3,2,1,0:T(1,128)}, u32[]{:S(2)}) copy-start(s32[4,2,1,256]{3,2,1,0:T(1,128)} %constant.109.clone.lanew) | copy-start | bytes 24580
  6.9 6.9 %collective-permute-start.7 = (bf16[128,512]{1,0:T(8,128)(2,1)S(1)}, bf16[128,512]{1,0:T(8,128)(2,1)S(1)}, u32[]{:S(2)}, u32[]{:S(2)}) collective-permute-start(bf16[128,512]{1,0:T(8,128)(2,1)S(1)} %constant_dynamic-slice_fusion.2), channel_id=1, source_target_pairs={{0,2},{1,3},{2,0},{3,1},{4,6},{5,7},{6,4},{7,5},{8,10},{9,11},{10,... | collective-permute-start | bytes 393224 | tf_op jit(solution)/shard_map/ppermute | solution.py:21
  9.5 6.9 %collective-permute-start.1 = (bf16[128,512]{1,0:T(8,128)(2,1)S(1)}, bf16[128,512]{1,0:T(8,128)(2,1)S(1)}, u32[]{:S(2)}, u32[]{:S(2)}) collective-permute-start(bf16[128,512]{1,0:T(8,128)(2,1)S(1)} %constant_dynamic-slice_fusion.4), channel_id=1, source_target_pairs={{0,2},{1,3},{2,0},{3,1},{4,6},{5,7},{6,4},{7,5},{8,10},{9,11},{10,... | collective-permute-start | bytes 393224 | tf_op jit(solution)/shard_map/ppermute | solution.py:21
  13.9 4.5 %collective-permute-start.8 = (bf16[64,512]{1,0:T(8,128)(2,1)S(1)}, bf16[64,512]{1,0:T(8,128)(2,1)S(1)}, u32[]{:S(2)}, u32[]{:S(2)}) collective-permute-start(bf16[64,512]{1,0:T(8,128)(2,1)S(1)} %constant_dynamic-slice_fusion.1), channel_id=1, source_target_pairs={{0,4},{1,5},{2,6},{3,7},{4,0},{5,1},{6,2},{7,3},{8,12},{9,13},{10,... | collective-permute-start | bytes 196616 | tf_op jit(solution)/shard_map/ppermute | solution.py:21
  16.5 4.9 %collective-permute-start.2 = (bf16[64,512]{1,0:T(8,128)(2,1)S(1)}, bf16[64,512]{1,0:T(8,128)(2,1)S(1)}, u32[]{:S(2)}, u32[]{:S(2)}) collective-permute-start(bf16[64,512]{1,0:T(8,128)(2,1)S(1)} %constant_dynamic-slice_fusion.3), channel_id=1, source_target_pairs={{0,4},{1,5},{2,6},{3,7},{4,0},{5,1},{6,2},{7,3},{8,12},{9,13},{10,... | collective-permute-start | bytes 196616 | tf_op jit(solution)/shard_map/ppermute | solution.py:21
  18.4 5.4 %collective-permute-start.9 = (bf16[64,512]{1,0:T(8,128)(2,1)S(1)}, bf16[64,512]{1,0:T(8,128)(2,1)S(1)}, u32[]{:S(2)}, u32[]{:S(2)}) collective-permute-start(bf16[64,512]{1,0:T(8,128)(2,1)S(1)} %dynamic-slice_add_fusion.2), channel_id=1, source_target_pairs={{0,8},{1,9},{2,10},{3,11},{4,12},{5,13},{6,14},{7,15},{8,0},{9,1},... | collective-permute-start | bytes 196616 | tf_op jit(solution)/shard_map/ppermute | solution.py:21
  21.4 6.0 %collective-permute-start.3 = (bf16[64,512]{1,0:T(8,128)(2,1)S(1)}, bf16[64,512]{1,0:T(8,128)(2,1)S(1)}, u32[]{:S(2)}, u32[]{:S(2)}) collective-permute-start(bf16[64,512]{1,0:T(8,128)(2,1)S(1)} %dynamic-slice_add_fusion.3), channel_id=1, source_target_pairs={{0,8},{1,9},{2,10},{3,11},{4,12},{5,13},{6,14},{7,15},{8,0},{9,1},... | collective-permute-start | bytes 196616 | tf_op jit(solution)/shard_map/ppermute | solution.py:21
  23.8 5.7 %collective-permute-start.10 = (bf16[64,512]{1,0:T(8,128)(2,1)S(1)}, bf16[64,512]{1,0:T(8,128)(2,1)S(1)}, u32[]{:S(2)}, u32[]{:S(2)}) collective-permute-start(bf16[64,512]{1,0:T(8,128)(2,1)S(1)} %add.96), channel_id=1, source_target_pairs={{0,4},{1,5},{2,6},{3,7},{4,0},{5,1},{6,2},{7,3},{8,12},{9,13},{10,... | collective-permute-start | bytes 196616 | tf_op jit(solution)/shard_map/ppermute | solution.py:21
  27.5 4.5 %collective-permute-start.4 = (bf16[64,512]{1,0:T(8,128)(2,1)S(1)}, bf16[64,512]{1,0:T(8,128)(2,1)S(1)}, u32[]{:S(2)}, u32[]{:S(2)}) collective-permute-start(bf16[64,512]{1,0:T(8,128)(2,1)S(1)} %add.93), channel_id=1, source_target_pairs={{0,4},{1,5},{2,6},{3,7},{4,0},{5,1},{6,2},{7,3},{8,12},{9,13},{10,... | collective-permute-start | bytes 196616 | tf_op jit(solution)/shard_map/ppermute | solution.py:21
  29.5 5.8 %collective-permute-start.11 = (bf16[128,512]{1,0:T(8,128)(2,1)S(1)}, bf16[128,512]{1,0:T(8,128)(2,1)S(1)}, u32[]{:S(2)}, u32[]{:S(2)}) collective-permute-start(bf16[128,512]{1,0:T(8,128)(2,1)S(1)} %pad_maximum_fusion.6), channel_id=1, source_target_pairs={{0,2},{1,3},{2,0},{3,1},{4,6},{5,7},{6,4},{7,5},{8,10},{9,11},{10,... | collective-permute-start | bytes 393224 | tf_op jit(solution)/shard_map/ppermute | solution.py:21
  32.0 5.0 %collective-permute-start.5 = (bf16[128,512]{1,0:T(8,128)(2,1)S(1)}, bf16[128,512]{1,0:T(8,128)(2,1)S(1)}, u32[]{:S(2)}, u32[]{:S(2)}) collective-permute-start(bf16[128,512]{1,0:T(8,128)(2,1)S(1)} %pad_maximum_fusion.5), channel_id=1, source_target_pairs={{0,2},{1,3},{2,0},{3,1},{4,6},{5,7},{6,4},{7,5},{8,10},{9,11},{10,... | collective-permute-start | bytes 393224 | tf_op jit(solution)/shard_map/ppermute | solution.py:21
  35.4 5.5 %collective-permute-start.12 = (bf16[256,512]{1,0:T(8,128)(2,1)S(1)}, bf16[256,512]{1,0:T(8,128)(2,1)S(1)}, u32[]{:S(2)}, u32[]{:S(2)}) collective-permute-start(bf16[256,512]{1,0:T(8,128)(2,1)S(1)} %pad_maximum_fusion.3), channel_id=1, source_target_pairs={{0,1},{1,0},{2,3},{3,2},{4,5},{5,4},{6,7},{7,6},{8,9},{9,8},{10,11... | collective-permute-start | bytes 786440 | tf_op jit(solution)/shard_map/ppermute | solution.py:21
  37.1 14.5 %collective-permute-start.6 = (bf16[256,512]{1,0:T(8,128)(2,1)S(1)}, bf16[256,512]{1,0:T(8,128)(2,1)S(1)}, u32[]{:S(2)}, u32[]{:S(2)}) collective-permute-start(bf16[256,512]{1,0:T(8,128)(2,1)S(1)} %pad_maximum_fusion.2), channel_id=1, source_target_pairs={{0,1},{1,0},{2,3},{3,2},{4,5},{5,4},{6,7},{7,6},{8,9},{9,8},{10,11... | collective-permute-start | bytes 786440 | tf_op jit(solution)/shard_map/ppermute | solution.py:21
  60.2 5.9 %collective-permute-start.13 = (f32[2,2,32,256]{3,2,1,0:T(8,128)S(1)}, f32[2,2,32,256]{3,2,1,0:T(8,128)S(1)}, u32[]{:S(2)}, u32[]{:S(2)}) collective-permute-start(f32[2,2,32,256]{3,2,1,0:T(8,128)S(1)} %dynamic-slice_bitcast_fusion.1), channel_id=1, source_target_pairs={{0,2},{1,3},{2,0},{3,1},{4,6},{5,7},{6,4},{7,5},{8,10},{9,11},{10,... | collective-permute-start | bytes 393224 | tf_op jit(solution)/shard_map/ppermute | solution.py:21
  66.2 1.4 %collective-permute-start.14 = (f32[2,2,2,16,256]{4,3,2,1,0:T(8,128)S(1)}, f32[2,2,2,16,256]{4,3,2,1,0:T(8,128)S(1)}, u32[]{:S(2)}, u32[]{:S(2)}) collective-permute-start(f32[2,2,2,16,256]{4,3,2,1,0:T(8,128)S(1)} %fusion.1), channel_id=1, source_target_pairs={{0,1},{1,0},{2,3},{3,2},{4,5},{5,4},{6,7},{7,6},{8,9},{9,8},{10,11... | collective-permute-start | bytes 393224 | tf_op jit(solution)/shard_map/ppermute | solution.py:21
  (3 other events, 70.7 us)

commit v2 on v1

v2 whole, which is shorter than its diff:
```python
import functools
import math

import jax
import jax.numpy as jnp
import numpy as np
from jax import lax
from jax.experimental import pallas as pl
from jax.experimental.pallas import tpu as pltpu
from jax.sharding import PartitionSpec as P


FRESNEL = 4.7e-05
F32 = jnp.float32
BF16 = jnp.bfloat16
QUAD = 4
ROW_STEPS = 2


def flip(array, bit, groups):
    return lax.ppermute(array, "wide", [(i, i ^ bit) for i in range(groups)])


def half(array, which):
    rows = array.shape[0] // 2
    return lax.dynamic_slice_in_dim(array, which * rows, rows, 0)


def spread_slabs(own_slab, slice_owner, groups, device):
    count = slice_owner.shape[0]
    bits = [1 << b for b in range(groups.bit_length() - 1)]
    side = device & 1
    own = side
    kept = half(own_slab, side)
    received = flip(half(own_slab, 1 - side), 1, groups)
    mine = (slice_owner == device)[:, None, None]
    theirs = (slice_owner == (device ^ 1))[:, None, None]
    picked = jnp.where(mine, kept, jnp.where(theirs, received, jnp.zeros_like(kept)))
    parts = [picked[s] for s in range(count)]
    for bit in bits[1:-1]:
        side = (device // bit) & 1
        own = own * 2 + side
        parts = [half(p, side) + flip(half(p, 1 - side), bit, groups) for p in parts]
    parts = [p + flip(p, bits[-1], groups) for p in parts]
    for bit in reversed(bits[2:-1]):
        parts = [jnp.concatenate([p, flip(p, bit, groups)], axis=0) for p in parts]
    pieces = []
    for part in parts:
        other = flip(part, 2, groups)
        pieces.append((part, other, flip(part, 1, groups), flip(other, 1, groups)))
    return pieces, own.astype(jnp.int32).reshape(1)


def class_frequencies(grid):
    top = grid // 3
    classes = [[u for u in range(-top, top + 1) if u % 4 == c] for c in range(4)]
    longest = max(len(c) for c in classes)
    return [(c[0], len(c)) for c in classes], -(-longest // 16) * 16


def cos_turns(turns, grid):
    turns = (turns + grid // 2) & (grid - 1)
    h = (turns - grid // 2).astype(F32) * (math.pi / grid)
    t = h * h
    p = -1.0 / math.factorial(11)
    for n in (9, 7, 5, 3, 1):
        p = p * t + (1.0 if n % 4 == 1 else -1.0) / math.factorial(n)
    s = h * p
    return 1.0 - 2.0 * (s * s)


def table_kernel(first_ref, wh, wl, vh, vl, pr, pi, dh, dl):
    q = wh.shape[1] // 2
    n = 4 * q
    kp = pr.shape[1]
    take = dh.shape[1] // 2
    classes, _ = class_frequencies(n)

    def iota(shape, axis):
        return lax.broadcasted_iota(jnp.int32, shape, axis)

    for c, (first, count) in enumerate(classes):
        lane = iota((q, q), 1)
        turn = iota((q, q), 0) * (first + 4 * lane)
        cos = jnp.where(lane < count, cos_turns(turn, n), 0.0)
        sin = jnp.where(lane < count, cos_turns(turn - n // 4, n), 0.0)
        for a, b, part in ((0, 0, cos), (0, 1, -sin), (1, 0, sin), (1, 1, cos)):
            wh[c, a * q : (a + 1) * q, b * q : (b + 1) * q], wl[c, a * q : (a + 1) * q, b * q : (b + 1) * q] = split(part)
        cos, sin = cos.T, sin.T
        for a, b, part in ((0, 0, cos), (0, 1, sin), (1, 0, -sin), (1, 1, cos)):
            vh[c, a * q : (a + 1) * q, b * q : (b + 1) * q], vl[c, a * q : (a + 1) * q, b * q : (b + 1) * q] = split(part)
        row, lane = iota((kp, q), 0), iota((kp, q), 1)
        for l, (first_l, count_l) in enumerate(classes):
            u, v = first + 4 * row, first_l + 4 * lane
            squared = u * u + v * v
            kept = (9 * squared <= n * n) & (row < count) & (lane < count_l)
            re, im = cos_sin(jnp.where(kept, FRESNEL * squared.astype(F32), 0.0))
            pr[c, :, l * q : (l + 1) * q] = jnp.where(kept, re * (1.0 / (n * n)), 0.0)
            pi[c, :, l * q : (l + 1) * q] = jnp.where(kept, im * (-1.0 / (n * n)), 0.0)
        lane = iota((take, q), 1)
        turn = (first_ref[0] + (iota((take, q), 0) ^ first_ref[1])) * (first + 4 * lane)
        cos = jnp.where(lane < count, cos_turns(turn, n), 0.0)
        sin = jnp.where(lane < count, cos_turns(turn - n // 4, n), 0.0)
        for a, b, part in ((0, 0, cos), (0, 1, -sin), (1, 0, sin), (1, 1, cos)):
            at = slice(a * take, (a + 1) * take)
            dh[c, at, b * q : (b + 1) * q], dl[c, at, b * q : (b + 1) * q] = split(part)


def make_tables(grid, first_row, order, rows):
    _, kp = class_frequencies(grid)
    q = grid // 4
    full = jax.ShapeDtypeStruct((4, 2 * q, 2 * q), BF16)
    prop = jax.ShapeDtypeStruct((4, kp, grid), F32)
    last = jax.ShapeDtypeStruct((4, 2 * rows, 2 * q), BF16)
    out = pl.pallas_call(
        table_kernel,
        name="tables",
        in_specs=[pl.BlockSpec(memory_space=pltpu.SMEM)],
        out_specs=[pl.BlockSpec(memory_space=pltpu.VMEM)] * 8,
        out_shape=[full, full, full, full, prop, prop, last, last],
        compiler_params=pltpu.CompilerParams(vmem_limit_bytes=12 << 20),
    )(jnp.stack([first_row, order]).astype(jnp.int32))
    return out[0:2], out[2:4], out[4:6], out[6:8]


def wave_kernel(place_ref, position_ref, beam_ref, left_ref, right_ref):
    probes, n, _ = left_ref.shape
    quarter = n // 4
    beams = beam_ref.shape[0]
    shift = beams.bit_length() - 1
    k = 6 * beams
    beam, position = beam_ref[...], position_ref[...]
    freq_x, freq_y, open_ = beam[:, 0:1], beam[:, 1:2], beam[:, 2:3]

    def part_group(index):
        return (index >> shift) & 1, index >> (shift + 1)

    lane = lax.broadcasted_iota(jnp.int32, (beams, k), 1)
    own = (lane & (beams - 1)) == lax.broadcasted_iota(jnp.int32, (beams, k), 0)

    def along_lanes(column):
        return jnp.sum(jnp.where(own, column.astype(F32), 0.0), axis=0, keepdims=True)

    def pick(value, low):
        high = value.astype(BF16).astype(F32)
        return jnp.where(low, value - high, high).astype(BF16)

    part, group = part_group(lax.broadcasted_iota(jnp.int32, (1, k), 1))
    row_freq = along_lanes(freq_x).astype(jnp.int32)
    weight = along_lanes(open_) * (1.0 / math.sqrt(beams))
    x = lax.broadcasted_iota(jnp.int32, (n, k), 0) * row_freq
    for p in range(probes):
        wanted = lax.broadcasted_iota(jnp.int32, position.shape, 0) == place_ref[0] * probes + p
        at = jnp.sum(jnp.where(wanted, position.astype(F32), 0.0), axis=0, keepdims=True).astype(jnp.int32)
        mixing = (freq_x * at[:, 0:1] + freq_y * at[:, 1:2]) & (n - 1)
        turn = -along_lanes(mixing).astype(jnp.int32) - quarter * part
        left_ref[p] = pick(cos_turns(x + turn, n) * weight, group == 1)
    part, group = part_group(lax.broadcasted_iota(jnp.int32, (k, n), 0))
    turn = lax.broadcasted_iota(jnp.int32, (k, n), 1) * jnp.concatenate([freq_y] * 6, axis=0)
    for c, extra in enumerate((quarter * part, quarter * part - quarter)):
        right_ref[c] = pick(cos_turns(turn + extra, n), group == 2)


def probe_waves(grid, beam_index, aperture, position, place):
    probes = position.shape[0] // QUAD
    k = 6 * beam_index.shape[0]
    beam = jnp.concatenate([beam_index, aperture[:, None]], axis=1)
    vmem = pl.BlockSpec(memory_space=pltpu.VMEM)
    return pl.pallas_call(
        wave_kernel,
        name="probe_waves",
        in_specs=[pl.BlockSpec(memory_space=pltpu.SMEM), vmem, vmem],
        out_specs=[vmem, vmem],
        out_shape=[jax.ShapeDtypeStruct((probes, grid, k), BF16), jax.ShapeDtypeStruct((2, k, grid), BF16)],
        compiler_params=pltpu.CompilerParams(vmem_limit_bytes=12 << 20),
    )(place.astype(jnp.int32).reshape(1), position, beam)


def split(x):
    high = x.astype(BF16)
    return high, (x - high.astype(F32)).astype(BF16)


def dot(a, b):
    return jnp.dot(a, b, preferred_element_type=F32)


def dot3(ah, al, bh, bl):
    return dot(ah, bh) + dot(al, bh) + dot(ah, bl)


def butterfly(parts, sign):
    (r0, i0), (r1, i1), (r2, i2), (r3, i3) = parts
    sr, si, dr, di = r0 + r2, i0 + i2, r0 - r2, i0 - i2
    tr, ti, er, ei = r1 + r3, i1 + i3, r1 - r3, i1 - i3
    up = (dr - sign * ei, di + sign * er)
    down = (dr + sign * ei, di - sign * er)
    return [(sr + tr, si + ti), up, (sr - tr, si - ti), down]


def chebyshev(function, top, terms):
    fit = np.polynomial.chebyshev.Chebyshev.interpolate(function, terms - 1, domain=[0.0, top])
    return [float(v) for v in fit.convert(kind=np.polynomial.Polynomial).coef]


COS = chebyshev(lambda t: np.cos(np.sqrt(t)), 2.56, 5)
SIN = chebyshev(lambda t: np.sinc(np.sqrt(t) / np.pi), 2.56, 5)


def horner(coefficients, t):
    value = coefficients[-1]
    for coefficient in coefficients[-2::-1]:
        value = value * t + coefficient
    return value


def cos_sin(v):
    t = v * v
    return horner(COS, t), v * horner(SIN, t)


def transmit_kernel(own_ref, *refs, blocks):
    pieces, (tr_ref, ti_ref) = refs[:-2], refs[-2:]
    block_rows = tr_ref.shape[0] // blocks
    each = blocks // len(pieces)
    for b in range(blocks):
        place = pl.multiple_of((own_ref[0] ^ b) * block_rows, block_rows)
        first = b % each * block_rows
        c, s = cos_sin(pieces[b // each][first : first + block_rows, :].astype(F32))
        tr_ref[pl.ds(place, block_rows), :] = c
        ti_ref[pl.ds(place, block_rows), :] = s


def transmit(own, pieces, blocks):
    vmem = pl.BlockSpec(memory_space=pltpu.VMEM)
    columns = pieces[0].shape[1]
    shape = jax.ShapeDtypeStruct((sum(piece.shape[0] for piece in pieces), columns), F32)
    return pl.pallas_call(
        functools.partial(transmit_kernel, blocks=blocks),
        name="transmit",
        in_specs=[pl.BlockSpec(memory_space=pltpu.SMEM)] + [vmem] * len(pieces),
        out_specs=[vmem, vmem],
        out_shape=[shape, shape],
        compiler_params=pltpu.CompilerParams(vmem_limit_bytes=8 << 20),
    )(own, *pieces)


def clear_padding(uh, ul, kp):
    q = uh.shape[1] // 2
    for spectrum in (uh, ul):
        for c in range(4):
            for first in (0, q):
                spectrum[c, first + kp : first + q] = jnp.zeros((q - kp, spectrum.shape[2]), BF16)


def forward(prepare, wave_ref, tr_ref, ti_ref, wh, wl, vh, vl, pr, pi, scratch, after):
    yh, yl, sr, si, zh, zl, uh, ul = scratch
    n = tr_ref.shape[0]
    q = n // 4
    kp = pr.shape[1]
    rows = 32

    def fold_lanes(first):
        at = pl.ds(first, rows)
        parts = []
        for j in range(4):
            lanes = pl.ds(j * q, q)
            wr, wi = wave_ref[0, at, lanes], wave_ref[1, at, lanes]
            cr, ci = tr_ref[at, lanes], ti_ref[at, lanes]
            parts.append((wr * cr - wi * ci, wr * ci + wi * cr))
        for c, (r, i) in enumerate(butterfly(parts, -1.0)):
            yh[c, at, :q], yl[c, at, :q] = split(r)
            yh[c, at, q:], yl[c, at, q:] = split(i)

    def fold_rows(l):
        lanes = pl.ds(l * q, q)
        for first in range(0, q, rows):
            parts = [(sr[pl.ds(j * q + first, rows), lanes], si[pl.ds(j * q + first, rows), lanes]) for j in range(4)]
            for c, (r, i) in enumerate(butterfly(parts, -1.0)):
                zh[c, pl.ds(first, rows), lanes], zl[c, pl.ds(first, rows), lanes] = split(r)
                zh[c, pl.ds(q + first, rows), lanes], zl[c, pl.ds(q + first, rows), lanes] = split(i)

    step = n // ROW_STEPS
    for b in range(ROW_STEPS):
        at = pl.ds(b * step, step)
        prepare(at)
        for first in range(b * step, (b + 1) * step, rows):
            fold_lanes(first)
        for c in range(4):
            out = dot3(yh[c, at], yl[c, at], wh[c], wl[c])
            sr[at, c * q : (c + 1) * q] = out[:, :q]
            si[at, c * q : (c + 1) * q] = out[:, q:]
            if b == ROW_STEPS - 1:
                fold_rows(c)
    for h in range(2):
        lanes = pl.ds(h * 2 * q, 2 * q)
        for c in range(4):
            zhc, zlc = zh[c, :, lanes], zl[c, :, lanes]
            r = dot3(vh[c, :kp], vl[c, :kp], zhc, zlc)
            i = dot3(vh[c, q : q + kp], vl[c, q : q + kp], zhc, zlc)
            re, im = pr[c, :, lanes], pi[c, :, lanes]
            uh[c, :kp, lanes], ul[c, :kp, lanes] = split(r * re - i * im)
            uh[c, q : q + kp, lanes], ul[c, q : q + kp, lanes] = split(r * im + i * re)
        after(h)


def first_kernel(probe, tr, ti, left_ref, right_ref, wh, wl, vh, vl, pr, pi, out_ref, wave_ref, *scratch):
    def prepare(at):
        for c in range(2):
            wave_ref[c, at] = dot(left_ref[probe, at], right_ref[c])

    slice_kernel(prepare, tr, ti, wave_ref, wh, wl, vh, vl, pr, pi, out_ref, *scratch)


def middle_kernel(tr, ti, wave_ref, wh, wl, vh, vl, pr, pi, out_ref, *scratch):
    slice_kernel(lambda at: None, tr, ti, wave_ref, wh, wl, vh, vl, pr, pi, out_ref, *scratch)


def slice_kernel(prepare, tr, ti, wave_ref, wh, wl, vh, vl, pr, pi, out_ref, yh, yl, sr, si, zh, zl, uh, ul, g, hr):
    n = tr.shape[0]
    q = n // 4
    rows = 32

    clear_padding(uh, ul, pr.shape[1])

    def unfold_rows(l):
        lanes = pl.ds(l * q, q)
        for first in range(0, q, rows):
            parts = [(g[c, pl.ds(first, rows), lanes], g[c, pl.ds(q + first, rows), lanes]) for c in range(4)]
            for j, (r, i) in enumerate(butterfly(parts, 1.0)):
                at = pl.ds(j * q + first, rows)
                yh[l, at, :q], yl[l, at, :q] = split(r)
                yh[l, at, q:], yl[l, at, q:] = split(i)

    def after(h):
        lanes = pl.ds(h * 2 * q, 2 * q)
        for c in range(4):
            g[c, :, lanes] = dot3(wh[c], wl[c], uh[c, :, lanes], ul[c, :, lanes])
        for l in (2 * h, 2 * h + 1):
            unfold_rows(l)

    forward(prepare, wave_ref, tr, ti, wh, wl, vh, vl, pr, pi, (yh, yl, sr, si, zh, zl, uh, ul), after)
    step = n // ROW_STEPS
    for b in range(ROW_STEPS):
        at = pl.ds(b * step, step)
        for c in range(4):
            hr[c, at] = dot3(yh[c, at], yl[c, at], vh[c], vl[c])
        for first in range(b * step, (b + 1) * step, rows):
            at = pl.ds(first, rows)
            parts = [(hr[c, at, :q], hr[c, at, q:]) for c in range(4)]
            for j, (r, i) in enumerate(butterfly(parts, 1.0)):
                out_ref[0, at, pl.ds(j * q, q)] = r
                out_ref[1, at, pl.ds(j * q, q)] = i


def last_kernel(tr, ti, wave_ref, wh, wl, vh, vl, pr, pi, dh, dl, keep_ref, away_ref, yh, yl, sr, si, zh, zl, uh, ul):
    n = tr.shape[0]
    q = n // 4
    take = dh.shape[1] // 2

    clear_padding(uh, ul, pr.shape[1])

    half_out = []

    def after(h):
        lanes = pl.ds(h * 2 * q, 2 * q)
        out = dot3(dh[0], dl[0], uh[0, :, lanes], ul[0, :, lanes])
        for c in range(1, 4):
            out = out + dot3(dh[c], dl[c], uh[c, :, lanes], ul[c, :, lanes])
        half_out.append(out)

    forward(lambda at: None, wave_ref, tr, ti, wh, wl, vh, vl, pr, pi, (yh, yl, sr, si, zh, zl, uh, ul), after)
    parts = []
    for c in range(4):
        lanes = slice(c % 2 * q, c % 2 * q + q)
        out = half_out[c // 2]
        high, low = split(jnp.concatenate([out[:take, lanes], out[take:, lanes]], axis=1))
        back = dot3(high, low, vh[c], vl[c])
        parts.append((back[:, :q], back[:, q:]))
    for j, (r, i) in enumerate(butterfly(parts, 1.0)[1:3]):
        for c, part in enumerate((r, i)):
            keep_ref[c, :, j * q : (j + 1) * q] = part[: take // 2]
            away_ref[c, :, j * q : (j + 1) * q] = part[take // 2 :]


def forward_scratch(n):
    q = n // 4
    return [
        pltpu.VMEM((4, n, 2 * q), BF16),
        pltpu.VMEM((4, n, 2 * q), BF16),
        pltpu.VMEM((n, n), F32),
        pltpu.VMEM((n, n), F32),
        pltpu.VMEM((4, 2 * q, n), BF16),
        pltpu.VMEM((4, 2 * q, n), BF16),
        pltpu.VMEM((4, 2 * q, n), BF16),
        pltpu.VMEM((4, 2 * q, n), BF16),
    ]


def run_kernel(kernel, inputs, out_shapes, first, extra):
    n = inputs[0].shape[-1]
    vmem = pl.BlockSpec(memory_space=pltpu.VMEM)
    return pl.pallas_call(
        kernel,
        in_specs=[vmem] * len(inputs),
        out_specs=[vmem] * len(out_shapes),
        out_shape=[jax.ShapeDtypeStruct(shape, F32) for shape in out_shapes],
        scratch_shapes=first + forward_scratch(n) + extra,
        compiler_params=pltpu.CompilerParams(vmem_limit_bytes=32 << 20),
    )(*inputs)


def local(potential_pool, slice_owner, beam_index, aperture, probe_position):
    grid = potential_pool.shape[-1]
    crop = grid // 2
    margin = grid // 4
    q = grid // 4
    groups = lax.axis_size("wide")
    device = lax.axis_index("wide")
    probes = probe_position.shape[0]
    per_device = probes // QUAD
    quad_rows = crop // (groups // QUAD)
    own_rows = crop // groups
    place = device % QUAD
    quad = device // QUAD

    slabs, own = spread_slabs(potential_pool[0], slice_owner, groups, device)
    blocks = groups // 2

    factors = probe_waves(grid, beam_index, aperture, probe_position, place)
    forward_table, inverse_table, prop, last_rows = make_tables(grid, margin + quad * quad_rows, place * own_rows, quad_rows)
    tables = (*forward_table, *inverse_table, *prop)
    extra = [pltpu.VMEM((4, 2 * q, grid), F32), pltpu.VMEM((4, grid, 2 * q), F32)]
    wave = [pltpu.VMEM((2, grid, grid), F32)]
    turned = transmit(own, slabs[0], blocks)
    waves = [
        run_kernel(functools.partial(first_kernel, p), (*turned, *factors, *tables), [(2, grid, grid)], wave, extra)[0]
        for p in range(per_device)
    ]
    for slab in slabs[1:-1]:
        turned = transmit(own, slab, blocks)
        waves = [run_kernel(middle_kernel, (*turned, w, *tables), [w.shape], [], extra)[0] for w in waves]
    turned = transmit(own, slabs[-1], blocks)

    kept, other = [], []
    for p in range(per_device):
        inputs = (*turned, waves[p], *tables, *last_rows)
        shape = (2, quad_rows // 2, crop)
        keep, away = run_kernel(last_kernel, inputs, [shape, shape], [], [])
        kept.append(keep)
        other.append(flip(away, 2, groups))
    pair = jnp.stack(kept + other)
    other = flip(pair[:, :, own_rows:], 1, groups)
    side_y, side_core = (place // 2) & 1, place & 1
    four = jnp.stack([pair[:, :, :own_rows], other]).reshape(2, 2, per_device, 2, own_rows, crop)
    four = jnp.where(side_core == 0, four, four[::-1])
    four = jnp.where(side_y == 0, four, four[:, ::-1])
    return jnp.transpose(four, (4, 3, 1, 0, 2, 5)).reshape(own_rows, 2, probes, crop)


def solution(mesh):
    placed = (P(("parts", "wide"), None, None), P("parts"), P(), P(), P("parts", None))

    return jax.shard_map(
        local,
        mesh=mesh,
        in_specs=placed,
        out_specs=P(("parts", "wide"), None, None, None),
        check_vma=False,
    )
```

time: 68.9 us -> 64.7 us (0.939)
  waiting for transfers between devices: 14.5 us -> 17.6 us
  between operations: 3.01 us -> 0.32 us
  local copies, waits for them, and re-layouts: 4.63 us -> 2.45 us
  starting transfers between devices: 22.2 us -> 20.6 us
    ppermute x15 -> x18, waiting for transfers between devices: 14.5 us -> 17.6 us  [flip(): return lax.ppermute(array, 'wide', [(i, i ^ bit) for i in range(groups)])]
    ppermute x15 -> x18, starting transfers between devices: 22.2 us -> 20.6 us  [flip(): return lax.ppermute(array, 'wide', [(i, i ^ bit) for i in range(groups)])]
    slice x1 -> x2, local copies, waits for them, and re-layouts: 1.38 us -> 0.06 us  [the longest x1 0.04 us: spread_slabs(): parts = [picked[s] for s in range(count)]]
    select_n x2, other arithmetic: 1.1 us -> 0.16 us  [the longest x1 0.13 us: spread_slabs(): jnp.where(mine, kept, jnp.where(theirs, received, jnp.zeros_like(kept)))]
    reshape x0 -> x1, local copies, waits for them, and re-layouts: none -> 0.88 us  [local(): jnp.transpose(four, (4, 3, 1, 0, 2, 5)).reshape(own_rows, 2, probes, crop)]
    pallas_call x3 -> x7, Pallas kernels: 21.2 us -> 20.4 us  [the longest x4 17.8 us: run_kernel(): pl.pallas_call(kernel, in_specs=[vmem] * len(inputs), out_specs=[vmem] *...]
    mul x2 -> x0, local copies, waits for them, and re-layouts: 0.76 us -> none  [the longest x1 0.76 us: probe_waves(): beam_index[:, 1][None, :] * position[:, 1][:, None]]
  transfers between devices with their start and end apart: 15 -> 18, of which waited for: 7 -> 11; matrix products, arithmetic and copies ran while one was open for 4% -> 2% of each run, Pallas kernels for 21% -> 28%
where the time goes in v2:
time: 64.7 us; the launch traced here: 64.6 us
  Pallas kernels  22.5 us (35%)
  starting transfers between devices  20.6 us (32%)
  waiting for transfers between devices  17.6 us (27%)
  local copies, waits for them, and re-layouts  2.45 us (4%)
  other arithmetic  1.13 us (2%)
    ppermute x18, starting transfers between devices, flip(): return lax.ppermute(array, 'wide', [(i, i ^ bit) for i in range(groups)])  20.6 us
    pallas_call x4, Pallas kernels, run_kernel(): pl.pallas_call(kernel, in_specs=[vmem] * len(inputs), out_specs=[vmem] *...  17.8 us
    ppermute x18, waiting for transfers between devices, flip(): return lax.ppermute(array, 'wide', [(i, i ^ bit) for i in range(groups)])  17.6 us
    pallas_call x1, Pallas kernels, make_tables(): pl.pallas_call(table_kernel, name='tables', in_specs=[pl.BlockSpec(memory...  2.13 us
    pallas_call x2, Pallas kernels, transmit(): pl.pallas_call(functools.partial(transmit_kernel, blocks=blocks), name='t...  1.34 us
  transfers between devices with their start and end apart: 18, of which 11 were waited for; matrix products, arithmetic and copies ran while one was open for 2% of the time, Pallas kernels for 28%

profile of v2, /device:TPU:0, one launch (start us, length us, event | category | flops | bytes accessed | tf_op | source)
XLA Modules:
  0.0 64.6 jit_solution(7374157631236428026)
XLA Ops:
  0.0 1.1 %dynamic-slice_bitcast_fusion.1 = (bf16[256,512]{1,0:T(8,128)(2,1)S(1)}, bf16[256,512]{1,0:T(8,128)(2,1)S(1)}) fusion(bf16[1,512,512]{2,1,0:T(8,128)(2,1)} %param.5, s32[]{:T(128)S(6)} %select_n.68, s32[]{:T(128)S(6)} %select_n.69), kind=kLoop, calls=%fused_computation.7 | loop fusion | bytes 1048584 | tf_op jit(solution)/shard_map/dynamic_slice | solution.py:26
  3.0 2.9 %collective-permute-start.1 = (bf16[128,512]{1,0:T(8,128)(2,1)S(1)}, bf16[128,512]{1,0:T(8,128)(2,1)S(1)}, u32[]{:S(2)}, u32[]{:S(2)}) collective-permute-start(bf16[128,512]{1,0:T(8,128)(2,1)S(1)} %dynamic-slice_bitcast_fusion.3), channel_id=1, source_target_pairs={{0,2},{1,3},{2,0},{3,1},{4,6},{5,7},{6,4},{7,5},{8,10},{9,11},{10,... | collective-permute-start | bytes 393224 | tf_op jit(solution)/shard_map/ppermute | solution.py:21
  6.1 4.2 %collective-permute-done.1 = bf16[128,512]{1,0:T(8,128)(2,1)S(1)} collective-permute-done((bf16[128,512]{1,0:T(8,128)(2,1)S(1)}, bf16[128,512]{1,0:T(8,128)(2,1)S(1)}, u32[]{:S(2)}, u32[]{:S(2)}) %collective-permute-start.1) | collective-permute-done | bytes 131104 | tf_op jit(solution)/shard_map/ppermute | solution.py:21
  10.4 2.1 %collective-permute-start.2 = (bf16[64,512]{1,0:T(8,128)(2,1)S(1)}, bf16[64,512]{1,0:T(8,128)(2,1)S(1)}, u32[]{:S(2)}, u32[]{:S(2)}) collective-permute-start(bf16[64,512]{1,0:T(8,128)(2,1)S(1)} %constant_dynamic-slice_fusion.1), channel_id=1, source_target_pairs={{0,4},{1,5},{2,6},{3,7},{4,0},{5,1},{6,2},{7,3},{8,12},{9,13},{10,... | collective-permute-start | bytes 196616 | tf_op jit(solution)/shard_map/ppermute | solution.py:21
  12.6 1.9 %collective-permute-start.9 = (bf16[64,512]{1,0:T(8,128)(2,1)S(1)}, bf16[64,512]{1,0:T(8,128)(2,1)S(1)}, u32[]{:S(2)}, u32[]{:S(2)}) collective-permute-start(bf16[64,512]{1,0:T(8,128)(2,1)S(1)} %constant_dynamic-slice_fusion), channel_id=1, source_target_pairs={{0,4},{1,5},{2,6},{3,7},{4,0},{5,1},{6,2},{7,3},{8,12},{9,13},{10,... | collective-permute-start | bytes 196616 | tf_op jit(solution)/shard_map/ppermute | solution.py:21
  14.8 3.5 %collective-permute-start.3 = (bf16[64,512]{1,0:T(8,128)(2,1)S(1)}, bf16[64,512]{1,0:T(8,128)(2,1)S(1)}, u32[]{:S(2)}, u32[]{:S(2)}) collective-permute-start(bf16[64,512]{1,0:T(8,128)(2,1)S(1)} %dynamic-slice_add_fusion.1), channel_id=1, source_target_pairs={{0,8},{1,9},{2,10},{3,11},{4,12},{5,13},{6,14},{7,15},{8,0},{9,1},... | collective-permute-start | bytes 196616 | tf_op jit(solution)/shard_map/ppermute | solution.py:21
  18.3 1.7 %collective-permute-start.10 = (bf16[64,512]{1,0:T(8,128)(2,1)S(1)}, bf16[64,512]{1,0:T(8,128)(2,1)S(1)}, u32[]{:S(2)}, u32[]{:S(2)}) collective-permute-start(bf16[64,512]{1,0:T(8,128)(2,1)S(1)} %dynamic-slice_add_fusion), channel_id=1, source_target_pairs={{0,8},{1,9},{2,10},{3,11},{4,12},{5,13},{6,14},{7,15},{8,0},{9,1},... | collective-permute-start | bytes 196616 | tf_op jit(solution)/shard_map/ppermute | solution.py:21
  20.0 2.3 %collective-permute-done.3 = bf16[64,512]{1,0:T(8,128)(2,1)S(1)} collective-permute-done((bf16[64,512]{1,0:T(8,128)(2,1)S(1)}, bf16[64,512]{1,0:T(8,128)(2,1)S(1)}, u32[]{:S(2)}, u32[]{:S(2)}) %collective-permute-start.3) | collective-permute-done | bytes 65568 | tf_op jit(solution)/shard_map/ppermute | solution.py:21
  23.6 1.6 %collective-permute-start.11 = (bf16[64,512]{1,0:T(8,128)(2,1)S(1)}, bf16[64,512]{1,0:T(8,128)(2,1)S(1)}, u32[]{:S(2)}, u32[]{:S(2)}) collective-permute-start(bf16[64,512]{1,0:T(8,128)(2,1)S(1)} %add.70), channel_id=1, source_target_pairs={{0,4},{1,5},{2,6},{3,7},{4,0},{5,1},{6,2},{7,3},{8,12},{9,13},{10,... | collective-permute-start | bytes 196616 | tf_op jit(solution)/shard_map/ppermute | solution.py:21
  25.2 1.4 %collective-permute-done.4 = bf16[64,512]{1,0:T(8,128)(2,1)S(1)} collective-permute-done((bf16[64,512]{1,0:T(8,128)(2,1)S(1)}, bf16[64,512]{1,0:T(8,128)(2,1)S(1)}, u32[]{:S(2)}, u32[]{:S(2)}) %collective-permute-start.4) | collective-permute-done | bytes 65568 | tf_op jit(solution)/shard_map/ppermute | solution.py:21
  26.7 1.6 %collective-permute-start.5 = (bf16[128,512]{1,0:T(8,128)(2,1)S(1)}, bf16[128,512]{1,0:T(8,128)(2,1)S(1)}, u32[]{:S(2)}, u32[]{:S(2)}) collective-permute-start(bf16[128,512]{1,0:T(8,128)(2,1)S(1)} %pad_maximum_fusion.2.refs_0_), channel_id=1, source_target_pairs={{0,2},{1,3},{2,0},{3,1},{4,6},{5,7},{6,4},{7,5},{8,10},{9,11},{10,... | collective-permute-start | bytes 393224 | tf_op jit(solution)/shard_map/ppermute | solution.py:21
  28.3 1.2 %collective-permute-start.12 = (bf16[128,512]{1,0:T(8,128)(2,1)S(1)}, bf16[128,512]{1,0:T(8,128)(2,1)S(1)}, u32[]{:S(2)}, u32[]{:S(2)}) collective-permute-start(bf16[128,512]{1,0:T(8,128)(2,1)S(1)} %pad_maximum_fusion.3.refs_0_), channel_id=1, source_target_pairs={{0,2},{1,3},{2,0},{3,1},{4,6},{5,7},{6,4},{7,5},{8,10},{9,11},{10,... | collective-permute-start | bytes 393224 | tf_op jit(solution)/shard_map/ppermute | solution.py:21
  30.0 1.7 %collective-permute-done.5.refs_1_ = bf16[128,512]{1,0:T(8,128)(2,1)S(1)} collective-permute-done((bf16[128,512]{1,0:T(8,128)(2,1)S(1)}, bf16[128,512]{1,0:T(8,128)(2,1)S(1)}, u32[]{:S(2)}, u32[]{:S(2)}) %collective-permute-start.5) | collective-permute-done | bytes 131104 | tf_op jit(solution)/shard_map/ppermute | solution.py:21
  31.7 1.6 %collective-permute-done.12.refs_1_ = bf16[128,512]{1,0:T(8,128)(2,1)S(1)} collective-permute-done((bf16[128,512]{1,0:T(8,128)(2,1)S(1)}, bf16[128,512]{1,0:T(8,128)(2,1)S(1)}, u32[]{:S(2)}, u32[]{:S(2)}) %collective-permute-start.12) | collective-permute-done | bytes 131104 | tf_op jit(solution)/shard_map/ppermute | solution.py:21
  33.6 2.1 %tables.1 = (bf16[4,256,256]{2,1,0:T(8,128)(2,1)S(1)}, bf16[4,256,256]{2,1,0:T(8,128)(2,1)S(1)}, bf16[4,256,256]{2,1,0:T(8,128)(2,1)S(1)}, bf16[4,256,256]{2,1,0...) custom-call(s32[2]{0:T(128)S(1)} %pad_add_fusion.1.first_ref), custom_call_target="tpu_custom_call" | custom-call | tf_op jit(solution)/shard_map/tables/pallas_call | solution.py:115
  35.7 1.2 %probe_waves.1 = (bf16[2,512,96]{2,1,0:T(8,128)(2,1)S(1)}, bf16[2,96,512]{2,1,0:T(8,128)(2,1)S(1)}) custom-call(s32[1]{0:T(128)} %bitcast.7.place_ref, s32[8,2]{1,0:T(8,128)S(1)} %copy.10.position_ref, s32[16,3]{1,0:T(8,128)S(1)} %copy.11.beam_ref), custom_call_target="tpu_custom_call" | custom-call | tf_op jit(solution)/shard_map/probe_waves/pallas_call | solution.py:169
  37.7 5.2 %shard_map.57.wave_ref = f32[2,512,512]{2,1,0:T(8,128)S(1)} custom-call(f32[512,512]{1,0:T(8,128)S(1)} %get-tuple-element.25.tr, f32[512,512]{1,0:T(8,128)S(1)} %get-tuple-element.26.ti, bf16[2,512,96]{2,1,0:T(8,128)(2,1)S(1)} %get-tuple-element.27.left_ref, bf16[2,96,512]{2,1,0:T(8,128)(2,1)S(1)} %get-tuple-element.28.right_ref, ...), custom_call_target="tpu_custom_call" | custom-call | tf_op jit(solution)/shard_map/pallas_call | solution.py:403
  42.8 5.3 %shard_map.55.wave_ref = f32[2,512,512]{2,1,0:T(8,128)S(1)} custom-call(f32[512,512]{1,0:T(8,128)S(1)} %get-tuple-element.25.tr, f32[512,512]{1,0:T(8,128)S(1)} %get-tuple-element.26.ti, bf16[2,512,96]{2,1,0:T(8,128)(2,1)S(1)} %get-tuple-element.27.left_ref, bf16[2,96,512]{2,1,0:T(8,128)(2,1)S(1)} %get-tuple-element.28.right_ref, ...), custom_call_target="tpu_custom_call" | custom-call | tf_op jit(solution)/shard_map/pallas_call | solution.py:403
  48.9 3.6 %shard_map.58 = (f32[2,32,256]{2,1,0:T(8,128)S(1)}, f32[2,32,256]{2,1,0:T(8,128)S(1)}) custom-call(f32[512,512]{1,0:T(8,128)S(1)} %get-tuple-element.23.tr, f32[512,512]{1,0:T(8,128)S(1)} %get-tuple-element.24.ti, f32[2,512,512]{2,1,0:T(8,128)S(1)} %shard_map.57.wave_ref, bf16[4,256,256]{2,1,0:T(8,128)(2,1)S(1)} %get-tuple-element.29.wh, ...), custom_call_target="tpu_custom_call" | custom-call | tf_op jit(solution)/shard_map/pallas_call | solution.py:403
  52.5 1.4 %collective-permute-start.16 = (f32[2,32,256]{2,1,0:T(8,128)S(1)}, f32[2,32,256]{2,1,0:T(8,128)S(1)}, u32[]{:S(2)}, u32[]{:S(2)}) collective-permute-start(f32[2,32,256]{2,1,0:T(8,128)S(1)} %get-tuple-element.40), channel_id=1, source_target_pairs={{0,2},{1,3},{2,0},{3,1},{4,6},{5,7},{6,4},{7,5},{8,10},{9,11},{10,... | collective-permute-start | bytes 196616 | tf_op jit(solution)/shard_map/ppermute | solution.py:21
  53.9 3.6 %shard_map.56 = (f32[2,32,256]{2,1,0:T(8,128)S(1)}, f32[2,32,256]{2,1,0:T(8,128)S(1)}) custom-call(f32[512,512]{1,0:T(8,128)S(1)} %get-tuple-element.23.tr, f32[512,512]{1,0:T(8,128)S(1)} %get-tuple-element.24.ti, f32[2,512,512]{2,1,0:T(8,128)S(1)} %shard_map.55.wave_ref, bf16[4,256,256]{2,1,0:T(8,128)(2,1)S(1)} %get-tuple-element.29.wh, ...), custom_call_target="tpu_custom_call" | custom-call | tf_op jit(solution)/shard_map/pallas_call | solution.py:403
  58.3 3.6 %collective-permute-done.15 = f32[2,32,256]{2,1,0:T(8,128)S(1)} collective-permute-done((f32[2,32,256]{2,1,0:T(8,128)S(1)}, f32[2,32,256]{2,1,0:T(8,128)S(1)}, u32[]{:S(2)}, u32[]{:S(2)}) %collective-permute-start.15) | collective-permute-done | bytes 65568 | tf_op jit(solution)/shard_map/ppermute | solution.py:21
  62.1 1.3 %collective-permute-done.17 = f32[4,2,16,256]{3,2,1,0:T(8,128)S(1)} collective-permute-done((f32[4,2,16,256]{3,2,1,0:T(8,128)S(1)}, f32[4,2,16,256]{3,2,1,0:T(8,128)S(1)}, u32[]{:S(2)}, u32[]{:S(2)}) %collective-permute-start.17) | collective-permute-done | bytes 131104 | tf_op jit(solution)/shard_map/ppermute | solution.py:21
  63.7 0.9 %reshape.24 = f32[16,2,8,256]{3,2,1,0:T(8,128)} reshape(f32[16,2,2,2,2,256]{5,4,3,2,1,0:T(2,128)S(1)} %copy.12) | data formatting | bytes 524288 | tf_op jit(solution)/shard_map/reshape | solution.py:458
  (53 shorter events, 7.1 us)
Async XLA Ops:
  1.1 1.7 %collective-permute-start = (bf16[256,512]{1,0:T(8,128)(2,1)S(1)}, bf16[256,512]{1,0:T(8,128)(2,1)S(1)}, u32[]{:S(2)}, u32[]{:S(2)}) collective-permute-start(bf16[256,512]{1,0:T(8,128)(2,1)S(1)} %get-tuple-element.44), channel_id=1, source_target_pairs={{0,1},{1,0},{2,3},{3,2},{4,5},{5,4},{6,7},{7,6},{8,9},{9,8},{10,11... | collective-permute-start | bytes 786440 | tf_op jit(solution)/shard_map/ppermute | solution.py:21
  2.9 30.4 %copy-start = (s32[16,2]{0,1:T(2,128)S(1)}, s32[16,2]{0,1:T(2,128)}, u32[]{:S(2)}) copy-start(s32[16,2]{0,1:T(2,128)} %param.7) | copy-start | bytes 388
  2.9 30.4 %copy-start.2 = (s32[16]{0:T(128)S(1)}, s32[16]{0:T(128)}, u32[]{:S(2)}) copy-start(s32[16]{0:T(128)} %param.8) | copy-start | bytes 196
  2.9 30.4 %copy-start.1 = (s32[8,2]{0,1:T(2,128)S(1)}, s32[8,2]{0,1:T(2,128)}, u32[]{:S(2)}) copy-start(s32[8,2]{0,1:T(2,128)} %param.9) | copy-start | bytes 196
  3.0 7.3 %collective-permute-start.1 = (bf16[128,512]{1,0:T(8,128)(2,1)S(1)}, bf16[128,512]{1,0:T(8,128)(2,1)S(1)}, u32[]{:S(2)}, u32[]{:S(2)}) collective-permute-start(bf16[128,512]{1,0:T(8,128)(2,1)S(1)} %dynamic-slice_bitcast_fusion.3), channel_id=1, source_target_pairs={{0,2},{1,3},{2,0},{3,1},{4,6},{5,7},{6,4},{7,5},{8,10},{9,11},{10,... | collective-permute-start | bytes 393224 | tf_op jit(solution)/shard_map/ppermute | solution.py:21
  6.0 6.6 %collective-permute-start.8 = (bf16[128,512]{1,0:T(8,128)(2,1)S(1)}, bf16[128,512]{1,0:T(8,128)(2,1)S(1)}, u32[]{:S(2)}, u32[]{:S(2)}) collective-permute-start(bf16[128,512]{1,0:T(8,128)(2,1)S(1)} %dynamic-slice_bitcast_fusion.2), channel_id=1, source_target_pairs={{0,2},{1,3},{2,0},{3,1},{4,6},{5,7},{6,4},{7,5},{8,10},{9,11},{10,... | collective-permute-start | bytes 393224 | tf_op jit(solution)/shard_map/ppermute | solution.py:21
  10.4 4.4 %collective-permute-start.2 = (bf16[64,512]{1,0:T(8,128)(2,1)S(1)}, bf16[64,512]{1,0:T(8,128)(2,1)S(1)}, u32[]{:S(2)}, u32[]{:S(2)}) collective-permute-start(bf16[64,512]{1,0:T(8,128)(2,1)S(1)} %constant_dynamic-slice_fusion.1), channel_id=1, source_target_pairs={{0,4},{1,5},{2,6},{3,7},{4,0},{5,1},{6,2},{7,3},{8,12},{9,13},{10,... | collective-permute-start | bytes 196616 | tf_op jit(solution)/shard_map/ppermute | solution.py:21
  12.6 5.7 %collective-permute-start.9 = (bf16[64,512]{1,0:T(8,128)(2,1)S(1)}, bf16[64,512]{1,0:T(8,128)(2,1)S(1)}, u32[]{:S(2)}, u32[]{:S(2)}) collective-permute-start(bf16[64,512]{1,0:T(8,128)(2,1)S(1)} %constant_dynamic-slice_fusion), channel_id=1, source_target_pairs={{0,4},{1,5},{2,6},{3,7},{4,0},{5,1},{6,2},{7,3},{8,12},{9,13},{10,... | collective-permute-start | bytes 196616 | tf_op jit(solution)/shard_map/ppermute | solution.py:21
  14.8 7.5 %collective-permute-start.3 = (bf16[64,512]{1,0:T(8,128)(2,1)S(1)}, bf16[64,512]{1,0:T(8,128)(2,1)S(1)}, u32[]{:S(2)}, u32[]{:S(2)}) collective-permute-start(bf16[64,512]{1,0:T(8,128)(2,1)S(1)} %dynamic-slice_add_fusion.1), channel_id=1, source_target_pairs={{0,8},{1,9},{2,10},{3,11},{4,12},{5,13},{6,14},{7,15},{8,0},{9,1},... | collective-permute-start | bytes 196616 | tf_op jit(solution)/shard_map/ppermute | solution.py:21
  18.3 5.2 %collective-permute-start.10 = (bf16[64,512]{1,0:T(8,128)(2,1)S(1)}, bf16[64,512]{1,0:T(8,128)(2,1)S(1)}, u32[]{:S(2)}, u32[]{:S(2)}) collective-permute-start(bf16[64,512]{1,0:T(8,128)(2,1)S(1)} %dynamic-slice_add_fusion), channel_id=1, source_target_pairs={{0,8},{1,9},{2,10},{3,11},{4,12},{5,13},{6,14},{7,15},{8,0},{9,1},... | collective-permute-start | bytes 196616 | tf_op jit(solution)/shard_map/ppermute | solution.py:21
  22.3 4.3 %collective-permute-start.4 = (bf16[64,512]{1,0:T(8,128)(2,1)S(1)}, bf16[64,512]{1,0:T(8,128)(2,1)S(1)}, u32[]{:S(2)}, u32[]{:S(2)}) collective-permute-start(bf16[64,512]{1,0:T(8,128)(2,1)S(1)} %add.67), channel_id=1, source_target_pairs={{0,4},{1,5},{2,6},{3,7},{4,0},{5,1},{6,2},{7,3},{8,12},{9,13},{10,... | collective-permute-start | bytes 196616 | tf_op jit(solution)/shard_map/ppermute | solution.py:21
  23.6 4.7 %collective-permute-start.11 = (bf16[64,512]{1,0:T(8,128)(2,1)S(1)}, bf16[64,512]{1,0:T(8,128)(2,1)S(1)}, u32[]{:S(2)}, u32[]{:S(2)}) collective-permute-start(bf16[64,512]{1,0:T(8,128)(2,1)S(1)} %add.70), channel_id=1, source_target_pairs={{0,4},{1,5},{2,6},{3,7},{4,0},{5,1},{6,2},{7,3},{8,12},{9,13},{10,... | collective-permute-start | bytes 196616 | tf_op jit(solution)/shard_map/ppermute | solution.py:21
  26.7 5.0 %collective-permute-start.5 = (bf16[128,512]{1,0:T(8,128)(2,1)S(1)}, bf16[128,512]{1,0:T(8,128)(2,1)S(1)}, u32[]{:S(2)}, u32[]{:S(2)}) collective-permute-start(bf16[128,512]{1,0:T(8,128)(2,1)S(1)} %pad_maximum_fusion.2.refs_0_), channel_id=1, source_target_pairs={{0,2},{1,3},{2,0},{3,1},{4,6},{5,7},{6,4},{7,5},{8,10},{9,11},{10,... | collective-permute-start | bytes 393224 | tf_op jit(solution)/shard_map/ppermute | solution.py:21
  28.3 5.0 %collective-permute-start.12 = (bf16[128,512]{1,0:T(8,128)(2,1)S(1)}, bf16[128,512]{1,0:T(8,128)(2,1)S(1)}, u32[]{:S(2)}, u32[]{:S(2)}) collective-permute-start(bf16[128,512]{1,0:T(8,128)(2,1)S(1)} %pad_maximum_fusion.3.refs_0_), channel_id=1, source_target_pairs={{0,2},{1,3},{2,0},{3,1},{4,6},{5,7},{6,4},{7,5},{8,10},{9,11},{10,... | collective-permute-start | bytes 393224 | tf_op jit(solution)/shard_map/ppermute | solution.py:21
  29.5 18.7 %collective-permute-start.6 = (bf16[128,512]{1,0:T(8,128)(2,1)S(1)}, bf16[128,512]{1,0:T(8,128)(2,1)S(1)}, u32[]{:S(2)}, u32[]{:S(2)}) collective-permute-start(bf16[128,512]{1,0:T(8,128)(2,1)S(1)} %pad_maximum_fusion.2.refs_0_), channel_id=1, source_target_pairs={{0,1},{1,0},{2,3},{3,2},{4,5},{5,4},{6,7},{7,6},{8,9},{9,8},{10,11... | collective-permute-start | bytes 393224 | tf_op jit(solution)/shard_map/ppermute | solution.py:21
  29.5 7.5 %collective-permute-start.13 = (bf16[128,512]{1,0:T(8,128)(2,1)S(1)}, bf16[128,512]{1,0:T(8,128)(2,1)S(1)}, u32[]{:S(2)}, u32[]{:S(2)}) collective-permute-start(bf16[128,512]{1,0:T(8,128)(2,1)S(1)} %pad_maximum_fusion.3.refs_0_), channel_id=1, source_target_pairs={{0,1},{1,0},{2,3},{3,2},{4,5},{5,4},{6,7},{7,6},{8,9},{9,8},{10,11... | collective-permute-start | bytes 393224 | tf_op jit(solution)/shard_map/ppermute | solution.py:21
  31.7 16.5 %collective-permute-start.7 = (bf16[128,512]{1,0:T(8,128)(2,1)S(1)}, bf16[128,512]{1,0:T(8,128)(2,1)S(1)}, u32[]{:S(2)}, u32[]{:S(2)}) collective-permute-start(bf16[128,512]{1,0:T(8,128)(2,1)S(1)} %collective-permute-done.5.refs_1_), channel_id=1, source_target_pairs={{0,1},{1,0},{2,3},{3,2},{4,5},{5,4},{6,7},{7,6},{8,9},{9,8},{10,11... | collective-permute-start | bytes 393224 | tf_op jit(solution)/shard_map/ppermute | solution.py:21
  33.3 3.7 %collective-permute-start.14 = (bf16[128,512]{1,0:T(8,128)(2,1)S(1)}, bf16[128,512]{1,0:T(8,128)(2,1)S(1)}, u32[]{:S(2)}, u32[]{:S(2)}) collective-permute-start(bf16[128,512]{1,0:T(8,128)(2,1)S(1)} %collective-permute-done.12.refs_1_), channel_id=1, source_target_pairs={{0,1},{1,0},{2,3},{3,2},{4,5},{5,4},{6,7},{7,6},{8,9},{9,8},{10,11... | collective-permute-start | bytes 393224 | tf_op jit(solution)/shard_map/ppermute | solution.py:21
  52.5 5.8 %collective-permute-start.16 = (f32[2,32,256]{2,1,0:T(8,128)S(1)}, f32[2,32,256]{2,1,0:T(8,128)S(1)}, u32[]{:S(2)}, u32[]{:S(2)}) collective-permute-start(f32[2,32,256]{2,1,0:T(8,128)S(1)} %get-tuple-element.40), channel_id=1, source_target_pairs={{0,2},{1,3},{2,0},{3,1},{4,6},{5,7},{6,4},{7,5},{8,10},{9,11},{10,... | collective-permute-start | bytes 196616 | tf_op jit(solution)/shard_map/ppermute | solution.py:21
  57.6 4.3 %collective-permute-start.15 = (f32[2,32,256]{2,1,0:T(8,128)S(1)}, f32[2,32,256]{2,1,0:T(8,128)S(1)}, u32[]{:S(2)}, u32[]{:S(2)}) collective-permute-start(f32[2,32,256]{2,1,0:T(8,128)S(1)} %get-tuple-element.39), channel_id=1, source_target_pairs={{0,2},{1,3},{2,0},{3,1},{4,6},{5,7},{6,4},{7,5},{8,10},{9,11},{10,... | collective-permute-start | bytes 196616 | tf_op jit(solution)/shard_map/ppermute | solution.py:21
  62.0 1.4 %collective-permute-start.17 = (f32[4,2,16,256]{3,2,1,0:T(8,128)S(1)}, f32[4,2,16,256]{3,2,1,0:T(8,128)S(1)}, u32[]{:S(2)}, u32[]{:S(2)}) collective-permute-start(f32[4,2,16,256]{3,2,1,0:T(8,128)S(1)} %get-tuple-element.46), channel_id=1, source_target_pairs={{0,1},{1,0},{2,3},{3,2},{4,5},{5,4},{6,7},{7,6},{8,9},{9,8},{10,11... | collective-permute-start | bytes 393224 | tf_op jit(solution)/shard_map/ppermute | solution.py:21

commit v3 on v2

--- a/solution.py
+++ b/solution.py
@@ -42,12 +42,14 @@
         own = own * 2 + side
         parts = [half(p, side) + flip(half(p, 1 - side), bit, groups) for p in parts]
     parts = [p + flip(p, bits[-1], groups) for p in parts]
-    for bit in reversed(bits[2:-1]):
+    for bit in reversed(bits[3:-1]):
         parts = [jnp.concatenate([p, flip(p, bit, groups)], axis=0) for p in parts]
     pieces = []
     for part in parts:
-        other = flip(part, 2, groups)
-        pieces.append((part, other, flip(part, 1, groups), flip(other, 1, groups)))
+        grown = [part]
+        for bit in reversed(bits[:3]):
+            grown = grown + [flip(p, bit, groups) for p in grown]
+        pieces.append(grown)
     return pieces, own.astype(jnp.int32).reshape(1)
 
 
@@ -69,11 +71,9 @@
     return 1.0 - 2.0 * (s * s)
 
 
-def table_kernel(first_ref, wh, wl, vh, vl, pr, pi, dh, dl):
+def table_kernel(wh, wl, vh, vl):
     q = wh.shape[1] // 2
     n = 4 * q
-    kp = pr.shape[1]
-    take = dh.shape[1] // 2
     classes, _ = class_frequencies(n)
 
     def iota(shape, axis):
@@ -89,6 +89,19 @@
         cos, sin = cos.T, sin.T
         for a, b, part in ((0, 0, cos), (0, 1, sin), (1, 0, -sin), (1, 1, cos)):
             vh[c, a * q : (a + 1) * q, b * q : (b + 1) * q], vl[c, a * q : (a + 1) * q, b * q : (b + 1) * q] = split(part)
+
+
+def late_table_kernel(first_ref, pr, pi, dh, dl):
+    q = dh.shape[2] // 2
+    n = 4 * q
+    kp = pr.shape[1]
+    take = dh.shape[1] // 2
+    classes, _ = class_frequencies(n)
+
+    def iota(shape, axis):
+        return lax.broadcasted_iota(jnp.int32, shape, axis)
+
+    for c, (first, count) in enumerate(classes):
         row, lane = iota((kp, q), 0), iota((kp, q), 1)
         for l, (first_l, count_l) in enumerate(classes):
             u, v = first + 4 * row, first_l + 4 * lane
@@ -112,15 +125,24 @@
     full = jax.ShapeDtypeStruct((4, 2 * q, 2 * q), BF16)
     prop = jax.ShapeDtypeStruct((4, kp, grid), F32)
     last = jax.ShapeDtypeStruct((4, 2 * rows, 2 * q), BF16)
+    vmem = pl.BlockSpec(memory_space=pltpu.VMEM)
+    params = pltpu.CompilerParams(vmem_limit_bytes=12 << 20)
     out = pl.pallas_call(
         table_kernel,
         name="tables",
+        out_specs=[vmem] * 4,
+        out_shape=[full] * 4,
+        compiler_params=params,
+    )()
+    late = pl.pallas_call(
+        late_table_kernel,
+        name="late_tables",
         in_specs=[pl.BlockSpec(memory_space=pltpu.SMEM)],
-        out_specs=[pl.BlockSpec(memory_space=pltpu.VMEM)] * 8,
-        out_shape=[full, full, full, full, prop, prop, last, last],
-        compiler_params=pltpu.CompilerParams(vmem_limit_bytes=12 << 20),
+        out_specs=[vmem] * 4,
+        out_shape=[prop, prop, last, last],
+        compiler_params=params,
     )(jnp.stack([first_row, order]).astype(jnp.int32))
-    return out[0:2], out[2:4], out[4:6], out[6:8]
+    return out[0:2], out[2:4], late[0:2], late[2:4]
 
 
 def wave_kernel(place_ref, position_ref, beam_ref, left_ref, right_ref):
@@ -353,7 +375,16 @@
                 out_ref[1, at, pl.ds(j * q, q)] = i
 
 
-def last_kernel(tr, ti, wave_ref, wh, wl, vh, vl, pr, pi, dh, dl, keep_ref, away_ref, yh, yl, sr, si, zh, zl, uh, ul):
+def last_kernel(probes, tr, ti, *refs):
+    waves, (wh, wl, vh, vl, pr, pi, dh, dl, keep_ref, away_ref) = refs[:probes], refs[probes : probes + 10]
+    scratch = refs[probes + 10 :]
+    each = len(scratch) // probes
+    for p in range(probes):
+        own = scratch[p * each : (p + 1) * each]
+        last_one(tr, ti, waves[p], wh, wl, vh, vl, pr, pi, dh, dl, keep_ref.at[p], away_ref.at[p], *own)
+
+
+def last_one(tr, ti, wave_ref, wh, wl, vh, vl, pr, pi, dh, dl, keep_ref, away_ref, yh, yl, sr, si, zh, zl, uh, ul):
     n = tr.shape[0]
     q = n // 4
     take = dh.shape[1] // 2
@@ -383,6 +414,20 @@
             away_ref[c, :, j * q : (j + 1) * q] = part[take // 2 :]
 
 
+def gather_kernel(place_ref, pair_ref, other_ref, out_ref, buffer):
+    rows, _, probes, _ = out_ref.shape
+    per_device = probes // QUAD
+    for y in range(2):
+        for core in range(2):
+            slot = (place_ref[0] ^ (2 * y + core)) * per_device
+            for p in range(per_device):
+                source = other_ref[y * per_device + p] if core else pair_ref[y * per_device + p, :, :rows]
+                buffer[slot + p] = source
+    for r in range(rows):
+        for c in range(2):
+            out_ref[r, c] = buffer[:, c, r, :]
+
+
 def forward_scratch(n):
     q = n // 4
     return [
@@ -406,7 +451,7 @@
         out_specs=[vmem] * len(out_shapes),
         out_shape=[jax.ShapeDtypeStruct(shape, F32) for shape in out_shapes],
         scratch_shapes=first + forward_scratch(n) + extra,
-        compiler_params=pltpu.CompilerParams(vmem_limit_bytes=32 << 20),
+        compiler_params=pltpu.CompilerParams(vmem_limit_bytes=36 << 20),
     )(*inputs)
 
 
@@ -442,20 +487,22 @@
         waves = [run_kernel(middle_kernel, (*turned, w, *tables), [w.shape], [], extra)[0] for w in waves]
     turned = transmit(own, slabs[-1], blocks)
 
-    kept, other = [], []
-    for p in range(per_device):
-        inputs = (*turned, waves[p], *tables, *last_rows)
-        shape = (2, quad_rows // 2, crop)
-        keep, away = run_kernel(last_kernel, inputs, [shape, shape], [], [])
-        kept.append(keep)
-        other.append(flip(away, 2, groups))
-    pair = jnp.stack(kept + other)
+    inputs = (*turned, *waves, *tables, *last_rows)
+    shape = (per_device, 2, quad_rows // 2, crop)
+    more = forward_scratch(grid) * (per_device - 1)
+    keep, away = run_kernel(functools.partial(last_kernel, per_device), inputs, [shape, shape], [], more)
+    pair = jnp.concatenate([keep, flip(away, 2, groups)], axis=0)
     other = flip(pair[:, :, own_rows:], 1, groups)
-    side_y, side_core = (place // 2) & 1, place & 1
-    four = jnp.stack([pair[:, :, :own_rows], other]).reshape(2, 2, per_device, 2, own_rows, crop)
-    four = jnp.where(side_core == 0, four, four[::-1])
-    four = jnp.where(side_y == 0, four, four[:, ::-1])
-    return jnp.transpose(four, (4, 3, 1, 0, 2, 5)).reshape(own_rows, 2, probes, crop)
+    vmem = pl.BlockSpec(memory_space=pltpu.VMEM)
+    return pl.pallas_call(
+        gather_kernel,
+        name="gather_probes",
+        in_specs=[pl.BlockSpec(memory_space=pltpu.SMEM), vmem, vmem],
+        out_specs=vmem,
+        out_shape=jax.ShapeDtypeStruct((own_rows, 2, probes, crop), F32),
+        scratch_shapes=[pltpu.VMEM((probes, 2, own_rows, crop), F32)],
+        compiler_params=pltpu.CompilerParams(vmem_limit_bytes=8 << 20),
+    )(place.astype(jnp.int32).reshape(1), pair, other)
 
 
 def solution(mesh):

time: 64.7 us -> 70.3 us (1.087)
  local copies, waits for them, and re-layouts: 2.45 us -> 8.28 us
  waiting for transfers between devices: 17.6 us -> 13.2 us
  Pallas kernels: 22.5 us -> 24.9 us
  starting transfers between devices: 20.6 us -> 22.3 us
    unnamed x7 -> x28, local copies, waits for them, and re-layouts: 0.1 us -> 7.02 us
    ppermute x18 -> x23, waiting for transfers between devices: 17.6 us -> 13.2 us  [flip(): return lax.ppermute(array, 'wide', [(i, i ^ bit) for i in range(groups)])]
    pallas_call x2, Pallas kernels: 1.34 us -> 3.29 us  [transmit(): pl.pallas_call(functools.partial(transmit_kernel, blocks=blocks), name='t...]
    ppermute x18 -> x23, starting transfers between devices: 20.6 us -> 22.3 us  [flip(): return lax.ppermute(array, 'wide', [(i, i ^ bit) for i in range(groups)])]
    reshape x1 -> x0, local copies, waits for them, and re-layouts: 0.88 us -> none  [local(): jnp.transpose(four, (4, 3, 1, 0, 2, 5)).reshape(own_rows, 2, probes, crop)]
    pallas_call x1 -> x3, Pallas kernels: 2.13 us -> 2.95 us  [the longest x1 1.49 us: make_tables(): pl.pallas_call(late_table_kernel, name='late_tables', in_specs=[pl.BlockS...]
    pallas_call x4 -> x3, Pallas kernels: 17.8 us -> 17.4 us  [run_kernel(): pl.pallas_call(kernel, in_specs=[vmem] * len(inputs), out_specs=[vmem] *...]
  transfers between devices with their start and end apart: 18 -> 23, of which waited for: 11 -> 7; matrix products, arithmetic and copies ran while one was open for 2% -> 2% of each run, Pallas kernels for 28% -> 22%
where the time goes in v3:
time: 70.3 us; the launch traced here: 69.9 us
  Pallas kernels  24.9 us (35%)
  starting transfers between devices  22.3 us (32%)
  waiting for transfers between devices  13.2 us (19%)
  local copies, waits for them, and re-layouts  8.28 us (12%)
  other arithmetic  1.02 us (1%)
    ppermute x23, starting transfers between devices, flip(): return lax.ppermute(array, 'wide', [(i, i ^ bit) for i in range(groups)])  22.3 us
    pallas_call x3, Pallas kernels, run_kernel(): pl.pallas_call(kernel, in_specs=[vmem] * len(inputs), out_specs=[vmem] *...  17.4 us
    ppermute x23, waiting for transfers between devices, flip(): return lax.ppermute(array, 'wide', [(i, i ^ bit) for i in range(groups)])  13.2 us
    unnamed x28, local copies, waits for them, and re-layouts  7.02 us
    pallas_call x2, Pallas kernels, transmit(): pl.pallas_call(functools.partial(transmit_kernel, blocks=blocks), name='t...  3.29 us
    pallas_call x1, Pallas kernels, make_tables(): pl.pallas_call(late_table_kernel, name='late_tables', in_specs=[pl.BlockS...  1.49 us
  transfers between devices with their start and end apart: 23, of which 7 were waited for; matrix products, arithmetic and copies ran while one was open for 2% of the time, Pallas kernels for 22%

profile of v3, /device:TPU:0, one launch (start us, length us, event | category | flops | bytes accessed | tf_op | source)
XLA Modules:
  0.0 69.9 jit_solution(1784670089905776049)
XLA Ops:
  0.0 1.1 %dynamic-slice_bitcast_fusion.1 = (bf16[256,512]{1,0:T(8,128)(2,1)S(1)}, bf16[256,512]{1,0:T(8,128)(2,1)S(1)}) fusion(bf16[1,512,512]{2,1,0:T(8,128)(2,1)} %param.5, s32[]{:T(128)S(6)} %select_n.48, s32[]{:T(128)S(6)} %select_n.49), kind=kLoop, calls=%fused_computation.2 | loop fusion | bytes 1048584 | tf_op jit(solution)/shard_map/dynamic_slice | solution.py:26
  3.0 2.9 %collective-permute-start.11 = (bf16[128,512]{1,0:T(8,128)(2,1)S(1)}, bf16[128,512]{1,0:T(8,128)(2,1)S(1)}, u32[]{:S(2)}, u32[]{:S(2)}) collective-permute-start(bf16[128,512]{1,0:T(8,128)(2,1)S(1)} %dynamic-slice_bitcast_fusion.2), channel_id=1, source_target_pairs={{0,2},{1,3},{2,0},{3,1},{4,6},{5,7},{6,4},{7,5},{8,10},{9,11},{10,... | collective-permute-start | bytes 393224 | tf_op jit(solution)/shard_map/ppermute | solution.py:21
  6.1 4.2 %collective-permute-done.11 = bf16[128,512]{1,0:T(8,128)(2,1)S(1)} collective-permute-done((bf16[128,512]{1,0:T(8,128)(2,1)S(1)}, bf16[128,512]{1,0:T(8,128)(2,1)S(1)}, u32[]{:S(2)}, u32[]{:S(2)}) %collective-permute-start.11) | collective-permute-done | bytes 131104 | tf_op jit(solution)/shard_map/ppermute | solution.py:21
  10.3 2.1 %collective-permute-start.12 = (bf16[64,512]{1,0:T(8,128)(2,1)S(1)}, bf16[64,512]{1,0:T(8,128)(2,1)S(1)}, u32[]{:S(2)}, u32[]{:S(2)}) collective-permute-start(bf16[64,512]{1,0:T(8,128)(2,1)S(1)} %constant_dynamic-slice_fusion), channel_id=1, source_target_pairs={{0,4},{1,5},{2,6},{3,7},{4,0},{5,1},{6,2},{7,3},{8,12},{9,13},{10,... | collective-permute-start | bytes 196616 | tf_op jit(solution)/shard_map/ppermute | solution.py:21
  12.6 1.9 %collective-permute-start.2 = (bf16[64,512]{1,0:T(8,128)(2,1)S(1)}, bf16[64,512]{1,0:T(8,128)(2,1)S(1)}, u32[]{:S(2)}, u32[]{:S(2)}) collective-permute-start(bf16[64,512]{1,0:T(8,128)(2,1)S(1)} %constant_dynamic-slice_fusion.1), channel_id=1, source_target_pairs={{0,4},{1,5},{2,6},{3,7},{4,0},{5,1},{6,2},{7,3},{8,12},{9,13},{10,... | collective-permute-start | bytes 196616 | tf_op jit(solution)/shard_map/ppermute | solution.py:21
  14.8 3.5 %collective-permute-start.13 = (bf16[64,512]{1,0:T(8,128)(2,1)S(1)}, bf16[64,512]{1,0:T(8,128)(2,1)S(1)}, u32[]{:S(2)}, u32[]{:S(2)}) collective-permute-start(bf16[64,512]{1,0:T(8,128)(2,1)S(1)} %dynamic-slice_add_fusion), channel_id=1, source_target_pairs={{0,8},{1,9},{2,10},{3,11},{4,12},{5,13},{6,14},{7,15},{8,0},{9,1},... | collective-permute-start | bytes 196616 | tf_op jit(solution)/shard_map/ppermute | solution.py:21
  18.3 1.7 %collective-permute-start.3 = (bf16[64,512]{1,0:T(8,128)(2,1)S(1)}, bf16[64,512]{1,0:T(8,128)(2,1)S(1)}, u32[]{:S(2)}, u32[]{:S(2)}) collective-permute-start(bf16[64,512]{1,0:T(8,128)(2,1)S(1)} %dynamic-slice_add_fusion.1), channel_id=1, source_target_pairs={{0,8},{1,9},{2,10},{3,11},{4,12},{5,13},{6,14},{7,15},{8,0},{9,1},... | collective-permute-start | bytes 196616 | tf_op jit(solution)/shard_map/ppermute | solution.py:21
  20.0 2.3 %collective-permute-done.13 = bf16[64,512]{1,0:T(8,128)(2,1)S(1)} collective-permute-done((bf16[64,512]{1,0:T(8,128)(2,1)S(1)}, bf16[64,512]{1,0:T(8,128)(2,1)S(1)}, u32[]{:S(2)}, u32[]{:S(2)}) %collective-permute-start.13) | collective-permute-done | bytes 65568 | tf_op jit(solution)/shard_map/ppermute | solution.py:21
  22.9 1.5 %collective-permute-start.15 = (bf16[64,512]{1,0:T(8,128)(2,1)S(1)}, bf16[64,512]{1,0:T(8,128)(2,1)}, u32[]{:S(2)}, u32[]{:S(2)}) collective-permute-start(bf16[64,512]{1,0:T(8,128)(2,1)S(1)} %add.69.refs_0_), channel_id=1, source_target_pairs={{0,2},{1,3},{2,0},{3,1},{4,6},{5,7},{6,4},{7,5},{8,10},{9,11},{10,... | collective-permute-start | bytes 196616 | tf_op jit(solution)/shard_map/ppermute | solution.py:21
  24.4 1.6 %collective-permute-start.4 = (bf16[64,512]{1,0:T(8,128)(2,1)S(1)}, bf16[64,512]{1,0:T(8,128)(2,1)}, u32[]{:S(2)}, u32[]{:S(2)}) collective-permute-start(bf16[64,512]{1,0:T(8,128)(2,1)S(1)} %add.66.refs_0_), channel_id=1, source_target_pairs={{0,4},{1,5},{2,6},{3,7},{4,0},{5,1},{6,2},{7,3},{8,12},{9,13},{10,... | collective-permute-start | bytes 196616 | tf_op jit(solution)/shard_map/ppermute | solution.py:21
  28.2 1.3 %collective-permute-start.16 = (bf16[64,512]{1,0:T(8,128)(2,1)}, bf16[64,512]{1,0:T(8,128)(2,1)}, u32[]{:S(2)}, u32[]{:S(2)}) collective-permute-start(bf16[64,512]{1,0:T(8,128)(2,1)} %collective-permute-done.14.refs_1_), channel_id=1, source_target_pairs={{0,2},{1,3},{2,0},{3,1},{4,6},{5,7},{6,4},{7,5},{8,10},{9,11},{10,... | collective-permute-start | bytes 196616 | tf_op jit(solution)/shard_map/ppermute | solution.py:21
  31.4 1.5 %late_tables.1 = (f32[4,96,512]{2,1,0:T(8,128)S(1)}, f32[4,96,512]{2,1,0:T(8,128)S(1)}, bf16[4,128,256]{2,1,0:T(8,128)(2,1)S(1)}, bf16[4,128,256]{2,1,0:T(8,128)(2,1)S(1)}) custom-call(s32[2]{0:T(128)S(1)} %pad_add_fusion.1.first_ref), custom_call_target="tpu_custom_call" | custom-call | tf_op jit(solution)/shard_map/late_tables/pallas_call | solution.py:137
  36.2 1.2 %probe_waves.1 = (bf16[2,512,96]{2,1,0:T(8,128)(2,1)S(1)}, bf16[2,96,512]{2,1,0:T(8,128)(2,1)S(1)}) custom-call(s32[1]{0:T(128)} %bitcast.place_ref, s32[8,2]{1,0:T(8,128)S(1)} %copy.9.position_ref, s32[16,3]{1,0:T(8,128)S(1)} %copy.10.beam_ref), custom_call_target="tpu_custom_call" | custom-call | tf_op jit(solution)/shard_map/probe_waves/pallas_call | solution.py:191
  38.3 0.8 %copy-done.7 = bf16[64,512]{1,0:T(8,128)(2,1)S(1)} copy-done((bf16[64,512]{1,0:T(8,128)(2,1)S(1)}, bf16[64,512]{1,0:T(8,128)(2,1)}, u32[]{:S(2)}) %copy-start.7) | copy-done | bytes 65560
  39.1 0.8 %copy-done.9 = bf16[64,512]{1,0:T(8,128)(2,1)S(1)} copy-done((bf16[64,512]{1,0:T(8,128)(2,1)S(1)}, bf16[64,512]{1,0:T(8,128)(2,1)}, u32[]{:S(2)}) %copy-start.9) | copy-done | bytes 65560
  39.9 1.6 %transmit.3 = (f32[512,512]{1,0:T(8,128)S(1)}, f32[512,512]{1,0:T(8,128)S(1)}) custom-call(s32[1]{0:T(128)} %bitcast.1.own_ref, bf16[64,512]{1,0:T(8,128)(2,1)S(1)} %add.69.refs_0_, bf16[64,512]{1,0:T(8,128)(2,1)} %collective-permute-done.14.refs_1_, bf16[64,512]{1,0:T(8,128)(2,1)} %collective-permute-done.15.refs_2_, ...), custom_call_target="tpu_custom_call" | custom-call | tf_op jit(solution)/shard_map/transmit/pallas_call | solution.py:260
  41.6 1.0 %copy-done.1 = bf16[4,256,256]{2,1,0:T(8,128)(2,1)S(1)} copy-done((bf16[4,256,256]{2,1,0:T(8,128)(2,1)S(1)}, bf16[4,256,256]{2,1,0:T(8,128)(2,1)}, u32[]{:S(2)}) %copy-start.1) | copy-done | bytes 524312
  42.6 5.1 %shard_map.56.refs_1_ = f32[2,512,512]{2,1,0:T(8,128)S(1)} custom-call(f32[512,512]{1,0:T(8,128)S(1)} %get-tuple-element.23.tr, f32[512,512]{1,0:T(8,128)S(1)} %get-tuple-element.24.ti, bf16[2,512,96]{2,1,0:T(8,128)(2,1)S(1)} %get-tuple-element.25.left_ref, bf16[2,96,512]{2,1,0:T(8,128)(2,1)S(1)} %get-tuple-element.26.right_ref, ...), custom_call_target="tpu_custom_call" | custom-call | tf_op jit(solution)/shard_map/pallas_call | solution.py:448
  47.7 5.3 %shard_map.55.refs_0_ = f32[2,512,512]{2,1,0:T(8,128)S(1)} custom-call(f32[512,512]{1,0:T(8,128)S(1)} %get-tuple-element.23.tr, f32[512,512]{1,0:T(8,128)S(1)} %get-tuple-element.24.ti, bf16[2,512,96]{2,1,0:T(8,128)(2,1)S(1)} %get-tuple-element.25.left_ref, bf16[2,96,512]{2,1,0:T(8,128)(2,1)S(1)} %get-tuple-element.26.right_ref, ...), custom_call_target="tpu_custom_call" | custom-call | tf_op jit(solution)/shard_map/pallas_call | solution.py:448
  53.1 1.7 %transmit.2 = (f32[512,512]{1,0:T(8,128)S(1)}, f32[512,512]{1,0:T(8,128)S(1)}) custom-call(s32[1]{0:T(128)} %bitcast.1.own_ref, bf16[64,512]{1,0:T(8,128)(2,1)S(1)} %add.66.refs_0_, bf16[64,512]{1,0:T(8,128)(2,1)} %collective-permute-done.4.refs_1_, bf16[64,512]{1,0:T(8,128)(2,1)} %collective-permute-done.5.refs_2_, ...), custom_call_target="tpu_custom_call" | custom-call | tf_op jit(solution)/shard_map/transmit/pallas_call | solution.py:260
  54.8 6.9 %shard_map.57 = (f32[2,2,32,256]{3,2,1,0:T(8,128)S(1)}, f32[2,2,32,256]{3,2,1,0:T(8,128)S(1)}) custom-call(f32[512,512]{1,0:T(8,128)S(1)} %get-tuple-element.21.tr, f32[512,512]{1,0:T(8,128)S(1)} %get-tuple-element.22.ti, f32[2,512,512]{2,1,0:T(8,128)S(1)} %shard_map.55.refs_0_, f32[2,512,512]{2,1,0:T(8,128)S(1)} %shard_map.56.refs_1_, ...), custom_call_target="tpu_custom_call" | custom-call | tf_op jit(solution)/shard_map/pallas_call | solution.py:448
  61.8 1.4 %collective-permute-start.21 = (f32[2,2,32,256]{3,2,1,0:T(8,128)S(1)}, f32[2,2,32,256]{3,2,1,0:T(8,128)S(1)}, u32[]{:S(2)}, u32[]{:S(2)}) collective-permute-start(f32[2,2,32,256]{3,2,1,0:T(8,128)S(1)} %get-tuple-element.36), channel_id=1, source_target_pairs={{0,2},{1,3},{2,0},{3,1},{4,6},{5,7},{6,4},{7,5},{8,10},{9,11},{10,... | collective-permute-start | bytes 393224 | tf_op jit(solution)/shard_map/ppermute | solution.py:21
  63.1 4.5 %collective-permute-done.21 = f32[2,2,32,256]{3,2,1,0:T(8,128)S(1)} collective-permute-done((f32[2,2,32,256]{3,2,1,0:T(8,128)S(1)}, f32[2,2,32,256]{3,2,1,0:T(8,128)S(1)}, u32[]{:S(2)}, u32[]{:S(2)}) %collective-permute-start.21) | collective-permute-done | bytes 131104 | tf_op jit(solution)/shard_map/ppermute | solution.py:21
  67.8 1.3 %collective-permute-done.22.other_ref = f32[4,2,16,256]{3,2,1,0:T(8,128)S(1)} collective-permute-done((f32[4,2,16,256]{3,2,1,0:T(8,128)S(1)}, f32[4,2,16,256]{3,2,1,0:T(8,128)S(1)}, u32[]{:S(2)}, u32[]{:S(2)}) %collective-permute-start.22) | collective-permute-done | bytes 131104 | tf_op jit(solution)/shard_map/ppermute | solution.py:21
  (78 shorter events, 12.2 us)
Async XLA Ops:
  1.1 1.7 %collective-permute-start = (bf16[256,512]{1,0:T(8,128)(2,1)S(1)}, bf16[256,512]{1,0:T(8,128)(2,1)S(1)}, u32[]{:S(2)}, u32[]{:S(2)}) collective-permute-start(bf16[256,512]{1,0:T(8,128)(2,1)S(1)} %get-tuple-element.40), channel_id=1, source_target_pairs={{0,1},{1,0},{2,3},{3,2},{4,5},{5,4},{6,7},{7,6},{8,9},{9,8},{10,11... | collective-permute-start | bytes 786440 | tf_op jit(solution)/shard_map/ppermute | solution.py:21
  2.8 33.3 %copy-start.11 = (s32[8,2]{0,1:T(2,128)S(1)}, s32[8,2]{0,1:T(2,128)}, u32[]{:S(2)}) copy-start(s32[8,2]{0,1:T(2,128)} %param.9) | copy-start | bytes 196
  3.0 7.3 %collective-permute-start.11 = (bf16[128,512]{1,0:T(8,128)(2,1)S(1)}, bf16[128,512]{1,0:T(8,128)(2,1)S(1)}, u32[]{:S(2)}, u32[]{:S(2)}) collective-permute-start(bf16[128,512]{1,0:T(8,128)(2,1)S(1)} %dynamic-slice_bitcast_fusion.2), channel_id=1, source_target_pairs={{0,2},{1,3},{2,0},{3,1},{4,6},{5,7},{6,4},{7,5},{8,10},{9,11},{10,... | collective-permute-start | bytes 393224 | tf_op jit(solution)/shard_map/ppermute | solution.py:21
  6.0 6.6 %collective-permute-start.1 = (bf16[128,512]{1,0:T(8,128)(2,1)S(1)}, bf16[128,512]{1,0:T(8,128)(2,1)S(1)}, u32[]{:S(2)}, u32[]{:S(2)}) collective-permute-start(bf16[128,512]{1,0:T(8,128)(2,1)S(1)} %dynamic-slice_bitcast_fusion.3), channel_id=1, source_target_pairs={{0,2},{1,3},{2,0},{3,1},{4,6},{5,7},{6,4},{7,5},{8,10},{9,11},{10,... | collective-permute-start | bytes 393224 | tf_op jit(solution)/shard_map/ppermute | solution.py:21
  10.3 4.4 %collective-permute-start.12 = (bf16[64,512]{1,0:T(8,128)(2,1)S(1)}, bf16[64,512]{1,0:T(8,128)(2,1)S(1)}, u32[]{:S(2)}, u32[]{:S(2)}) collective-permute-start(bf16[64,512]{1,0:T(8,128)(2,1)S(1)} %constant_dynamic-slice_fusion), channel_id=1, source_target_pairs={{0,4},{1,5},{2,6},{3,7},{4,0},{5,1},{6,2},{7,3},{8,12},{9,13},{10,... | collective-permute-start | bytes 196616 | tf_op jit(solution)/shard_map/ppermute | solution.py:21
  12.6 5.7 %collective-permute-start.2 = (bf16[64,512]{1,0:T(8,128)(2,1)S(1)}, bf16[64,512]{1,0:T(8,128)(2,1)S(1)}, u32[]{:S(2)}, u32[]{:S(2)}) collective-permute-start(bf16[64,512]{1,0:T(8,128)(2,1)S(1)} %constant_dynamic-slice_fusion.1), channel_id=1, source_target_pairs={{0,4},{1,5},{2,6},{3,7},{4,0},{5,1},{6,2},{7,3},{8,12},{9,13},{10,... | collective-permute-start | bytes 196616 | tf_op jit(solution)/shard_map/ppermute | solution.py:21
  14.8 7.5 %collective-permute-start.13 = (bf16[64,512]{1,0:T(8,128)(2,1)S(1)}, bf16[64,512]{1,0:T(8,128)(2,1)S(1)}, u32[]{:S(2)}, u32[]{:S(2)}) collective-permute-start(bf16[64,512]{1,0:T(8,128)(2,1)S(1)} %dynamic-slice_add_fusion), channel_id=1, source_target_pairs={{0,8},{1,9},{2,10},{3,11},{4,12},{5,13},{6,14},{7,15},{8,0},{9,1},... | collective-permute-start | bytes 196616 | tf_op jit(solution)/shard_map/ppermute | solution.py:21
  18.3 6.1 %collective-permute-start.3 = (bf16[64,512]{1,0:T(8,128)(2,1)S(1)}, bf16[64,512]{1,0:T(8,128)(2,1)S(1)}, u32[]{:S(2)}, u32[]{:S(2)}) collective-permute-start(bf16[64,512]{1,0:T(8,128)(2,1)S(1)} %dynamic-slice_add_fusion.1), channel_id=1, source_target_pairs={{0,8},{1,9},{2,10},{3,11},{4,12},{5,13},{6,14},{7,15},{8,0},{9,1},... | collective-permute-start | bytes 196616 | tf_op jit(solution)/shard_map/ppermute | solution.py:21
  22.3 5.9 %collective-permute-start.14 = (bf16[64,512]{1,0:T(8,128)(2,1)S(1)}, bf16[64,512]{1,0:T(8,128)(2,1)}, u32[]{:S(2)}, u32[]{:S(2)}) collective-permute-start(bf16[64,512]{1,0:T(8,128)(2,1)S(1)} %add.69.refs_0_), channel_id=1, source_target_pairs={{0,4},{1,5},{2,6},{3,7},{4,0},{5,1},{6,2},{7,3},{8,12},{9,13},{10,... | collective-permute-start | bytes 196616 | tf_op jit(solution)/shard_map/ppermute | solution.py:21
  22.9 6.6 %collective-permute-start.15 = (bf16[64,512]{1,0:T(8,128)(2,1)S(1)}, bf16[64,512]{1,0:T(8,128)(2,1)}, u32[]{:S(2)}, u32[]{:S(2)}) collective-permute-start(bf16[64,512]{1,0:T(8,128)(2,1)S(1)} %add.69.refs_0_), channel_id=1, source_target_pairs={{0,2},{1,3},{2,0},{3,1},{4,6},{5,7},{6,4},{7,5},{8,10},{9,11},{10,... | collective-permute-start | bytes 196616 | tf_op jit(solution)/shard_map/ppermute | solution.py:21
  24.4 5.1 %collective-permute-start.17 = (bf16[64,512]{1,0:T(8,128)(2,1)S(1)}, bf16[64,512]{1,0:T(8,128)(2,1)S(1)}, u32[]{:S(2)}, u32[]{:S(2)}) collective-permute-start(bf16[64,512]{1,0:T(8,128)(2,1)S(1)} %add.69.refs_0_), channel_id=1, source_target_pairs={{0,1},{1,0},{2,3},{3,2},{4,5},{5,4},{6,7},{7,6},{8,9},{9,8},{10,11... | collective-permute-start | bytes 196616 | tf_op jit(solution)/shard_map/ppermute | solution.py:21
  24.4 6.2 %collective-permute-start.4 = (bf16[64,512]{1,0:T(8,128)(2,1)S(1)}, bf16[64,512]{1,0:T(8,128)(2,1)}, u32[]{:S(2)}, u32[]{:S(2)}) collective-permute-start(bf16[64,512]{1,0:T(8,128)(2,1)S(1)} %add.66.refs_0_), channel_id=1, source_target_pairs={{0,4},{1,5},{2,6},{3,7},{4,0},{5,1},{6,2},{7,3},{8,12},{9,13},{10,... | collective-permute-start | bytes 196616 | tf_op jit(solution)/shard_map/ppermute | solution.py:21
  27.4 6.2 %collective-permute-start.5 = (bf16[64,512]{1,0:T(8,128)(2,1)S(1)}, bf16[64,512]{1,0:T(8,128)(2,1)}, u32[]{:S(2)}, u32[]{:S(2)}) collective-permute-start(bf16[64,512]{1,0:T(8,128)(2,1)S(1)} %add.66.refs_0_), channel_id=1, source_target_pairs={{0,2},{1,3},{2,0},{3,1},{4,6},{5,7},{6,4},{7,5},{8,10},{9,11},{10,... | collective-permute-start | bytes 196616 | tf_op jit(solution)/shard_map/ppermute | solution.py:21
  28.2 5.5 %collective-permute-start.16 = (bf16[64,512]{1,0:T(8,128)(2,1)}, bf16[64,512]{1,0:T(8,128)(2,1)}, u32[]{:S(2)}, u32[]{:S(2)}) collective-permute-start(bf16[64,512]{1,0:T(8,128)(2,1)} %collective-permute-done.14.refs_1_), channel_id=1, source_target_pairs={{0,2},{1,3},{2,0},{3,1},{4,6},{5,7},{6,4},{7,5},{8,10},{9,11},{10,... | collective-permute-start | bytes 196616 | tf_op jit(solution)/shard_map/ppermute | solution.py:21
  29.5 4.7 %collective-permute-start.18 = (bf16[64,512]{1,0:T(8,128)(2,1)}, bf16[64,512]{1,0:T(8,128)(2,1)S(1)}, u32[]{:S(2)}, u32[]{:S(2)}) collective-permute-start(bf16[64,512]{1,0:T(8,128)(2,1)} %collective-permute-done.14.refs_1_), channel_id=1, source_target_pairs={{0,1},{1,0},{2,3},{3,2},{4,5},{5,4},{6,7},{7,6},{8,9},{9,8},{10,11... | collective-permute-start | bytes 196616 | tf_op jit(solution)/shard_map/ppermute | solution.py:21
  30.1 4.7 %collective-permute-start.19 = (bf16[64,512]{1,0:T(8,128)(2,1)}, bf16[64,512]{1,0:T(8,128)(2,1)S(1)}, u32[]{:S(2)}, u32[]{:S(2)}) collective-permute-start(bf16[64,512]{1,0:T(8,128)(2,1)} %collective-permute-done.15.refs_2_), channel_id=1, source_target_pairs={{0,1},{1,0},{2,3},{3,2},{4,5},{5,4},{6,7},{7,6},{8,9},{9,8},{10,11... | collective-permute-start | bytes 196616 | tf_op jit(solution)/shard_map/ppermute | solution.py:21
  30.6 5.3 %collective-permute-start.6 = (bf16[64,512]{1,0:T(8,128)(2,1)}, bf16[64,512]{1,0:T(8,128)(2,1)}, u32[]{:S(2)}, u32[]{:S(2)}) collective-permute-start(bf16[64,512]{1,0:T(8,128)(2,1)} %collective-permute-done.4.refs_1_), channel_id=1, source_target_pairs={{0,2},{1,3},{2,0},{3,1},{4,6},{5,7},{6,4},{7,5},{8,10},{9,11},{10,... | collective-permute-start | bytes 196616 | tf_op jit(solution)/shard_map/ppermute | solution.py:21
  33.6 19.5 %collective-permute-start.7 = (bf16[64,512]{1,0:T(8,128)(2,1)S(1)}, bf16[64,512]{1,0:T(8,128)(2,1)}, u32[]{:S(2)}, u32[]{:S(2)}) collective-permute-start(bf16[64,512]{1,0:T(8,128)(2,1)S(1)} %add.66.refs_0_), channel_id=1, source_target_pairs={{0,1},{1,0},{2,3},{3,2},{4,5},{5,4},{6,7},{7,6},{8,9},{9,8},{10,11... | collective-permute-start | bytes 196616 | tf_op jit(solution)/shard_map/ppermute | solution.py:21
  33.6 19.5 %collective-permute-start.8 = (bf16[64,512]{1,0:T(8,128)(2,1)}, bf16[64,512]{1,0:T(8,128)(2,1)}, u32[]{:S(2)}, u32[]{:S(2)}) collective-permute-start(bf16[64,512]{1,0:T(8,128)(2,1)} %collective-permute-done.4.refs_1_), channel_id=1, source_target_pairs={{0,1},{1,0},{2,3},{3,2},{4,5},{5,4},{6,7},{7,6},{8,9},{9,8},{10,11... | collective-permute-start | bytes 196616 | tf_op jit(solution)/shard_map/ppermute | solution.py:21
  34.8 18.4 %collective-permute-start.9 = (bf16[64,512]{1,0:T(8,128)(2,1)}, bf16[64,512]{1,0:T(8,128)(2,1)}, u32[]{:S(2)}, u32[]{:S(2)}) collective-permute-start(bf16[64,512]{1,0:T(8,128)(2,1)} %collective-permute-done.5.refs_2_), channel_id=1, source_target_pairs={{0,1},{1,0},{2,3},{3,2},{4,5},{5,4},{6,7},{7,6},{8,9},{9,8},{10,11... | collective-permute-start | bytes 196616 | tf_op jit(solution)/shard_map/ppermute | solution.py:21
  35.5 2.0 %collective-permute-start.20 = (bf16[64,512]{1,0:T(8,128)(2,1)}, bf16[64,512]{1,0:T(8,128)(2,1)}, u32[]{:S(2)}, u32[]{:S(2)}) collective-permute-start(bf16[64,512]{1,0:T(8,128)(2,1)} %collective-permute-done.16.refs_3_), channel_id=1, source_target_pairs={{0,1},{1,0},{2,3},{3,2},{4,5},{5,4},{6,7},{7,6},{8,9},{9,8},{10,11... | collective-permute-start | bytes 196616 | tf_op jit(solution)/shard_map/ppermute | solution.py:21
  35.9 17.2 %collective-permute-start.10 = (bf16[64,512]{1,0:T(8,128)(2,1)}, bf16[64,512]{1,0:T(8,128)(2,1)}, u32[]{:S(2)}, u32[]{:S(2)}) collective-permute-start(bf16[64,512]{1,0:T(8,128)(2,1)} %collective-permute-done.6.refs_3_), channel_id=1, source_target_pairs={{0,1},{1,0},{2,3},{3,2},{4,5},{5,4},{6,7},{7,6},{8,9},{9,8},{10,11... | collective-permute-start | bytes 196616 | tf_op jit(solution)/shard_map/ppermute | solution.py:21
  61.8 5.9 %collective-permute-start.21 = (f32[2,2,32,256]{3,2,1,0:T(8,128)S(1)}, f32[2,2,32,256]{3,2,1,0:T(8,128)S(1)}, u32[]{:S(2)}, u32[]{:S(2)}) collective-permute-start(f32[2,2,32,256]{3,2,1,0:T(8,128)S(1)} %get-tuple-element.36), channel_id=1, source_target_pairs={{0,2},{1,3},{2,0},{3,1},{4,6},{5,7},{6,4},{7,5},{8,10},{9,11},{10,... | collective-permute-start | bytes 393224 | tf_op jit(solution)/shard_map/ppermute | solution.py:21
  67.7 1.4 %collective-permute-start.22 = (f32[4,2,16,256]{3,2,1,0:T(8,128)S(1)}, f32[4,2,16,256]{3,2,1,0:T(8,128)S(1)}, u32[]{:S(2)}, u32[]{:S(2)}) collective-permute-start(f32[4,2,16,256]{3,2,1,0:T(8,128)S(1)} %slice.14), channel_id=1, source_target_pairs={{0,1},{1,0},{2,3},{3,2},{4,5},{5,4},{6,7},{7,6},{8,9},{9,8},{10,11... | collective-permute-start | bytes 393224 | tf_op jit(solution)/shard_map/ppermute | solution.py:21
  (12 other events, 80.4 us)

commit v4 on v3

--- a/solution.py
+++ b/solution.py
@@ -32,7 +32,7 @@
     side = device & 1
     own = side
     kept = half(own_slab, side)
-    received = flip(half(own_slab, 1 - side), 1, groups)
+    received = half(flip(own_slab, 1, groups), side)
     mine = (slice_owner == device)[:, None, None]
     theirs = (slice_owner == (device ^ 1))[:, None, None]
     picked = jnp.where(mine, kept, jnp.where(theirs, received, jnp.zeros_like(kept)))
@@ -57,7 +57,11 @@
     top = grid // 3
     classes = [[u for u in range(-top, top + 1) if u % 4 == c] for c in range(4)]
     longest = max(len(c) for c in classes)
-    return [(c[0], len(c)) for c in classes], -(-longest // 16) * 16
+    return [(c[0], len(c)) for c in classes[:3]], -(-longest // 16) * 16
+
+
+def signed(c, sin):
+    return ((1, sin), (3, -sin)) if c == 1 else ((c, sin),)
 
 
 def cos_turns(turns, grid):
@@ -84,11 +88,15 @@
         turn = iota((q, q), 0) * (first + 4 * lane)
         cos = jnp.where(lane < count, cos_turns(turn, n), 0.0)
         sin = jnp.where(lane < count, cos_turns(turn - n // 4, n), 0.0)
-        for a, b, part in ((0, 0, cos), (0, 1, -sin), (1, 0, sin), (1, 1, cos)):
-            wh[c, a * q : (a + 1) * q, b * q : (b + 1) * q], wl[c, a * q : (a + 1) * q, b * q : (b + 1) * q] = split(part)
+        for k, sine in signed(c, sin):
+            for a, b, part in ((0, 0, cos), (0, 1, -sine), (1, 0, sine), (1, 1, cos)):
+                at = (k, slice(a * q, (a + 1) * q), slice(b * q, (b + 1) * q))
+                wh[at], wl[at] = split(part)
         cos, sin = cos.T, sin.T
-        for a, b, part in ((0, 0, cos), (0, 1, sin), (1, 0, -sin), (1, 1, cos)):
-            vh[c, a * q : (a + 1) * q, b * q : (b + 1) * q], vl[c, a * q : (a + 1) * q, b * q : (b + 1) * q] = split(part)
+        for k, sine in signed(c, sin):
+            for a, b, part in ((0, 0, cos), (0, 1, sine), (1, 0, -sine), (1, 1, cos)):
+                at = (k, slice(a * q, (a + 1) * q), slice(b * q, (b + 1) * q))
+                vh[at], vl[at] = split(part)
 
 
 def late_table_kernel(first_ref, pr, pi, dh, dl):
@@ -108,22 +116,25 @@
             squared = u * u + v * v
             kept = (9 * squared <= n * n) & (row < count) & (lane < count_l)
             re, im = cos_sin(jnp.where(kept, FRESNEL * squared.astype(F32), 0.0))
-            pr[c, :, l * q : (l + 1) * q] = jnp.where(kept, re * (1.0 / (n * n)), 0.0)
-            pi[c, :, l * q : (l + 1) * q] = jnp.where(kept, im * (-1.0 / (n * n)), 0.0)
+            re, im = jnp.where(kept, re * (1.0 / (n * n)), 0.0), jnp.where(kept, im * (-1.0 / (n * n)), 0.0)
+            for k in (1, 3) if l == 1 else (l,):
+                pr[c, :, k * q : (k + 1) * q] = re
+                pi[c, :, k * q : (k + 1) * q] = im
         lane = iota((take, q), 1)
         turn = (first_ref[0] + (iota((take, q), 0) ^ first_ref[1])) * (first + 4 * lane)
         cos = jnp.where(lane < count, cos_turns(turn, n), 0.0)
         sin = jnp.where(lane < count, cos_turns(turn - n // 4, n), 0.0)
-        for a, b, part in ((0, 0, cos), (0, 1, -sin), (1, 0, sin), (1, 1, cos)):
-            at = slice(a * take, (a + 1) * take)
-            dh[c, at, b * q : (b + 1) * q], dl[c, at, b * q : (b + 1) * q] = split(part)
+        for k, sine in signed(c, sin):
+            for a, b, part in ((0, 0, cos), (0, 1, -sine), (1, 0, sine), (1, 1, cos)):
+                at = (k, slice(a * take, (a + 1) * take), slice(b * q, (b + 1) * q))
+                dh[at], dl[at] = split(part)
 
 
 def make_tables(grid, first_row, order, rows):
     _, kp = class_frequencies(grid)
     q = grid // 4
     full = jax.ShapeDtypeStruct((4, 2 * q, 2 * q), BF16)
-    prop = jax.ShapeDtypeStruct((4, kp, grid), F32)
+    prop = jax.ShapeDtypeStruct((3, kp, grid), F32)
     last = jax.ShapeDtypeStruct((4, 2 * rows, 2 * q), BF16)
     vmem = pl.BlockSpec(memory_space=pltpu.VMEM)
     params = pltpu.CompilerParams(vmem_limit_bytes=12 << 20)
@@ -320,7 +331,8 @@
             zhc, zlc = zh[c, :, lanes], zl[c, :, lanes]
             r = dot3(vh[c, :kp], vl[c, :kp], zhc, zlc)
             i = dot3(vh[c, q : q + kp], vl[c, q : q + kp], zhc, zlc)
-            re, im = pr[c, :, lanes], pi[c, :, lanes]
+            k = 1 if c == 3 else c
+            re, im = pr[k, :, lanes], pi[k, :, lanes]
             uh[c, :kp, lanes], ul[c, :kp, lanes] = split(r * re - i * im)
             uh[c, q : q + kp, lanes], ul[c, q : q + kp, lanes] = split(r * im + i * re)
         after(h)

time: 70.3 us -> 69 us (0.982)
  local copies, waits for them, and re-layouts: 8.28 us -> 7.19 us
    unnamed x28, local copies, waits for them, and re-layouts: 7.02 us -> 6.01 us
  transfers between devices with their start and end apart: 23 -> 23, of which waited for: 7 -> 8; matrix products, arithmetic and copies ran while one was open for 2% -> 4% of each run, Pallas kernels for 22% -> 22%
where the time goes in v4:
time: 69 us; the launch traced here: 68.6 us
  Pallas kernels  24.4 us (35%)
  starting transfers between devices  22.1 us (32%)
  waiting for transfers between devices  13 us (19%)
  local copies, waits for them, and re-layouts  7.19 us (10%)
  other arithmetic  1.64 us (2%)
    ppermute x23, starting transfers between devices, flip(): return lax.ppermute(array, 'wide', [(i, i ^ bit) for i in range(groups)])  22.1 us
    pallas_call x3, Pallas kernels, run_kernel(): pl.pallas_call(kernel, in_specs=[vmem] * len(inputs), out_specs=[vmem] *...  17.4 us
    ppermute x23, waiting for transfers between devices, flip(): return lax.ppermute(array, 'wide', [(i, i ^ bit) for i in range(groups)])  13 us
    unnamed x28, local copies, waits for them, and re-layouts  6.01 us
    pallas_call x2, Pallas kernels, transmit(): pl.pallas_call(functools.partial(transmit_kernel, blocks=blocks), name='t...  3.32 us
  transfers between devices with their start and end apart: 23, of which 8 were waited for; matrix products, arithmetic and copies ran while one was open for 4% of the time, Pallas kernels for 22%

profile of v4, /device:TPU:0, one launch (start us, length us, event | category | flops | bytes accessed | tf_op | source)
XLA Modules:
  0.0 68.6 jit_solution(4649472848465389429)
XLA Ops:
  0.5 1.0 %dynamic-slice_bitcast_fusion = bf16[256,512]{1,0:T(8,128)(2,1)S(1)} fusion(bf16[1,512,512]{2,1,0:T(8,128)(2,1)} %param.5, s32[]{:T(128)S(6)} %select_n.46), kind=kLoop, calls=%fused_computation.1 | loop fusion | bytes 524292 | tf_op jit(solution)/shard_map/dynamic_slice | solution.py:26
  2.5 2.9 %collective-permute-start.11 = (bf16[128,512]{1,0:T(8,128)(2,1)S(1)}, bf16[128,512]{1,0:T(8,128)(2,1)S(1)}, u32[]{:S(2)}, u32[]{:S(2)}) collective-permute-start(bf16[128,512]{1,0:T(8,128)(2,1)S(1)} %dynamic-slice_bitcast_fusion.1), channel_id=1, source_target_pairs={{0,2},{1,3},{2,0},{3,1},{4,6},{5,7},{6,4},{7,5},{8,10},{9,11},{10,... | collective-permute-start | bytes 393224 | tf_op jit(solution)/shard_map/ppermute | solution.py:21
  5.6 4.2 %collective-permute-done.11 = bf16[128,512]{1,0:T(8,128)(2,1)S(1)} collective-permute-done((bf16[128,512]{1,0:T(8,128)(2,1)S(1)}, bf16[128,512]{1,0:T(8,128)(2,1)S(1)}, u32[]{:S(2)}, u32[]{:S(2)}) %collective-permute-start.11) | collective-permute-done | bytes 131104 | tf_op jit(solution)/shard_map/ppermute | solution.py:21
  9.9 2.1 %collective-permute-start.12 = (bf16[64,512]{1,0:T(8,128)(2,1)S(1)}, bf16[64,512]{1,0:T(8,128)(2,1)S(1)}, u32[]{:S(2)}, u32[]{:S(2)}) collective-permute-start(bf16[64,512]{1,0:T(8,128)(2,1)S(1)} %constant_dynamic-slice_fusion), channel_id=1, source_target_pairs={{0,4},{1,5},{2,6},{3,7},{4,0},{5,1},{6,2},{7,3},{8,12},{9,13},{10,... | collective-permute-start | bytes 196616 | tf_op jit(solution)/shard_map/ppermute | solution.py:21
  12.1 1.9 %collective-permute-start.2 = (bf16[64,512]{1,0:T(8,128)(2,1)S(1)}, bf16[64,512]{1,0:T(8,128)(2,1)S(1)}, u32[]{:S(2)}, u32[]{:S(2)}) collective-permute-start(bf16[64,512]{1,0:T(8,128)(2,1)S(1)} %constant_dynamic-slice_fusion.1), channel_id=1, source_target_pairs={{0,4},{1,5},{2,6},{3,7},{4,0},{5,1},{6,2},{7,3},{8,12},{9,13},{10,... | collective-permute-start | bytes 196616 | tf_op jit(solution)/shard_map/ppermute | solution.py:21
  14.3 3.5 %collective-permute-start.13 = (bf16[64,512]{1,0:T(8,128)(2,1)S(1)}, bf16[64,512]{1,0:T(8,128)(2,1)S(1)}, u32[]{:S(2)}, u32[]{:S(2)}) collective-permute-start(bf16[64,512]{1,0:T(8,128)(2,1)S(1)} %dynamic-slice_add_fusion), channel_id=1, source_target_pairs={{0,8},{1,9},{2,10},{3,11},{4,12},{5,13},{6,14},{7,15},{8,0},{9,1},... | collective-permute-start | bytes 196616 | tf_op jit(solution)/shard_map/ppermute | solution.py:21
  17.8 1.7 %collective-permute-start.3 = (bf16[64,512]{1,0:T(8,128)(2,1)S(1)}, bf16[64,512]{1,0:T(8,128)(2,1)S(1)}, u32[]{:S(2)}, u32[]{:S(2)}) collective-permute-start(bf16[64,512]{1,0:T(8,128)(2,1)S(1)} %dynamic-slice_add_fusion.1), channel_id=1, source_target_pairs={{0,8},{1,9},{2,10},{3,11},{4,12},{5,13},{6,14},{7,15},{8,0},{9,1},... | collective-permute-start | bytes 196616 | tf_op jit(solution)/shard_map/ppermute | solution.py:21
  19.5 2.3 %collective-permute-done.13 = bf16[64,512]{1,0:T(8,128)(2,1)S(1)} collective-permute-done((bf16[64,512]{1,0:T(8,128)(2,1)S(1)}, bf16[64,512]{1,0:T(8,128)(2,1)S(1)}, u32[]{:S(2)}, u32[]{:S(2)}) %collective-permute-start.13) | collective-permute-done | bytes 65568 | tf_op jit(solution)/shard_map/ppermute | solution.py:21
  22.4 1.5 %collective-permute-start.15 = (bf16[64,512]{1,0:T(8,128)(2,1)S(1)}, bf16[64,512]{1,0:T(8,128)(2,1)}, u32[]{:S(2)}, u32[]{:S(2)}) collective-permute-start(bf16[64,512]{1,0:T(8,128)(2,1)S(1)} %add.66.refs_0_), channel_id=1, source_target_pairs={{0,2},{1,3},{2,0},{3,1},{4,6},{5,7},{6,4},{7,5},{8,10},{9,11},{10,... | collective-permute-start | bytes 196616 | tf_op jit(solution)/shard_map/ppermute | solution.py:21
  24.6 1.5 %collective-permute-start.4 = (bf16[64,512]{1,0:T(8,128)(2,1)}, bf16[64,512]{1,0:T(8,128)(2,1)}, u32[]{:S(2)}, u32[]{:S(2)}) collective-permute-start(bf16[64,512]{1,0:T(8,128)(2,1)} %add.63.refs_0_), channel_id=1, source_target_pairs={{0,4},{1,5},{2,6},{3,7},{4,0},{5,1},{6,2},{7,3},{8,12},{9,13},{10,... | collective-permute-start | bytes 196616 | tf_op jit(solution)/shard_map/ppermute | solution.py:21
  27.4 1.3 %collective-permute-start.16 = (bf16[64,512]{1,0:T(8,128)(2,1)}, bf16[64,512]{1,0:T(8,128)(2,1)}, u32[]{:S(2)}, u32[]{:S(2)}) collective-permute-start(bf16[64,512]{1,0:T(8,128)(2,1)} %collective-permute-done.14.refs_1_), channel_id=1, source_target_pairs={{0,2},{1,3},{2,0},{3,1},{4,6},{5,7},{6,4},{7,5},{8,10},{9,11},{10,... | collective-permute-start | bytes 196616 | tf_op jit(solution)/shard_map/ppermute | solution.py:21
  30.6 1.1 %late_tables.1 = (f32[3,96,512]{2,1,0:T(8,128)S(1)}, f32[3,96,512]{2,1,0:T(8,128)S(1)}, bf16[4,128,256]{2,1,0:T(8,128)(2,1)S(1)}, bf16[4,128,256]{2,1,0:T(8,128)(2,1)S(1)}) custom-call(s32[2]{0:T(128)S(1)} %pad_add_fusion.1.first_ref), custom_call_target="tpu_custom_call" | custom-call | tf_op jit(solution)/shard_map/late_tables/pallas_call | solution.py:148
  35.1 1.2 %probe_waves.1 = (bf16[2,512,96]{2,1,0:T(8,128)(2,1)S(1)}, bf16[2,96,512]{2,1,0:T(8,128)(2,1)S(1)}) custom-call(s32[1]{0:T(128)} %bitcast.place_ref, s32[8,2]{1,0:T(8,128)S(1)} %copy.9.position_ref, s32[16,3]{1,0:T(8,128)S(1)} %copy.10.beam_ref), custom_call_target="tpu_custom_call" | custom-call | tf_op jit(solution)/shard_map/probe_waves/pallas_call | solution.py:202
  37.2 0.8 %copy-done.5 = bf16[64,512]{1,0:T(8,128)(2,1)S(1)} copy-done((bf16[64,512]{1,0:T(8,128)(2,1)S(1)}, bf16[64,512]{1,0:T(8,128)(2,1)}, u32[]{:S(2)}) %copy-start.5) | copy-done | bytes 65560
  38.0 0.8 %copy-done.7 = bf16[64,512]{1,0:T(8,128)(2,1)S(1)} copy-done((bf16[64,512]{1,0:T(8,128)(2,1)S(1)}, bf16[64,512]{1,0:T(8,128)(2,1)}, u32[]{:S(2)}) %copy-start.7) | copy-done | bytes 65560
  38.9 0.8 %copy-done.9 = bf16[64,512]{1,0:T(8,128)(2,1)S(1)} copy-done((bf16[64,512]{1,0:T(8,128)(2,1)S(1)}, bf16[64,512]{1,0:T(8,128)(2,1)}, u32[]{:S(2)}) %copy-start.9) | copy-done | bytes 65560
  39.7 1.6 %transmit.3 = (f32[512,512]{1,0:T(8,128)S(1)}, f32[512,512]{1,0:T(8,128)S(1)}) custom-call(s32[1]{0:T(128)} %bitcast.1.own_ref, bf16[64,512]{1,0:T(8,128)(2,1)S(1)} %copy-done.3, bf16[64,512]{1,0:T(8,128)(2,1)} %collective-permute-done.14.refs_1_, bf16[64,512]{1,0:T(8,128)(2,1)} %collective-permute-done.15.refs_2_, ...), custom_call_target="tpu_custom_call" | custom-call | tf_op jit(solution)/shard_map/transmit/pallas_call | solution.py:271
  41.3 5.1 %shard_map.56.refs_1_ = f32[2,512,512]{2,1,0:T(8,128)S(1)} custom-call(f32[512,512]{1,0:T(8,128)S(1)} %get-tuple-element.23.tr, f32[512,512]{1,0:T(8,128)S(1)} %get-tuple-element.24.ti, bf16[2,512,96]{2,1,0:T(8,128)(2,1)S(1)} %get-tuple-element.25.left_ref, bf16[2,96,512]{2,1,0:T(8,128)(2,1)S(1)} %get-tuple-element.26.right_ref, ...), custom_call_target="tpu_custom_call" | custom-call | tf_op jit(solution)/shard_map/pallas_call | solution.py:460
  46.5 5.3 %shard_map.55.refs_0_ = f32[2,512,512]{2,1,0:T(8,128)S(1)} custom-call(f32[512,512]{1,0:T(8,128)S(1)} %get-tuple-element.23.tr, f32[512,512]{1,0:T(8,128)S(1)} %get-tuple-element.24.ti, bf16[2,512,96]{2,1,0:T(8,128)(2,1)S(1)} %get-tuple-element.25.left_ref, bf16[2,96,512]{2,1,0:T(8,128)(2,1)S(1)} %get-tuple-element.26.right_ref, ...), custom_call_target="tpu_custom_call" | custom-call | tf_op jit(solution)/shard_map/pallas_call | solution.py:460
  51.8 1.7 %transmit.2 = (f32[512,512]{1,0:T(8,128)S(1)}, f32[512,512]{1,0:T(8,128)S(1)}) custom-call(s32[1]{0:T(128)} %bitcast.1.own_ref, bf16[64,512]{1,0:T(8,128)(2,1)} %add.63.refs_0_, bf16[64,512]{1,0:T(8,128)(2,1)} %collective-permute-done.4.refs_1_, bf16[64,512]{1,0:T(8,128)(2,1)} %collective-permute-done.5.refs_2_, ...), custom_call_target="tpu_custom_call" | custom-call | tf_op jit(solution)/shard_map/transmit/pallas_call | solution.py:271
  53.6 6.9 %shard_map.57 = (f32[2,2,32,256]{3,2,1,0:T(8,128)S(1)}, f32[2,2,32,256]{3,2,1,0:T(8,128)S(1)}) custom-call(f32[512,512]{1,0:T(8,128)S(1)} %get-tuple-element.21.tr, f32[512,512]{1,0:T(8,128)S(1)} %get-tuple-element.22.ti, f32[2,512,512]{2,1,0:T(8,128)S(1)} %shard_map.55.refs_0_, f32[2,512,512]{2,1,0:T(8,128)S(1)} %shard_map.56.refs_1_, ...), custom_call_target="tpu_custom_call" | custom-call | tf_op jit(solution)/shard_map/pallas_call | solution.py:460
  60.5 1.3 %collective-permute-start.21 = (f32[2,2,32,256]{3,2,1,0:T(8,128)S(1)}, f32[2,2,32,256]{3,2,1,0:T(8,128)S(1)}, u32[]{:S(2)}, u32[]{:S(2)}) collective-permute-start(f32[2,2,32,256]{3,2,1,0:T(8,128)S(1)} %get-tuple-element.36), channel_id=1, source_target_pairs={{0,2},{1,3},{2,0},{3,1},{4,6},{5,7},{6,4},{7,5},{8,10},{9,11},{10,... | collective-permute-start | bytes 393224 | tf_op jit(solution)/shard_map/ppermute | solution.py:21
  61.8 4.5 %collective-permute-done.21 = f32[2,2,32,256]{3,2,1,0:T(8,128)S(1)} collective-permute-done((f32[2,2,32,256]{3,2,1,0:T(8,128)S(1)}, f32[2,2,32,256]{3,2,1,0:T(8,128)S(1)}, u32[]{:S(2)}, u32[]{:S(2)}) %collective-permute-start.21) | collective-permute-done | bytes 131104 | tf_op jit(solution)/shard_map/ppermute | solution.py:21
  66.5 1.3 %collective-permute-done.22.other_ref = f32[4,2,16,256]{3,2,1,0:T(8,128)S(1)} collective-permute-done((f32[4,2,16,256]{3,2,1,0:T(8,128)S(1)}, f32[4,2,16,256]{3,2,1,0:T(8,128)S(1)}, u32[]{:S(2)}, u32[]{:S(2)}) %collective-permute-start.22) | collective-permute-done | bytes 131104 | tf_op jit(solution)/shard_map/ppermute | solution.py:21
  (79 shorter events, 11.6 us)
Async XLA Ops:
  0.0 2.2 %collective-permute-start = (bf16[512,512]{1,0:T(8,128)(2,1)}, bf16[512,512]{1,0:T(8,128)(2,1)S(1)}, u32[]{:S(2)}, u32[]{:S(2)}) collective-permute-start(bf16[512,512]{1,0:T(8,128)(2,1)} %bitcast.16), channel_id=1, source_target_pairs={{0,1},{1,0},{2,3},{3,2},{4,5},{5,4},{6,7},{7,6},{8,9},{9,8},{10,11... | collective-permute-start | bytes 1572872 | tf_op jit(solution)/shard_map/ppermute | solution.py:21
  2.3 32.7 %copy-start.11 = (s32[8,2]{0,1:T(2,128)S(1)}, s32[8,2]{0,1:T(2,128)}, u32[]{:S(2)}) copy-start(s32[8,2]{0,1:T(2,128)} %param.9) | copy-start | bytes 196
  2.5 7.3 %collective-permute-start.11 = (bf16[128,512]{1,0:T(8,128)(2,1)S(1)}, bf16[128,512]{1,0:T(8,128)(2,1)S(1)}, u32[]{:S(2)}, u32[]{:S(2)}) collective-permute-start(bf16[128,512]{1,0:T(8,128)(2,1)S(1)} %dynamic-slice_bitcast_fusion.1), channel_id=1, source_target_pairs={{0,2},{1,3},{2,0},{3,1},{4,6},{5,7},{6,4},{7,5},{8,10},{9,11},{10,... | collective-permute-start | bytes 393224 | tf_op jit(solution)/shard_map/ppermute | solution.py:21
  5.5 6.6 %collective-permute-start.1 = (bf16[128,512]{1,0:T(8,128)(2,1)S(1)}, bf16[128,512]{1,0:T(8,128)(2,1)S(1)}, u32[]{:S(2)}, u32[]{:S(2)}) collective-permute-start(bf16[128,512]{1,0:T(8,128)(2,1)S(1)} %dynamic-slice_bitcast_fusion.2), channel_id=1, source_target_pairs={{0,2},{1,3},{2,0},{3,1},{4,6},{5,7},{6,4},{7,5},{8,10},{9,11},{10,... | collective-permute-start | bytes 393224 | tf_op jit(solution)/shard_map/ppermute | solution.py:21
  9.9 4.4 %collective-permute-start.12 = (bf16[64,512]{1,0:T(8,128)(2,1)S(1)}, bf16[64,512]{1,0:T(8,128)(2,1)S(1)}, u32[]{:S(2)}, u32[]{:S(2)}) collective-permute-start(bf16[64,512]{1,0:T(8,128)(2,1)S(1)} %constant_dynamic-slice_fusion), channel_id=1, source_target_pairs={{0,4},{1,5},{2,6},{3,7},{4,0},{5,1},{6,2},{7,3},{8,12},{9,13},{10,... | collective-permute-start | bytes 196616 | tf_op jit(solution)/shard_map/ppermute | solution.py:21
  12.1 5.7 %collective-permute-start.2 = (bf16[64,512]{1,0:T(8,128)(2,1)S(1)}, bf16[64,512]{1,0:T(8,128)(2,1)S(1)}, u32[]{:S(2)}, u32[]{:S(2)}) collective-permute-start(bf16[64,512]{1,0:T(8,128)(2,1)S(1)} %constant_dynamic-slice_fusion.1), channel_id=1, source_target_pairs={{0,4},{1,5},{2,6},{3,7},{4,0},{5,1},{6,2},{7,3},{8,12},{9,13},{10,... | collective-permute-start | bytes 196616 | tf_op jit(solution)/shard_map/ppermute | solution.py:21
  14.3 7.5 %collective-permute-start.13 = (bf16[64,512]{1,0:T(8,128)(2,1)S(1)}, bf16[64,512]{1,0:T(8,128)(2,1)S(1)}, u32[]{:S(2)}, u32[]{:S(2)}) collective-permute-start(bf16[64,512]{1,0:T(8,128)(2,1)S(1)} %dynamic-slice_add_fusion), channel_id=1, source_target_pairs={{0,8},{1,9},{2,10},{3,11},{4,12},{5,13},{6,14},{7,15},{8,0},{9,1},... | collective-permute-start | bytes 196616 | tf_op jit(solution)/shard_map/ppermute | solution.py:21
  17.8 6.1 %collective-permute-start.3 = (bf16[64,512]{1,0:T(8,128)(2,1)S(1)}, bf16[64,512]{1,0:T(8,128)(2,1)S(1)}, u32[]{:S(2)}, u32[]{:S(2)}) collective-permute-start(bf16[64,512]{1,0:T(8,128)(2,1)S(1)} %dynamic-slice_add_fusion.1), channel_id=1, source_target_pairs={{0,8},{1,9},{2,10},{3,11},{4,12},{5,13},{6,14},{7,15},{8,0},{9,1},... | collective-permute-start | bytes 196616 | tf_op jit(solution)/shard_map/ppermute | solution.py:21
  21.8 5.6 %collective-permute-start.14 = (bf16[64,512]{1,0:T(8,128)(2,1)S(1)}, bf16[64,512]{1,0:T(8,128)(2,1)}, u32[]{:S(2)}, u32[]{:S(2)}) collective-permute-start(bf16[64,512]{1,0:T(8,128)(2,1)S(1)} %add.66.refs_0_), channel_id=1, source_target_pairs={{0,4},{1,5},{2,6},{3,7},{4,0},{5,1},{6,2},{7,3},{8,12},{9,13},{10,... | collective-permute-start | bytes 196616 | tf_op jit(solution)/shard_map/ppermute | solution.py:21
  22.4 6.3 %collective-permute-start.15 = (bf16[64,512]{1,0:T(8,128)(2,1)S(1)}, bf16[64,512]{1,0:T(8,128)(2,1)}, u32[]{:S(2)}, u32[]{:S(2)}) collective-permute-start(bf16[64,512]{1,0:T(8,128)(2,1)S(1)} %add.66.refs_0_), channel_id=1, source_target_pairs={{0,2},{1,3},{2,0},{3,1},{4,6},{5,7},{6,4},{7,5},{8,10},{9,11},{10,... | collective-permute-start | bytes 196616 | tf_op jit(solution)/shard_map/ppermute | solution.py:21
  23.9 4.8 %collective-permute-start.17 = (bf16[64,512]{1,0:T(8,128)(2,1)S(1)}, bf16[64,512]{1,0:T(8,128)(2,1)S(1)}, u32[]{:S(2)}, u32[]{:S(2)}) collective-permute-start(bf16[64,512]{1,0:T(8,128)(2,1)S(1)} %add.66.refs_0_), channel_id=1, source_target_pairs={{0,1},{1,0},{2,3},{3,2},{4,5},{5,4},{6,7},{7,6},{8,9},{9,8},{10,11... | collective-permute-start | bytes 196616 | tf_op jit(solution)/shard_map/ppermute | solution.py:21
  24.6 5.3 %collective-permute-start.4 = (bf16[64,512]{1,0:T(8,128)(2,1)}, bf16[64,512]{1,0:T(8,128)(2,1)}, u32[]{:S(2)}, u32[]{:S(2)}) collective-permute-start(bf16[64,512]{1,0:T(8,128)(2,1)} %add.63.refs_0_), channel_id=1, source_target_pairs={{0,4},{1,5},{2,6},{3,7},{4,0},{5,1},{6,2},{7,3},{8,12},{9,13},{10,... | collective-permute-start | bytes 196616 | tf_op jit(solution)/shard_map/ppermute | solution.py:21
  26.6 5.9 %collective-permute-start.5 = (bf16[64,512]{1,0:T(8,128)(2,1)}, bf16[64,512]{1,0:T(8,128)(2,1)}, u32[]{:S(2)}, u32[]{:S(2)}) collective-permute-start(bf16[64,512]{1,0:T(8,128)(2,1)} %add.63.refs_0_), channel_id=1, source_target_pairs={{0,2},{1,3},{2,0},{3,1},{4,6},{5,7},{6,4},{7,5},{8,10},{9,11},{10,... | collective-permute-start | bytes 196616 | tf_op jit(solution)/shard_map/ppermute | solution.py:21
  27.4 5.2 %collective-permute-start.16 = (bf16[64,512]{1,0:T(8,128)(2,1)}, bf16[64,512]{1,0:T(8,128)(2,1)}, u32[]{:S(2)}, u32[]{:S(2)}) collective-permute-start(bf16[64,512]{1,0:T(8,128)(2,1)} %collective-permute-done.14.refs_1_), channel_id=1, source_target_pairs={{0,2},{1,3},{2,0},{3,1},{4,6},{5,7},{6,4},{7,5},{8,10},{9,11},{10,... | collective-permute-start | bytes 196616 | tf_op jit(solution)/shard_map/ppermute | solution.py:21
  28.7 4.3 %collective-permute-start.18 = (bf16[64,512]{1,0:T(8,128)(2,1)}, bf16[64,512]{1,0:T(8,128)(2,1)S(1)}, u32[]{:S(2)}, u32[]{:S(2)}) collective-permute-start(bf16[64,512]{1,0:T(8,128)(2,1)} %collective-permute-done.14.refs_1_), channel_id=1, source_target_pairs={{0,1},{1,0},{2,3},{3,2},{4,5},{5,4},{6,7},{7,6},{8,9},{9,8},{10,11... | collective-permute-start | bytes 196616 | tf_op jit(solution)/shard_map/ppermute | solution.py:21
  29.3 4.4 %collective-permute-start.19 = (bf16[64,512]{1,0:T(8,128)(2,1)}, bf16[64,512]{1,0:T(8,128)(2,1)S(1)}, u32[]{:S(2)}, u32[]{:S(2)}) collective-permute-start(bf16[64,512]{1,0:T(8,128)(2,1)} %collective-permute-done.15.refs_2_), channel_id=1, source_target_pairs={{0,1},{1,0},{2,3},{3,2},{4,5},{5,4},{6,7},{7,6},{8,9},{9,8},{10,11... | collective-permute-start | bytes 196616 | tf_op jit(solution)/shard_map/ppermute | solution.py:21
  29.9 4.9 %collective-permute-start.6 = (bf16[64,512]{1,0:T(8,128)(2,1)}, bf16[64,512]{1,0:T(8,128)(2,1)}, u32[]{:S(2)}, u32[]{:S(2)}) collective-permute-start(bf16[64,512]{1,0:T(8,128)(2,1)} %collective-permute-done.4.refs_1_), channel_id=1, source_target_pairs={{0,2},{1,3},{2,0},{3,1},{4,6},{5,7},{6,4},{7,5},{8,10},{9,11},{10,... | collective-permute-start | bytes 196616 | tf_op jit(solution)/shard_map/ppermute | solution.py:21
  32.5 19.3 %collective-permute-start.7 = (bf16[64,512]{1,0:T(8,128)(2,1)}, bf16[64,512]{1,0:T(8,128)(2,1)}, u32[]{:S(2)}, u32[]{:S(2)}) collective-permute-start(bf16[64,512]{1,0:T(8,128)(2,1)} %add.63.refs_0_), channel_id=1, source_target_pairs={{0,1},{1,0},{2,3},{3,2},{4,5},{5,4},{6,7},{7,6},{8,9},{9,8},{10,11... | collective-permute-start | bytes 196616 | tf_op jit(solution)/shard_map/ppermute | solution.py:21
  32.6 19.2 %collective-permute-start.8 = (bf16[64,512]{1,0:T(8,128)(2,1)}, bf16[64,512]{1,0:T(8,128)(2,1)}, u32[]{:S(2)}, u32[]{:S(2)}) collective-permute-start(bf16[64,512]{1,0:T(8,128)(2,1)} %collective-permute-done.4.refs_1_), channel_id=1, source_target_pairs={{0,1},{1,0},{2,3},{3,2},{4,5},{5,4},{6,7},{7,6},{8,9},{9,8},{10,11... | collective-permute-start | bytes 196616 | tf_op jit(solution)/shard_map/ppermute | solution.py:21
  33.6 18.2 %collective-permute-start.9 = (bf16[64,512]{1,0:T(8,128)(2,1)}, bf16[64,512]{1,0:T(8,128)(2,1)}, u32[]{:S(2)}, u32[]{:S(2)}) collective-permute-start(bf16[64,512]{1,0:T(8,128)(2,1)} %collective-permute-done.5.refs_2_), channel_id=1, source_target_pairs={{0,1},{1,0},{2,3},{3,2},{4,5},{5,4},{6,7},{7,6},{8,9},{9,8},{10,11... | collective-permute-start | bytes 196616 | tf_op jit(solution)/shard_map/ppermute | solution.py:21
  34.4 2.0 %collective-permute-start.20 = (bf16[64,512]{1,0:T(8,128)(2,1)}, bf16[64,512]{1,0:T(8,128)(2,1)}, u32[]{:S(2)}, u32[]{:S(2)}) collective-permute-start(bf16[64,512]{1,0:T(8,128)(2,1)} %collective-permute-done.16.refs_3_), channel_id=1, source_target_pairs={{0,1},{1,0},{2,3},{3,2},{4,5},{5,4},{6,7},{7,6},{8,9},{9,8},{10,11... | collective-permute-start | bytes 196616 | tf_op jit(solution)/shard_map/ppermute | solution.py:21
  34.8 17.1 %collective-permute-start.10 = (bf16[64,512]{1,0:T(8,128)(2,1)}, bf16[64,512]{1,0:T(8,128)(2,1)}, u32[]{:S(2)}, u32[]{:S(2)}) collective-permute-start(bf16[64,512]{1,0:T(8,128)(2,1)} %collective-permute-done.6.refs_3_), channel_id=1, source_target_pairs={{0,1},{1,0},{2,3},{3,2},{4,5},{5,4},{6,7},{7,6},{8,9},{9,8},{10,11... | collective-permute-start | bytes 196616 | tf_op jit(solution)/shard_map/ppermute | solution.py:21
  60.5 5.8 %collective-permute-start.21 = (f32[2,2,32,256]{3,2,1,0:T(8,128)S(1)}, f32[2,2,32,256]{3,2,1,0:T(8,128)S(1)}, u32[]{:S(2)}, u32[]{:S(2)}) collective-permute-start(f32[2,2,32,256]{3,2,1,0:T(8,128)S(1)} %get-tuple-element.36), channel_id=1, source_target_pairs={{0,2},{1,3},{2,0},{3,1},{4,6},{5,7},{6,4},{7,5},{8,10},{9,11},{10,... | collective-permute-start | bytes 393224 | tf_op jit(solution)/shard_map/ppermute | solution.py:21
  66.4 1.4 %collective-permute-start.22 = (f32[4,2,16,256]{3,2,1,0:T(8,128)S(1)}, f32[4,2,16,256]{3,2,1,0:T(8,128)S(1)}, u32[]{:S(2)}, u32[]{:S(2)}) collective-permute-start(f32[4,2,16,256]{3,2,1,0:T(8,128)S(1)} %slice.14), channel_id=1, source_target_pairs={{0,1},{1,0},{2,3},{3,2},{4,5},{5,4},{6,7},{7,6},{8,9},{9,8},{10,11... | collective-permute-start | bytes 393224 | tf_op jit(solution)/shard_map/ppermute | solution.py:21
  (12 other events, 87.1 us)
